TPU v7x, 512 devices: a whole 4x4x16 slice. The times are simulated.
512 devices in a mesh: dp: 128 (over y, z, core), mp: 4 (over x).
Axes of the slice: x: 4, y: 4, z: 16, core: 2. Of those that a mesh axis runs over, the one named last changes fastest.
Arguments:
- cams: int32 [768], replicated, may hold values from 5 to 11, as said below
- pack: int32 [6144], replicated, may hold values from 0 to 6143, as said below
- visible: int32 [768, 11, 4], P('dp'), may hold values from 0 to 1, as said below
- align: int32 [768, 4, 512], P('dp', None, 'mp'), may hold values from 0 to 511, as said below
- images: bfloat16 [6144, 32, 1024], P('dp', 'mp'), may hold values from -24 to 24
- cam_keys: bfloat16 [6144, 32, 256], P('dp', 'mp'), may hold values from -8 to 8
- neck_weight: bfloat16 [1024, 256], replicated, may hold values from -0.1875 to 0.1875
- bev_query: bfloat16 [512, 256], P('mp'), may hold values from -8 to 8
- prev_bev: bfloat16 [768, 512, 256], P('dp', 'mp'), may hold values from -6 to 6
- point_weight: bfloat16 [256, 32], replicated, may hold values from -0.375 to 0.375
- norm_gain: float32 [256], replicated, may hold values from 0.5 to 1.5
- out_grad: bfloat16 [768, 512, 256], P('dp', 'mp'), may hold values from -6 to 6
Outputs:
- bev_out: bfloat16 [768, 512, 256], P('dp', 'mp')
- neck_grad: float32 [1024, 256], P(('dp', 'mp'))
Inputs may be any that keep to these rules, and one draw needn't show every extreme that they name: `cams`: the counts of all samples sum to 6144. `pack`: A permutation of the bin-slot positions; the bin of a position is position // 48. No bin holds more than 1 cameras of the samples of one owner (samples o * 6 to o * 6 + 5). `visible`: every grid row of a sample is seen by 1 to 3 of its cameras, some row by exactly 3; entries of camera slots j >= cams[s] are 0. `align`: cell numbers row * 128 + column of the sample's previous grid, in the same band of 1 row (row) as the query cell.
All inputs are finite; a program needn't handle non-finite values.
Results may differ from a plain program's by a relative error of at most 0.008.
Values may be sent and summed in bfloat16 or wider, within the bound.
No kernel may reach another device: no remote copies, remote signals or barrier semaphores. Data moves between devices by JAX's collectives and lax.ppermute only.
A program may use at most 64 MiB of HBM per device.

v0:
```python
import jax
import jax.numpy as jnp
from jax import lax
from jax.sharding import PartitionSpec as P

HEADS = 8
KT = 4
MAXCAM = 11
SPD = 6
GW = 128


NORM_EPS = 1e-05
MASKED = -1e30


def layer_norm(pre_norm, norm_gain):
    row_mean = jnp.mean(pre_norm, axis=-1, keepdims=True)
    centred = pre_norm - row_mean
    spread = jnp.mean(centred * centred, axis=-1, keepdims=True)
    return centred * lax.rsqrt(spread + NORM_EPS) * norm_gain


def on_device(
    cams,
    pack,
    visible,
    align,
    images,
    cam_keys,
    neck_weight,
    bev_query,
    prev_bev,
    point_weight,
    norm_gain,
    out_grad,
):
    owner_count = lax.axis_size("dp")
    band_count = lax.axis_size("mp")
    owner_id = lax.axis_index("dp")
    band_id = lax.axis_index("mp")
    sample_total = cams.shape[0]
    camera_total = pack.shape[0]
    bin_size = camera_total // owner_count
    quarter = images.shape[1]
    tokens = quarter * band_count
    channels = neck_weight.shape[1]
    head_dim = channels // HEADS
    scale_factor = float(head_dim) ** (-0.5)
    pair_cap = (SPD * MAXCAM + owner_count - 1) // owner_count
    slot_count = SPD * MAXCAM
    band_queries = prev_bev.shape[1]
    lane_total = owner_count * pair_cap
    sample_of = jnp.repeat(
        jnp.arange(sample_total, dtype=jnp.int32), cams, total_repeat_length=camera_total
    )
    starts = jnp.cumsum(cams) - cams
    camera_at = (
        jnp.zeros((camera_total,), jnp.int32)
        .at[pack]
        .set(jnp.arange(camera_total, dtype=jnp.int32))
    )
    owner_at = (sample_of[camera_at] // SPD).reshape(owner_count, bin_size)
    slot_index = jnp.arange(bin_size, dtype=jnp.int32)
    earlier = (owner_at[:, :, None] == owner_at[:, None, :]) & (
        slot_index[None, None, :] < slot_index[None, :, None]
    )
    rank_at = jnp.sum(earlier.astype(jnp.int32), axis=2)
    send_lane = owner_at[owner_id] * pair_cap + rank_at[owner_id]
    local_ids = owner_id * SPD + jnp.arange(SPD, dtype=jnp.int32)
    camera_slot = jnp.arange(MAXCAM, dtype=jnp.int32)
    live_slots = camera_slot[None, :] < cams[local_ids][:, None]
    camera_ids = jnp.where(live_slots, starts[local_ids][:, None] + camera_slot[None, :], 0)
    positions = pack[camera_ids]
    source_bin = positions // bin_size
    receive_lane = (source_bin * pair_cap + rank_at[source_bin, positions % bin_size]).reshape(
        slot_count
    )
    flat_images = images.reshape(bin_size * quarter, images.shape[2])
    features = jnp.dot(flat_images, neck_weight, preferred_element_type=jnp.float32)
    features = features.astype(jnp.bfloat16).reshape(bin_size, quarter, channels)

    def to_lanes(source_block):
        flat_block = source_block.reshape(source_block.shape[0], -1)
        return (
            jnp.zeros((lane_total, flat_block.shape[1]), flat_block.dtype)
            .at[send_lane]
            .set(flat_block)
        )

    whole_feat, whole_keys = (
        lax.all_gather(features, "mp", axis=1, tiled=True),
        lax.all_gather(cam_keys, "mp", axis=1, tiled=True),
    )
    got_feat, got_keys = (
        lax.all_to_all(to_lanes(whole_feat), "dp", split_axis=0, concat_axis=0, tiled=True),
        lax.all_to_all(to_lanes(whole_keys), "dp", split_axis=0, concat_axis=0, tiled=True),
    )
    own_feat = jnp.take(got_feat, receive_lane, axis=0).reshape(SPD, MAXCAM, tokens, channels)
    own_keys = jnp.take(got_keys, receive_lane, axis=0).reshape(SPD, MAXCAM, tokens, channels)
    query_wide = bev_query.astype(jnp.float32)
    query_split = bev_query.reshape(band_queries, HEADS, head_dim)
    modulation = jax.nn.sigmoid(
        jnp.dot(bev_query, point_weight, preferred_element_type=jnp.float32)
    )
    modulation = modulation.reshape(band_queries, HEADS, KT)
    grid_rows = (band_id * band_queries + jnp.arange(band_queries, dtype=jnp.int32)) // GW
    outputs = []
    value_parts = []
    for member in range(SPD):
        is_live = live_slots[member]
        key_heads = own_keys[member].reshape(MAXCAM * tokens, HEADS, head_dim)
        value_heads = own_feat[member].reshape(MAXCAM * tokens, HEADS, head_dim)
        seen_mask = (jnp.take(visible[member], grid_rows, axis=1) > 0) & is_live[:, None]
        key_mask = jnp.repeat(seen_mask, tokens, axis=0).T
        scores = (
            jnp.einsum("qhd,khd->hqk", query_split, key_heads, preferred_element_type=jnp.float32)
            * scale_factor
        )
        scores = jnp.where(key_mask[None], scores, MASKED)
        row_max = jnp.max(scores, axis=-1, keepdims=True)
        raised = jnp.exp(scores - row_max)
        attn_probs = (raised / jnp.sum(raised, axis=-1, keepdims=True)).astype(jnp.bfloat16)
        cross_out = jnp.einsum(
            "hqk,khd->qhd", attn_probs, value_heads, preferred_element_type=jnp.float32
        )
        cross_out = cross_out.reshape(band_queries, channels)
        local_cells = align[member] - band_id * band_queries
        picked = jnp.take(prev_bev[member], local_cells, axis=0).astype(jnp.float32)
        picked = picked.reshape(KT, band_queries, HEADS, head_dim)
        temporal = jnp.einsum("qhk,kqhd->qhd", modulation, picked, precision=lax.Precision.HIGHEST)
        pre_norm = query_wide + cross_out + temporal.reshape(band_queries, channels)
        normed, pull_back = jax.vjp(lambda pre_value: layer_norm(pre_value, norm_gain), pre_norm)
        (pre_grad,) = pull_back(out_grad[member].astype(jnp.float32))
        cross_grad = pre_grad.astype(jnp.bfloat16)
        value_part = jnp.einsum(
            "hqk,qhd->khd",
            attn_probs,
            cross_grad.reshape(band_queries, HEADS, head_dim),
            preferred_element_type=jnp.float32,
        )
        value_part = value_part.reshape(MAXCAM, tokens, channels)
        outputs.append(normed.astype(jnp.bfloat16))
        value_parts.append(value_part)
    value_partial = jnp.stack(value_parts).reshape(slot_count, tokens, channels)
    value_sum = lax.psum_scatter(
        value_partial.astype(jnp.bfloat16), "mp", scatter_dimension=1, tiled=True
    )
    value_half = value_sum.reshape(slot_count, quarter * channels)
    back_lane = jnp.where(live_slots.reshape(slot_count), receive_lane, lane_total)
    back_buffer = (
        jnp.zeros((lane_total + 1, quarter * channels), jnp.bfloat16)
        .at[back_lane]
        .set(value_half)[:lane_total]
    )
    returned = lax.all_to_all(back_buffer, "dp", split_axis=0, concat_axis=0, tiled=True)
    feature_grad = jnp.take(returned, send_lane, axis=0).reshape(bin_size * quarter, channels)
    neck_part = lax.psum_scatter(
        lax.dot_general(
            flat_images, feature_grad, (((0,), (0,)), ((), ())), preferred_element_type=jnp.float32
        ),
        ("dp", "mp"),
        scatter_dimension=0,
        tiled=True,
    )
    return (jnp.stack(outputs), neck_part / sample_total)


def solution(mesh):
    return jax.shard_map(
        on_device,
        mesh=mesh,
        in_specs=(
            P(),
            P(),
            P("dp", None, None),
            P("dp", None, "mp"),
            P("dp", "mp", None),
            P("dp", "mp", None),
            P(),
            P("mp", None),
            P("dp", "mp", None),
            P(),
            P(),
            P("dp", "mp", None),
        ),
        out_specs=(P("dp", "mp", None), P(("dp", "mp"), None)),
        check_vma=False,
    )
```

profile of v0, /device:TPU:1, one launch (start us, length us, event | category | flops | bytes accessed | tf_op | source)
XLA Modules:
  0.0 1021.8 jit_solution(15421255479687964466)
XLA Ops:
  10.5 5.9 scatter_custom_fusion
  17.9 23.0 %scatter_custom_fusion.1 = s32[6144]{0:T(1024)S(1)} fusion(s32[6144]{0:T(1024)S(1)} %compare_select_fusion.2, s32[6144]{0:T(1024)S(1)} %iota.41, s32[]{:T(128)} %constant.182.clone.1), kind=kCustom, calls=%fused_computation.242 | custom fusion | bytes 24580 | tf_op jit(solution)/shard_map/scatter | solution.py:61
  40.9 24.8 %gather_fusion = s32[6144]{0:T(1024)S(1)} fusion(s32[768]{0:T(1024)S(1)} %iota.40, s32[6144]{0:T(1024)S(1)} %get-tuple-element.183), kind=kCustom, calls=%fused_computation.14 | custom fusion | bytes 73728 | tf_op jit(solution)/shard_map/jit(_take)/gather | solution.py:54
  65.7 34.3 %gather_fusion.1 = s32[6144]{0:T(1024)S(1)} fusion(s32[6144]{0:T(1024)S(1)} %and_select_fusion, s32[6144]{0:T(1024)S(1)} %get-tuple-element.182), kind=kCustom, calls=%fused_computation.15 | custom fusion | bytes 73728 | tf_op jit(solution)/shard_map/gather | solution.py:63
  101.2 11.6 %all_gather.7 = bf16[48,32,256]{2,1,0:T(8,128)(2,1)S(1)} all-gather(bf16[48,8,256]{2,1,0:T(8,128)(2,1)S(1)} %copy-done.54), channel_id=1, replica_groups=mesh['dp'=128,'mp'=4] {'mp'}, dimensions={1}, use_global_device_ids=true | all-gather | bytes 983040 | tf_op jit(solution)/shard_map/all_gather | solution.py:93
  114.1 3.0 scatter_custom_fusion.3
  117.6 2.8 reduce.26
  120.4 4.5 reshape.1255
  124.9 22.8 %all-to-all-start.1 = ((bf16[128,2,4096]{2,1,0:T(2,128)(2,1)}), bf16[128,2,4096]{2,1,0:T(2,128)(2,1)S(1)}, u32[]{:S(2)}, u32[]{:S(2)}) async-start(bf16[128,2,4096]{2,1,0:T(2,128)(2,1)} %reshape.1255), calls=%async_computation.1 | async-start | bytes 4194304 | tf_op jit(solution)/shard_map/all_to_all | solution.py:97
  148.1 12.3 %all_gather.6 = bf16[48,32,256]{2,1,0:T(8,128)(2,1)S(1)} all-gather(bf16[48,8,256]{2,1,0:T(8,128)(2,1)S(1)} %fusion.36), channel_id=1, replica_groups=mesh['dp'=128,'mp'=4] {'mp'}, dimensions={1}, use_global_device_ids=true | all-gather | bytes 983040 | tf_op jit(solution)/shard_map/all_gather | solution.py:92
  161.7 3.9 scatter_custom_fusion.2
  165.6 4.5 reduce.25
  170.1 4.5 reshape.1257
  174.5 72.3 %all-to-all-done.1 = bf16[128,2,4096]{2,1,0:T(2,128)(2,1)S(1)} async-done(((bf16[128,2,4096]{2,1,0:T(2,128)(2,1)}), bf16[128,2,4096]{2,1,0:T(2,128)(2,1)S(1)}, u32[]{:S(2)}, u32[]{:S(2)}) %all-to-all-start.1) | async-done | bytes 2097184 | tf_op jit(solution)/shard_map/all_to_all | solution.py:97
  246.8 9.2 all-to-all-start
  260.2 2.3 gather_fusion.5
  272.7 2.6 gather_fusion.10
  276.4 2.6 gather_fusion.12
  279.0 1.8 copy.270
  281.5 2.6 gather_fusion.14
  284.0 1.8 copy.274
  285.8 2.6 gather_fusion.16
  288.4 1.8 copy.278
  290.2 2.6 gather_fusion.18
  292.8 1.8 copy.282
  294.6 2.6 gather_fusion.20
  297.2 1.8 copy.286
  312.9 6.8 reshape.1256
  319.6 4.5 copy.423
  324.1 30.7 %all-to-all-done = bf16[128,2,4096]{2,1,0:T(2,128)(2,1)} async-done(((bf16[128,2,4096]{2,1,0:T(2,128)(2,1)}), bf16[128,2,4096]{2,1,0:T(2,128)(2,1)}, u32[]{:S(2)}, u32[]{:S(2)}) %all-to-all-start) | async-done | bytes 2097184 | tf_op jit(solution)/shard_map/all_to_all | solution.py:96
  354.8 22.3 %reshape.1258 = bf16[128,1,8192]{2,1,0:T(2,128)(2,1)} reshape(bf16[128,2,4096]{2,1,0:T(2,128)(2,1)} %all-to-all-done) | data formatting | bytes 4194304
  377.1 5.8 copy.424
  382.9 2.3 gather_fusion.9
  385.2 5.2 gather_fusion.7
  401.6 2.4 reshape_squeeze.42
  405.4 2.4 reshape_squeeze.40
  413.5 2.8 fusion.216
  418.8 2.8 fusion.213
  424.2 2.8 fusion.210
  429.6 2.8 fusion.207
  435.8 2.8 fusion.204
  442.1 2.8 fusion.201
  454.5 2.2 fusion.34
  462.9 1.9 fusion.32
  472.9 22.9 %reduce-scatter.5.cloned.1.call-done = bf16[8,16896]{1,0:T(8,128)(2,1)} async-done(((bf16[32,16896]{1,0:T(8,128)(2,1)}), bf16[8,16896]{1,0:T(8,128)(2,1)}) %reduce-scatter.5.cloned.1.call-update) | async-done | bytes 270352
  500.5 18.6 %all-to-all-start.2 = ((bf16[128,2,1024]{2,1,0:T(2,128)(2,1)}), bf16[128,2,1024]{2,1,0:T(2,128)(2,1)S(1)}, u32[]{:S(2)}, u32[]{:S(2)}) async-start(bf16[128,2,1024]{2,1,0:T(2,128)(2,1)} %reshape.1259), calls=%async_computation.2 | async-start | bytes 1048576 | tf_op jit(solution)/shard_map/all_to_all | solution.py:156
  519.7 32.7 %all-to-all-done.2 = bf16[128,2,1024]{2,1,0:T(2,128)(2,1)S(1)} async-done(((bf16[128,2,1024]{2,1,0:T(2,128)(2,1)}), bf16[128,2,1024]{2,1,0:T(2,128)(2,1)S(1)}, u32[]{:S(2)}, u32[]{:S(2)}) %all-to-all-start.2) | async-done | bytes 524320 | tf_op jit(solution)/shard_map/all_to_all | solution.py:156
  557.0 455.8 %all-reduce.3.cloned.1.call-done = f32[1024,256]{0,1:T(8,128)} async-done(((f32[1024,256]{0,1:T(8,128)}), f32[1024,256]{0,1:T(8,128)}) %all-reduce.3.cloned.1.call-update) | async-done | bytes 1048592
  (416 shorter events, 106.4 us)
Async XLA Ops:
  7.2 140.5 %copy-start = (bf16[48,8,1024]{2,1,0:T(8,128)(2,1)S(1)}, bf16[48,8,1024]{2,1,0:T(8,128)(2,1)}, u32[]{:S(2)}) copy-start(bf16[48,8,1024]{2,1,0:T(8,128)(2,1)} %param.24) | copy-start | bytes 2359300
  65.7 35.4 %copy-start.54 = (bf16[48,8,256]{2,1,0:T(8,128)(2,1)S(1)}, bf16[48,8,256]{2,1,0:T(8,128)(2,1)}, u32[]{:S(2)}) copy-start(bf16[48,8,256]{2,1,0:T(8,128)(2,1)} %param.25) | copy-start | bytes 589828
  101.1 13.0 %copy-start.97 = (s32[48]{0:T(128)}, s32[48]{0:T(128)S(1)}, u32[]{:S(2)}) copy-start(s32[48]{0:T(128)S(1)} %add_reduce_fusion) | copy-start | bytes 580
  101.2 60.6 %copy-start.99 = (s32[48]{0:T(128)}, s32[48]{0:T(128)S(1)}, u32[]{:S(2)}) copy-start(s32[48]{0:T(128)S(1)} %fusion.147) | copy-start | bytes 580
  124.9 22.8 %copy-start.38 = (bf16[1024,256]{1,0:T(8,128)(2,1)S(1)}, bf16[1024,256]{1,0:T(8,128)(2,1)}, u32[]{:S(2)}) copy-start(bf16[1024,256]{1,0:T(8,128)(2,1)} %param.26) | copy-start | bytes 1572868
  124.9 121.9 %all-to-all-start.1 = ((bf16[128,2,4096]{2,1,0:T(2,128)(2,1)}), bf16[128,2,4096]{2,1,0:T(2,128)(2,1)S(1)}, u32[]{:S(2)}, u32[]{:S(2)}) async-start(bf16[128,2,4096]{2,1,0:T(2,128)(2,1)} %reshape.1255), calls=%async_computation.1 | async-start | bytes 4194304 | tf_op jit(solution)/shard_map/all_to_all | solution.py:97
  174.5 81.5 %copy-start.2 = (s32[768]{0:T(1024)S(1)}, s32[768]{0:T(1024)}, u32[]{:S(2)}) copy-start(s32[768]{0:T(1024)} %param.20) | copy-start | bytes 9220
  246.8 108.0 %all-to-all-start = ((bf16[128,2,4096]{2,1,0:T(2,128)(2,1)}), bf16[128,2,4096]{2,1,0:T(2,128)(2,1)}, u32[]{:S(2)}, u32[]{:S(2)}) async-start(bf16[128,2,4096]{2,1,0:T(2,128)(2,1)} %reshape.1257), calls=%async_computation | async-start | bytes 4194304 | tf_op jit(solution)/shard_map/all_to_all | solution.py:96
  256.0 239.9 %reduce-scatter.5.cloned.1.call-start = ((), (), s32[]{:S(2)}) async-start(), calls=%async_computation.4 | async-start | bytes 1351680
  259.3 3.2 copy-start.58
  260.2 10.2 copy-start.56
  260.2 10.9 %copy-start.60 = (s32[6,4,128]{2,1,0:T(4,128)S(1)}, s32[6,4,128]{2,1,0:T(4,128)}, u32[]{:S(2)}) copy-start(s32[6,4,128]{2,1,0:T(4,128)} %param.23) | copy-start | bytes 36868
  294.6 4.4 copy-start.102
  297.2 12.4 %copy-start.17 = (bf16[4,128,256]{1,2,0:T(8,128)(2,1)S(1)}, bf16[4,128,256]{1,2,0:T(8,128)(2,1)}, u32[]{:S(2)}) copy-start(bf16[4,128,256]{1,2,0:T(8,128)(2,1)} %copy.270) | copy-start | bytes 786436
  307.9 2.7 copy-start.18
  307.9 2.7 copy-start.19
  307.9 2.7 copy-start.20
  385.2 5.2 copy-start.8
  395.7 4.5 copy-start.23
  398.7 5.3 copy-start.21
  404.0 5.2 copy-start.24
  407.7 4.2 copy-start.22
  409.1 4.3 copy-start.70
  409.1 4.4 copy-start.50
  416.3 2.5 copy-start.69
  421.6 2.5 copy-start.68
  432.4 2.4 copy-start.15
  438.6 2.4 copy-start.14
  447.5 2.5 copy-start.9
  447.5 2.5 copy-start.11
  447.5 2.5 copy-start.81
  447.5 2.6 copy-start.71
  447.6 2.4 copy-start.87
  447.6 2.5 copy-start.83
  448.3 2.6 copy-start.75
  454.5 4.8 copy-start.53
  459.3 3.6 copy-start.4
  462.9 4.5 copy-start.6
  462.9 4.5 copy-start.52
  498.3 20.9 %copy-start.100 = (s32[48]{0:T(128)S(1)}, s32[48]{0:T(128)}, u32[]{:S(2)}) copy-start(s32[48]{0:T(128)} %copy-done.99) | copy-start | bytes 580
  498.4 20.9 %copy-start.98 = (s32[48]{0:T(128)S(1)}, s32[48]{0:T(128)}, u32[]{:S(2)}) copy-start(s32[48]{0:T(128)} %copy-done.97) | copy-start | bytes 580
  498.4 21.0 %copy-start.10 = (f32[128,256]{0,1:T(8,128)S(1)}, f32[128,256]{0,1:T(8,128)}, u32[]{:S(2)}) copy-start(f32[128,256]{0,1:T(8,128)} %copy-done.9) | copy-start | bytes 393220
  498.4 21.0 %copy-start.88 = (f32[128]{0:T(128)S(1)}, f32[128]{0:T(128)}, u32[]{:S(2)}) copy-start(f32[128]{0:T(128)} %copy-done.87) | copy-start | bytes 1540
  498.4 21.0 %copy-start.90 = (f32[128]{0:T(128)S(1)}, f32[128]{0:T(128)}, u32[]{:S(2)}) copy-start(f32[128]{0:T(128)} %copy-done.89) | copy-start | bytes 1540
  499.4 20.2 %copy-start.72 = (f32[128]{0:T(128)S(1)}, f32[128]{0:T(128)}, u32[]{:S(2)}) copy-start(f32[128]{0:T(128)} %copy-done.71) | copy-start | bytes 1540
  500.5 51.9 %all-to-all-start.2 = ((bf16[128,2,1024]{2,1,0:T(2,128)(2,1)}), bf16[128,2,1024]{2,1,0:T(2,128)(2,1)S(1)}, u32[]{:S(2)}, u32[]{:S(2)}) async-start(bf16[128,2,1024]{2,1,0:T(2,128)(2,1)} %reshape.1259), calls=%async_computation.2 | async-start | bytes 1048576 | tf_op jit(solution)/shard_map/all_to_all | solution.py:156
  519.2 493.6 %all-reduce.3.cloned.1.call-start = ((), (), s32[]{:S(2)}) async-start(), calls=%async_computation.5 | async-start | bytes 2097152
  519.7 32.7 %copy-start.36 = (bf16[6,128,256]{1,2,0:T(8,128)(2,1)}, bf16[6,128,256]{1,2,0:T(8,128)(2,1)S(1)}, u32[]{:S(2)}) copy-start(bf16[6,128,256]{1,2,0:T(8,128)(2,1)S(1)} %fusion.107) | copy-start | bytes 1179652
  (60 other events, 98.3 us)
Sparse Core Ops, SparseCore 0:
  472.9 22.8 reduce-scatter.4
  555.8 457.0 all-reduce.2
where the time goes:
time: 1030 us; the launch traced here: 1020 us
  waiting for transfers between devices  614 us (60%)
  local copies, waits for them, and re-layouts  245 us (24%)
  starting transfers between devices  50.7 us (5%)
  other arithmetic  40 us (4%)
  matrix products  31.2 us (3%)
  blocking collectives  23.9 us (2%)
  between operations  16.3 us (2%)
    unnamed x4, waiting for transfers between devices  479 us
    all_to_all x1, waiting for transfers between devices, on_device(): lax.all_to_all(to_lanes(whole_keys), 'dp', split_axis=0, concat_axis=0, t...  72.3 us
    unnamed x237, local copies, waits for them, and re-layouts  68.1 us
    gather x1, local copies, waits for them, and re-layouts, on_device(): owner_at = (sample_of[camera_at] // SPD).reshape(owner_count, bin_size)  34.3 us
    all_to_all x1, waiting for transfers between devices, on_device(): lax.all_to_all(back_buffer, 'dp', split_axis=0, concat_axis=0, tiled=True)  32.7 us
    all_to_all x1, waiting for transfers between devices, on_device(): lax.all_to_all(to_lanes(whole_feat), 'dp', split_axis=0, concat_axis=0, t...  30.7 us
    gather x12, local copies, waits for them, and re-layouts, on_device(): picked = jnp.take(prev_bev[member], local_cells, axis=0).astype(jnp.float32)  25.6 us
    gather x1, local copies, waits for them, and re-layouts, on_device(): jnp.repeat(jnp.arange(sample_total, dtype=jnp.int32), cams, total_repeat_...  24.8 us
  transfers between devices with their start and end apart: 5, of which 5 were waited for; matrix products, arithmetic and copies ran while one was open for 8% of the time, Pallas kernels for 0%

commit v1 on v0

v1 whole, which is shorter than its diff:
```python
import jax
import jax.numpy as jnp
from jax import lax
from jax.experimental import pallas as pl
from jax.experimental.pallas import tpu as pltpu
from jax.sharding import PartitionSpec as P

HEADS = 8
KT = 4
SEEN = 3

NORM_EPS = 1e-05
MASKED = -1e30
BF16 = jnp.bfloat16
F32 = jnp.float32
I32 = jnp.int32


def dot(a, b, a_dim=1, b_dim=0):
    return lax.dot_general(a, b, (((a_dim,), (b_dim,)), ((), ())), preferred_element_type=F32)


def iota(shape, dim):
    return lax.broadcasted_iota(I32, shape, dim)


def vmem():
    return pl.BlockSpec(memory_space=pltpu.VMEM)


def smem():
    return pl.BlockSpec(memory_space=pltpu.SMEM)


def call(body, outs, *args, specs=None, scratch=(), cost=(1 << 20, 1 << 20)):
    return pl.pallas_call(
        body,
        out_shape=outs,
        in_specs=specs or [vmem()] * len(args),
        out_specs=jax.tree.map(lambda _: vmem(), outs),
        scratch_shapes=scratch,
        cost_estimate=pl.CostEstimate(flops=cost[0], bytes_accessed=cost[1], transcendentals=0),
    )(*args)


def pack_kernel(bin_ref, cams_ref, pack_ref, image_ref, key_ref, weight_ref, lane_ref, target_ref):
    samples, cameras = cams_ref.shape[1], pack_ref.shape[1]
    rows, channels = key_ref.shape
    lanes = lane_ref.shape[0]
    owners = lanes // target_ref.shape[0]
    quarter = target_ref.shape[0]
    slots = rows // quarter
    spd = samples // owners
    counts = cams_ref[...].astype(F32)
    before = iota((owners, samples), 1) < iota((owners, samples), 0) * spd
    start = jnp.sum(jnp.where(before, counts, 0.0), axis=1, keepdims=True)
    begun = start <= iota((owners, cameras), 1).astype(F32)
    owner = jnp.sum(begun.astype(F32), axis=0, keepdims=True) - 1.0
    here = (pack_ref[...] - bin_ref[0] * slots) == iota((slots, cameras), 0)
    owner_of = dot(jnp.broadcast_to(owner, (8, cameras)).astype(BF16), here.astype(F32).astype(BF16), 1, 1)
    spread = (iota((slots, rows), 1) // quarter == iota((slots, rows), 0)).astype(F32).astype(BF16)
    owner_of = dot(owner_of.astype(BF16), spread).astype(I32)
    target = owner_of * quarter + iota((8, rows), 1) % quarter
    target_ref[...] = target
    place = (iota((lanes, rows), 0) == target[:1]).astype(F32).astype(BF16)
    features = dot(image_ref[...], weight_ref[...]).astype(BF16)
    lane_ref[:, :channels] = dot(place, features).astype(BF16)
    lane_ref[:, channels:] = dot(place, key_ref[...]).astype(BF16)


def temporal_kernel(band_ref, query_ref, point_ref, prev_ref, align_ref, base_ref):
    samples, cells, channels = prev_ref.shape
    query = query_ref[...]
    head_dim = channels // HEADS
    wide = query.astype(F32)
    gates = []
    for k in range(KT):
        shape = (HEADS * KT, channels)
        pick = iota(shape, 0) == (iota(shape, 1) // head_dim) * KT + k
        weight = dot(point_ref[...], pick.astype(F32).astype(BF16)).astype(BF16)
        gates.append(jax.nn.sigmoid(dot(query, weight)))
    for m in range(samples):
        total = wide
        for k in range(KT):
            cell = align_ref[m, k : k + 1, :] - band_ref[0] * cells
            pick = (iota((cells, cells), 0) == cell).astype(F32).astype(BF16)
            total = total + gates[k] * dot(pick, prev_ref[m], 0, 0)
        base_ref[m] = total


def select_kernel(target_ref, lane_ref, out_ref):
    pick = (iota((out_ref.shape[0], lane_ref.shape[0]), 1) == target_ref[...]).astype(F32).astype(BF16)
    out_ref[...] = dot(pick, lane_ref[...]).astype(BF16)


def attention_kernel(count_ref, kv_ref, base_ref, cotangent_ref, query_ref, gain_ref, out_ref, grad_ref):
    parts, rows, width = kv_ref.shape
    channels = width // 2
    keys = parts * rows
    head_dim = channels // HEADS
    quarter = rows // SEEN
    count = count_ref[pl.program_id(0)]
    query, gain = query_ref[...], gain_ref[...]
    queries = query.shape[0]
    lane_head = iota((1, channels), 1) // head_dim
    masks = [(lane_head == h).astype(F32) for h in range(HEADS)]
    values = kv_ref[:, :, :channels].reshape(keys, channels)
    ray = kv_ref[:, :, channels:].reshape(keys, channels)
    ray = jnp.concatenate([ray * mask.astype(BF16) for mask in masks], axis=0)
    values = jnp.concatenate([values * mask.astype(BF16) for mask in masks], axis=0)
    scores = dot(ray, query, 1, 1) * (float(head_dim) ** -0.5)
    kept = iota((keys, queries), 0) % rows // quarter < count
    scores = jnp.where(kept[None], scores.reshape(HEADS, keys, queries), MASKED)
    raised = jnp.exp(scores - jnp.max(scores, axis=1, keepdims=True))
    probs = (raised / jnp.sum(raised, axis=1, keepdims=True)).astype(BF16)
    probs = probs.reshape(HEADS * keys, queries)
    pre_norm = base_ref[0] + dot(probs, values, 0, 0)
    centred = pre_norm - jnp.mean(pre_norm, axis=1, keepdims=True)
    scale = lax.rsqrt(jnp.mean(centred * centred, axis=1, keepdims=True) + NORM_EPS)
    unit = centred * scale
    out_ref[0] = (unit * gain).astype(BF16)
    pull = cotangent_ref[0].astype(F32) * gain
    pull = pull - jnp.mean(pull, axis=1, keepdims=True) - unit * jnp.mean(pull * unit, axis=1, keepdims=True)
    spread = dot(probs, (pull * scale).astype(BF16))
    total = spread[:keys] * masks[0]
    for h in range(1, HEADS):
        total = total + spread[h * keys : (h + 1) * keys] * masks[h]
    grad_ref[...] = total.astype(BF16).reshape(parts, rows, channels)


def return_kernel(target_ref, grad_ref, lane_ref):
    pick = (iota((lane_ref.shape[0], grad_ref.shape[0]), 0) == target_ref[...]).astype(F32).astype(BF16)
    lane_ref[...] = dot(pick, grad_ref[...]).astype(BF16)


def neck_kernel(target_ref, lane_ref, image_ref, out_ref, sum_ref):
    pick = (iota((lane_ref.shape[0], image_ref.shape[0]), 0) == target_ref[:1]).astype(F32).astype(BF16)
    grads = dot(pick, lane_ref[...], 0, 0).astype(BF16)
    total = dot(image_ref[...], grads, 0, 0)
    cores, pieces, chips, _ = out_ref.shape
    half = sum_ref.shape[2]
    for i in range(sum_ref.shape[0]):
        sum_ref[i] = total[:, i * half : (i + 1) * half]
        for c in range(cores):
            for j in range(pieces):
                out_ref[c, j, :, i * half : (i + 1) * half] = sum_ref.at[i][
                    pl.ds(c * pieces + j, chips, stride=cores * pieces), :
                ]


def on_device(
    cams,
    pack,
    visible,
    align,
    images,
    cam_keys,
    neck_weight,
    bev_query,
    prev_bev,
    point_weight,
    norm_gain,
    out_grad,
):
    owners = lax.axis_size("dp")
    bands = lax.axis_size("mp")
    owner_id = lax.axis_index("dp").astype(I32)
    band_id = lax.axis_index("mp").astype(I32)
    samples, max_cams, _ = visible.shape
    slots, quarter, depth = images.shape
    channels = neck_weight.shape[1]
    queries = bev_query.shape[0]
    rows = slots * quarter
    flat_images = images.reshape(rows, depth)
    lanes, target = call(
        pack_kernel,
        (
            jax.ShapeDtypeStruct((owners * quarter, 2 * channels), BF16),
            jax.ShapeDtypeStruct((8, rows), I32),
        ),
        owner_id[None],
        cams[None],
        pack[None],
        flat_images,
        cam_keys.reshape(rows, channels),
        neck_weight,
        specs=[smem()] + [vmem()] * 5,
    )
    got = lax.all_to_all(
        lanes.reshape(owners, quarter, 2 * channels), "dp", split_axis=0, concat_axis=0, tiled=True
    )
    base = call(
        temporal_kernel,
        jax.ShapeDtypeStruct((samples, queries, channels), F32),
        band_id[None],
        bev_query,
        point_weight,
        prev_bev,
        align,
        specs=[smem()] + [vmem()] * 4,
        cost=(1 << 30, 1 << 22),
    )
    first = owner_id * samples
    sample_ids = jnp.arange(cams.shape[0], dtype=I32)
    start = jnp.sum(jnp.where(sample_ids < first, cams, 0))
    local = lax.dynamic_slice(cams, (first,), (samples,))
    window = samples * max_cams
    padded = jnp.concatenate([pack, jnp.zeros((window,), I32)])
    bins = lax.dynamic_slice(padded, (start,), (window,)) // slots
    member = jnp.arange(samples, dtype=I32)
    offset = jnp.sum(jnp.where(member[None, :] < member[:, None], local[None, :], 0), axis=1)
    camera = jnp.arange(max_cams, dtype=I32)
    seen = (visible > 0).astype(I32)
    earlier = (camera[:, None] < camera[None, :]).astype(I32)
    rank = jnp.sum(seen[:, :, None, :] * earlier[None, :, :, None], axis=1)
    place = jnp.arange(SEEN, dtype=I32)
    chosen = (rank[:, :, :, None] == place) & (seen[:, :, :, None] > 0)
    position = jnp.sum(
        jnp.where(chosen, offset[:, None, None, None] + camera[None, :, None, None] + 1, 0), axis=1
    )
    in_window = position[..., None] == jnp.arange(1, window + 1, dtype=I32)
    lane_of = jnp.sum(jnp.where(in_window, bins + 1, 0), axis=-1) - 1
    lane_of = lane_of.transpose(1, 0, 2).reshape(bands * samples * SEEN)
    count = lax.dynamic_slice_in_dim(jnp.sum(seen, axis=1), band_id, 1, axis=1)[:, 0]
    token = jnp.arange(quarter, dtype=I32)
    picks = jnp.where(lane_of[:, None] >= 0, lane_of[:, None] * quarter + token, -1).reshape(-1)
    piece = samples * SEEN * quarter
    chosen_kv = call(
        select_kernel,
        jax.ShapeDtypeStruct((bands * piece, 2 * channels), BF16),
        picks[:, None],
        got.reshape(owners * quarter, 2 * channels),
    )
    kv = lax.all_to_all(
        chosen_kv.reshape(bands, piece, 2 * channels), "mp", split_axis=0, concat_axis=0, tiled=True
    )
    step = SEEN * quarter
    bev_out, grads = pl.pallas_call(
        attention_kernel,
        grid_spec=pltpu.PrefetchScalarGridSpec(
            num_scalar_prefetch=1,
            grid=(samples,),
            in_specs=[
                pl.BlockSpec((bands, step, 2 * channels), lambda m, _: (0, m, 0)),
                pl.BlockSpec((1, queries, channels), lambda m, _: (m, 0, 0)),
                pl.BlockSpec((1, queries, channels), lambda m, _: (m, 0, 0)),
                pl.BlockSpec((queries, channels), lambda m, _: (0, 0)),
                pl.BlockSpec((1, channels), lambda m, _: (0, 0)),
            ],
            out_specs=[
                pl.BlockSpec((1, queries, channels), lambda m, _: (m, 0, 0)),
                pl.BlockSpec((bands, step, channels), lambda m, _: (0, m, 0)),
            ],
        ),
        out_shape=(
            jax.ShapeDtypeStruct((samples, queries, channels), BF16),
            jax.ShapeDtypeStruct((bands, piece, channels), BF16),
        ),
    )(count, kv, base, out_grad, bev_query, norm_gain[None])
    grads = lax.all_to_all(grads, "mp", split_axis=0, concat_axis=0, tiled=True)
    back = call(
        return_kernel,
        jax.ShapeDtypeStruct((owners * quarter, channels), BF16),
        picks[None],
        grads.reshape(bands * piece, channels),
    )
    back = lax.all_to_all(
        back.reshape(owners, quarter, channels), "dp", split_axis=0, concat_axis=0, tiled=True
    )
    chips = owners // 2
    share = depth // (owners * bands)
    neck = call(
        neck_kernel,
        jax.ShapeDtypeStruct((2, bands * share, chips, channels), F32),
        target,
        back.reshape(owners * quarter, channels),
        flat_images,
        scratch=[pltpu.VMEM((channels // 128, depth, 128), F32)],
    )
    pairs = [[2 * i, 2 * i + 1] for i in range(chips)]
    neck = lax.all_to_all(
        neck.reshape(2, bands * share * chips, channels),
        "dp",
        split_axis=0,
        concat_axis=0,
        tiled=True,
        axis_index_groups=pairs,
    )
    neck = jnp.sum(neck, axis=0).reshape(bands, share * chips, channels)
    neck = lax.all_to_all(neck, "mp", split_axis=0, concat_axis=0, tiled=True)
    neck = jnp.sum(neck, axis=0).reshape(share, chips, channels).transpose(1, 0, 2)
    sides = [[2 * i + c for i in range(chips)] for c in range(2)]
    neck = lax.all_to_all(
        neck, "dp", split_axis=0, concat_axis=0, tiled=True, axis_index_groups=sides
    )
    return bev_out, jnp.sum(neck, axis=0) / cams.shape[0]


def solution(mesh):
    return jax.shard_map(
        on_device,
        mesh=mesh,
        in_specs=(
            P(),
            P(),
            P("dp", None, None),
            P("dp", None, "mp"),
            P("dp", "mp", None),
            P("dp", "mp", None),
            P(),
            P("mp", None),
            P("dp", "mp", None),
            P(),
            P(),
            P("dp", "mp", None),
        ),
        out_specs=(P("dp", "mp", None), P(("dp", "mp"), None)),
        check_vma=False,
    )
```

time: 1030 us -> 208 us (0.20)
  waiting for transfers between devices: 614 us -> 56.1 us
  local copies, waits for them, and re-layouts: 245 us -> 7.6 us
  blocking collectives: 23.9 us -> 83.1 us
  other arithmetic: 40 us -> 3.02 us
  matrix products: 31.2 us -> 0 us
  Pallas kernels: 0 us -> 25.7 us
  starting transfers between devices: 50.7 us -> 28.2 us
  between operations: 16.3 us -> 2.71 us
    unnamed x4 -> x0, waiting for transfers between devices: 479 us -> none
    gather x33 -> x0, local copies, waits for them, and re-layouts: 105 us -> none  [the longest x1 34.3 us: on_device(): owner_at = (sample_of[camera_at] // SPD).reshape(owner_count, bin_size)]
    all_to_all x0 -> x4, blocking collectives: none -> 83.1 us  [the longest x1 45.8 us: on_device(): lax.all_to_all(back.reshape(owners, quarter, channels), 'dp', split_axis=...]
    all_to_all x3, waiting for transfers between devices: 136 us -> 56.1 us  [the longest x1 48.7 us: on_device(): lax.all_to_all(lanes.reshape(owners, quarter, 2 * channels), 'dp', split_...]
    unnamed x237 -> x15, local copies, waits for them, and re-layouts: 68.1 us -> 3.93 us
    scatter x5 -> x0, local copies, waits for them, and re-layouts: 31 us -> none  [the longest x1 23 us: on_device(): camera_at = jnp.zeros((camera_total,), jnp.int32).at[pack].set(jnp.arange...]
    another operation x25 -> x0, local copies, waits for them, and re-layouts: 25.9 us -> none  [the longest x6 10.7 us: on_device(): value_heads = own_feat[member].reshape(MAXCAM * tokens, HEADS, head_dim)]
    pallas_call x0 -> x6, Pallas kernels: none -> 25.7 us  [the longest x5 16.5 us: call(): pl.pallas_call(body, out_shape=outs, in_specs=specs or [vmem()] * len(arg...]
  transfers between devices with their start and end apart: 5 -> 3, of which waited for: 5 -> 3; matrix products, arithmetic and copies ran while one was open for 8% -> 3% of each run, Pallas kernels for 0% -> 2%
where the time goes in v1:
time: 208 us; the launch traced here: 206 us
  blocking collectives  83.1 us (40%)
  waiting for transfers between devices  56.1 us (27%)
  starting transfers between devices  28.2 us (14%)
  Pallas kernels  25.7 us (12%)
  local copies, waits for them, and re-layouts  7.6 us (4%)
  other arithmetic  3.02 us (1%)
  between operations  2.71 us (1%)
    all_to_all x1, waiting for transfers between devices, on_device(): lax.all_to_all(lanes.reshape(owners, quarter, 2 * channels), 'dp', split_...  48.7 us
    all_to_all x1, blocking collectives, on_device(): lax.all_to_all(back.reshape(owners, quarter, channels), 'dp', split_axis=...  45.8 us
    all_to_all x1, starting transfers between devices, on_device(): lax.all_to_all(lanes.reshape(owners, quarter, 2 * channels), 'dp', split_...  20.6 us
    all_to_all x1, blocking collectives, on_device(): lax.all_to_all(neck, 'dp', split_axis=0, concat_axis=0, tiled=True, axis_...  19.1 us
    pallas_call x5, Pallas kernels, call(): pl.pallas_call(body, out_shape=outs, in_specs=specs or [vmem()] * len(arg...  16.5 us
    all_to_all x1, blocking collectives, on_device(): neck = lax.all_to_all(neck, 'mp', split_axis=0, concat_axis=0, tiled=True)  11.6 us
    pallas_call x1, Pallas kernels, on_device(): pl.pallas_call(attention_kernel, grid_spec=pltpu.PrefetchScalarGridSpec(n...  9.24 us
    all_to_all x1, blocking collectives, on_device(): lax.all_to_all(neck.reshape(2, bands * share * chips, channels), 'dp', sp...  6.51 us
  transfers between devices with their start and end apart: 3, of which 3 were waited for; matrix products, arithmetic and copies ran while one was open for 3% of the time, Pallas kernels for 2%

profile of v1, /device:TPU:1, one launch (start us, length us, event | category | flops | bytes accessed | tf_op | source)
XLA Modules:
  0.0 206.3 jit_solution(13065123671084348249)
XLA Ops:
  0.6 0.7 copy-done.6
  1.3 0.6 broadcast_in_dim.92.cams_ref
  1.9 4.2 %shard_map.131 = (bf16[1024,512]{1,0:T(8,128)(2,1)}, s32[8,384]{1,0:T(8,128)}) custom-call(s32[1]{0:T(128)} %bitcast.2.bin_ref, s32[1,768]{1,0:T(1,128)} %broadcast_in_dim.92.cams_ref, s32[1,6144]{1,0:T(1,128)} %bitcast.33, bf16[384,1024]{1,0:T(8,128)(2,1)} %bitcast.23, bf16[384,256]{1,0:T(8,128)(2,1)} %bitcast.32, bf16[1024,256]{1,0:T(8,128)(2,1)} %weight_ref.1), custom_call_target="tpu_custom_call" | custom-call | flops 1048576 | bytes 1048576 | tf_op jit(solution)/shard_map/pallas_call | solution.py:36
  6.1 20.6 %all-to-all-start = ((bf16[128,8,512]{2,1,0:T(8,128)(2,1)}), bf16[128,8,512]{2,1,0:T(8,128)(2,1)S(1)}, u32[]{:S(2)}, u32[]{:S(2)}) async-start(bf16[128,8,512]{2,1,0:T(8,128)(2,1)} %bitcast.30), calls=%async_computation | async-start | bytes 2097152 | tf_op jit(solution)/shard_map/all_to_all | solution.py:189
  26.6 0.0 copy-start.4
  26.6 0.6 select_reduce_fusion.2
  28.6 0.1 dynamic_slice.10
  28.7 0.0 copy-done.4
  28.7 0.0 copy-start.3
  28.7 0.1 copy.30
  29.5 0.0 copy-done.3
  29.5 0.1 fusion.2
  29.6 0.1 select_reduce_fusion.3
  29.7 0.1 multiply_reduce_fusion
  29.8 0.1 add_add_fusion
  29.9 0.4 select_reduce_fusion.1
  30.3 0.5 select_reduce_fusion
  30.8 0.1 copy.32
  30.9 0.1 mul.40
  31.0 0.1 copy.31
  31.2 0.1 ge.20
  31.3 0.1 add_select_fusion
  31.4 0.9 select_n.65.target_ref
  32.3 48.7 %all-to-all-done = bf16[128,8,512]{2,1,0:T(8,128)(2,1)S(1)} async-done(((bf16[128,8,512]{2,1,0:T(8,128)(2,1)}), bf16[128,8,512]{2,1,0:T(8,128)(2,1)S(1)}, u32[]{:S(2)}, u32[]{:S(2)}) %all-to-all-start) | async-done | bytes 1048608 | tf_op jit(solution)/shard_map/all_to_all | solution.py:189
  81.0 1.0 copy-done
  82.0 3.0 %shard_map.132 = bf16[576,512]{1,0:T(8,128)(2,1)} custom-call(s32[576,1]{1,0:T(8,128)} %select_n.65.target_ref, bf16[1024,512]{1,0:T(8,128)(2,1)} %bitcast.22), custom_call_target="tpu_custom_call" | custom-call | flops 1048576 | bytes 1048576 | tf_op jit(solution)/shard_map/pallas_call | solution.py:36
  85.0 4.1 %all-to-all-start.1 = ((bf16[4,144,512]{2,1,0:T(8,128)(2,1)}), bf16[4,144,512]{2,1,0:T(8,128)(2,1)S(1)}, u32[]{:S(2)}, u32[]{:S(2)}) async-start(bf16[4,144,512]{2,1,0:T(8,128)(2,1)} %bitcast.25), calls=%async_computation.1 | async-start | bytes 1179648 | tf_op jit(solution)/shard_map/all_to_all | solution.py:234
  89.1 0.7 copy.34.point_ref
  89.8 0.2 fusion.3
  90.0 0.8 dynamic-slice_reduce_fusion.count_ref
  90.8 3.4 %shard_map.133.base_ref = f32[6,128,256]{2,1,0:T(8,128)} custom-call(s32[1]{0:T(128)} %bitcast.9.band_ref, bf16[128,256]{1,0:T(8,128)(2,1)} %query_ref.3, bf16[256,32]{1,0:T(8,128)(2,1)} %copy.34.point_ref, bf16[6,128,256]{2,1,0:T(8,128)(2,1)} %prev_ref.1, s32[6,4,128]{2,1,0:T(4,128)} %align_ref.1), custom_call_target="tpu_custom_call" | custom-call | flops 1073741824 | bytes 4194304 | tf_op jit(solution)/shard_map/pallas_call | solution.py:36
  94.2 2.4 %all-to-all-done.1.kv_ref = bf16[4,144,512]{2,1,0:T(8,128)(2,1)S(1)} async-done(((bf16[4,144,512]{2,1,0:T(8,128)(2,1)}), bf16[4,144,512]{2,1,0:T(8,128)(2,1)S(1)}, u32[]{:S(2)}, u32[]{:S(2)}) %all-to-all-start.1) | async-done | bytes 589856 | tf_op jit(solution)/shard_map/all_to_all | solution.py:234
  96.5 0.8 copy-done.1
  97.4 9.2 %shard_map.134 = (bf16[6,128,256]{2,1,0:T(8,128)(2,1)}, bf16[4,144,256]{2,1,0:T(8,128)(2,1)}) custom-call(s32[6]{0:T(128)} %dynamic-slice_reduce_fusion.count_ref, bf16[4,144,512]{2,1,0:T(8,128)(2,1)} %copy-done.1, f32[6,128,256]{2,1,0:T(8,128)} %shard_map.133.base_ref, bf16[6,128,256]{2,1,0:T(8,128)(2,1)} %cotangent_ref.1, bf16[128,256]{1,0:T(8,128)(2,1)} %query_ref.3, ...), custom_call_target="tpu_custom_call" | custom-call | tf_op jit(solution)/shard_map/pallas_call | solution.py:238
  106.6 3.5 %all-to-all-start.2 = ((bf16[4,144,256]{2,1,0:T(8,128)(2,1)}), bf16[4,144,256]{2,1,0:T(8,128)(2,1)S(1)}, u32[]{:S(2)}, u32[]{:S(2)}) async-start(bf16[4,144,256]{2,1,0:T(8,128)(2,1)} %get-tuple-element.9), calls=%async_computation.2 | async-start | bytes 589824 | tf_op jit(solution)/shard_map/all_to_all | solution.py:260
  110.1 0.7 select_n.64.target_ref
  110.7 5.0 %all-to-all-done.2 = bf16[4,144,256]{2,1,0:T(8,128)(2,1)S(1)} async-done(((bf16[4,144,256]{2,1,0:T(8,128)(2,1)}), bf16[4,144,256]{2,1,0:T(8,128)(2,1)S(1)}, u32[]{:S(2)}, u32[]{:S(2)}) %all-to-all-start.2) | async-done | bytes 294944 | tf_op jit(solution)/shard_map/all_to_all | solution.py:260
  115.7 0.7 copy-done.2
  116.4 2.3 %shard_map.135 = bf16[1024,256]{1,0:T(8,128)(2,1)} custom-call(s32[1,576]{1,0:T(1,128)} %select_n.64.target_ref, bf16[576,256]{1,0:T(8,128)(2,1)} %bitcast.29), custom_call_target="tpu_custom_call" | custom-call | flops 1048576 | bytes 1048576 | tf_op jit(solution)/shard_map/pallas_call | solution.py:36
  118.8 45.8 %all_to_all.35 = bf16[128,8,256]{2,1,0:T(8,128)(2,1)} all-to-all(bf16[128,8,256]{2,1,0:T(8,128)(2,1)} %bitcast.26), channel_id=1, replica_groups=mesh['dp'=128,'mp'=4] {'dp'}, dimensions={0} | all-to-all | bytes 1048576 | tf_op jit(solution)/shard_map/all_to_all | solution.py:267
  164.6 3.6 %shard_map.136 = f32[2,8,64,256]{3,2,1,0:T(8,128)} custom-call(s32[8,384]{1,0:T(8,128)} %get-tuple-element.8.target_ref, bf16[1024,256]{1,0:T(8,128)(2,1)} %bitcast.28, bf16[384,1024]{1,0:T(8,128)(2,1)} %bitcast.24), custom_call_target="tpu_custom_call" | custom-call | flops 1048576 | bytes 1048576 | tf_op jit(solution)/shard_map/pallas_call | solution.py:36
  168.2 6.5 %all_to_all.36 = f32[2,512,256]{2,1,0:T(8,128)S(1)} all-to-all(f32[2,512,256]{2,1,0:T(8,128)} %bitcast.21), channel_id=1, replica_groups={{0,4},{8,12},{16,20},{24,28},{32,36},{40,44},{48,52},{56,60},{64,68},{7..., dimensions={0} | all-to-all | bytes 2097152 | tf_op jit(solution)/shard_map/all_to_all | solution.py:281
  174.7 0.1 reduce_sum.87
  174.8 11.6 %all_to_all.37 = f32[4,128,256]{2,1,0:T(8,128)S(1)} all-to-all(f32[4,128,256]{2,1,0:T(8,128)S(1)} %bitcast.27), channel_id=1, replica_groups=mesh['dp'=128,'mp'=4] {'mp'}, dimensions={0} | all-to-all | bytes 1048576 | tf_op jit(solution)/shard_map/all_to_all | solution.py:290
  186.5 0.1 copy.35
  186.6 19.1 %all_to_all.38 = f32[64,2,256]{2,1,0:T(2,128)S(1)} all-to-all(f32[64,2,256]{2,1,0:T(2,128)S(1)} %copy.35), channel_id=1, replica_groups={{0,8,16,24,32,40,48,56,64,72,80,88,96,104,112,120,128,136,144,152,160,1..., dimensions={0} | all-to-all | bytes 262144 | tf_op jit(solution)/shard_map/all_to_all | solution.py:293
  205.7 0.1 reduce_sum.89
  205.8 0.6 broadcast_multiply_fusion
  (11 shorter events, 0.1 us)
Async XLA Ops:
  0.6 0.7 copy-start.6
  6.1 74.9 %all-to-all-start = ((bf16[128,8,512]{2,1,0:T(8,128)(2,1)}), bf16[128,8,512]{2,1,0:T(8,128)(2,1)S(1)}, u32[]{:S(2)}, u32[]{:S(2)}) async-start(bf16[128,8,512]{2,1,0:T(8,128)(2,1)} %bitcast.30), calls=%async_computation | async-start | bytes 2097152 | tf_op jit(solution)/shard_map/all_to_all | solution.py:189
  26.6 2.0 copy-start.4
  28.7 0.8 copy-start.3
  81.0 1.0 copy-start
  84.9 4.1 %copy-start.5 = (bf16[256,32]{0,1:T(8,128)(2,1)S(1)}, bf16[256,32]{0,1:T(8,128)(2,1)}, u32[]{:S(2)}) copy-start(bf16[256,32]{0,1:T(8,128)(2,1)} %param.21) | copy-start | bytes 49156
  85.0 11.6 %all-to-all-start.1 = ((bf16[4,144,512]{2,1,0:T(8,128)(2,1)}), bf16[4,144,512]{2,1,0:T(8,128)(2,1)S(1)}, u32[]{:S(2)}, u32[]{:S(2)}) async-start(bf16[4,144,512]{2,1,0:T(8,128)(2,1)} %bitcast.25), calls=%async_computation.1 | async-start | bytes 1179648 | tf_op jit(solution)/shard_map/all_to_all | solution.py:234
  96.5 0.8 copy-start.1
  106.6 9.1 %all-to-all-start.2 = ((bf16[4,144,256]{2,1,0:T(8,128)(2,1)}), bf16[4,144,256]{2,1,0:T(8,128)(2,1)S(1)}, u32[]{:S(2)}, u32[]{:S(2)}) async-start(bf16[4,144,256]{2,1,0:T(8,128)(2,1)} %get-tuple-element.9), calls=%async_computation.2 | async-start | bytes 589824 | tf_op jit(solution)/shard_map/all_to_all | solution.py:260
  115.7 0.7 copy-start.2

commit v2 on v1

v2 whole, which is shorter than its diff:
```python
import functools

import jax
import jax.numpy as jnp
from jax import lax
from jax.experimental import pallas as pl
from jax.experimental.pallas import tpu as pltpu
from jax.sharding import PartitionSpec as P

HEADS = 8
KT = 4
CORES = 2
Y_CHIPS = 4
SEEN = 3

NORM_EPS = 1e-05
MASKED = -1e30
BF16 = jnp.bfloat16
F32 = jnp.float32
I32 = jnp.int32


def dot(a, b, a_dim=1, b_dim=0):
    return lax.dot_general(a, b, (((a_dim,), (b_dim,)), ((), ())), preferred_element_type=F32)


def iota(shape, dim):
    return lax.broadcasted_iota(I32, shape, dim)


def vmem():
    return pl.BlockSpec(memory_space=pltpu.VMEM)


def smem():
    return pl.BlockSpec(memory_space=pltpu.SMEM)


def on_chip(shape, dtype):
    return pltpu.VMEM(shape, dtype)


def call(body, outs, *args, specs=None, scratch=(), cost=(1 << 20, 1 << 20), pinned=True):
    specs = specs or [vmem()] * len(args)
    if pinned:
        args = [
            pltpu.with_memory_space_constraint(arg, spec.memory_space) for arg, spec in zip(args, specs)
        ]
    return pl.pallas_call(
        body,
        out_shape=outs,
        in_specs=specs,
        out_specs=jax.tree.map(lambda _: vmem(), outs),
        scratch_shapes=scratch,
        cost_estimate=pl.CostEstimate(flops=cost[0], bytes_accessed=cost[1], transcendentals=0),
    )(*args)


def pack_kernel(
    bin_ref,
    cams_ref,
    pack_ref,
    image_hbm,
    key_hbm,
    weight_hbm,
    lane_ref,
    owner_ref,
    image_ref,
    key_ref,
    weight_ref,
    sems,
):
    moves = [
        pltpu.make_async_copy(source, target, sems.at[i])
        for i, (source, target) in enumerate(
            ((image_hbm, image_ref), (weight_hbm, weight_ref), (key_hbm, key_ref))
        )
    ]
    for move in moves:
        move.start()
    cameras = pack_ref.shape[1]
    rows, channels = key_ref.shape
    slots = owner_ref.shape[1]
    quarter = rows // slots
    lanes = lane_ref.shape[0]
    owners = lanes // quarter
    groups, width = cams_ref.shape
    spd = groups * width // owners
    first = iota((owners, width), 0) * spd
    before = jnp.zeros((owners, width), F32)
    for g in range(groups):
        counts = cams_ref[g : g + 1, :].astype(F32)
        before += jnp.where(iota((owners, width), 1) + g * width < first, counts, 0.0)
    start = jnp.sum(before, axis=1, keepdims=True)
    here = (pack_ref[...] - bin_ref[0] * slots) == iota((slots, cameras), 0)
    here = here.astype(F32).astype(BF16)
    number = iota((8, cameras), 1)
    high = dot((number // 64).astype(F32).astype(BF16), here, 1, 1)
    low = dot((number % 64).astype(F32).astype(BF16), here, 1, 1)
    camera = (high * 64.0 + low)[:1]
    owner = jnp.sum((start <= camera).astype(F32), axis=0, keepdims=True) - 1.0
    owner = jnp.broadcast_to(owner, (8, slots))
    owner_ref[...] = owner.astype(I32)
    spread = (iota((slots, rows), 1) // quarter == iota((slots, rows), 0)).astype(F32).astype(BF16)
    target = dot(owner.astype(BF16), spread).astype(I32) * quarter + iota((8, rows), 1) % quarter
    place = (iota((lanes, rows), 0) == target[:1]).astype(F32).astype(BF16)
    moves[0].wait()
    moves[1].wait()
    features = dot(image_ref[...], weight_ref[...]).astype(BF16)
    lane_ref[:, :channels] = dot(place, features).astype(BF16)
    moves[2].wait()
    lane_ref[:, channels:] = dot(place, key_ref[...]).astype(BF16)


def turn_kernel(image_ref, out_ref, turned_ref, *, chips, depth, bands, share):
    turned = image_ref[...].astype(F32).T
    width = turned_ref.shape[2]
    for g in range(turned_ref.shape[0]):
        turned_ref[g] = turned[:, g * width : (g + 1) * width]
    step = CORES * bands * share
    at = 0
    for c in range(CORES):
        for y in range(chips):
            for j in range(bands * share):
                first = y * depth * step + c * bands * share + j
                for g in range(turned_ref.shape[0]):
                    part = turned_ref.at[g][pl.ds(first, depth, stride=step), :]
                    out_ref[at : at + depth, g * width : (g + 1) * width] = part.astype(BF16)
                at += depth


def temporal_kernel(band_ref, query_ref, point_ref, prev_ref, align_ref, base_ref):
    samples, cells, channels = prev_ref.shape
    query = query_ref[...]
    head_dim = channels // HEADS
    wide = query.astype(F32)
    gates = []
    for k in range(KT):
        shape = (HEADS * KT, channels)
        pick = iota(shape, 0) == (iota(shape, 1) // head_dim) * KT + k
        weight = dot(point_ref[...], pick.astype(F32).astype(BF16)).astype(BF16)
        gates.append(jax.nn.sigmoid(dot(query, weight)))
    for m in range(samples):
        total = wide
        for k in range(KT):
            cell = align_ref[m, k : k + 1, :] - band_ref[0] * cells
            pick = (iota((cells, cells), 0) == cell).astype(F32).astype(BF16)
            total = total + gates[k] * dot(pick, prev_ref[m], 0, 0)
        base_ref[m] = total


def select_kernel(source_ref, lane_ref, out_ref):
    for e in range(out_ref.shape[0]):
        out_ref[e] = lane_ref[source_ref[e]]


def attention_kernel(
    count_ref, kv_ref, base_ref, cotangent_ref, query_ref, gain_ref, out_ref, grad_ref
):
    parts, rows, width = kv_ref.shape
    samples, queries, channels = base_ref.shape
    step = rows // samples
    keys = parts * step
    head_dim = channels // HEADS
    quarter = step // SEEN
    query, gain = query_ref[...], gain_ref[...]
    lane_head = iota((1, channels), 1) // head_dim
    masks = [(lane_head == h).astype(F32) for h in range(HEADS)]
    place = iota((keys, queries), 0) % step // quarter
    for m in range(samples):
        here = slice(m * step, (m + 1) * step)
        values = kv_ref[:, here, :channels].reshape(keys, channels)
        ray = kv_ref[:, here, channels:].reshape(keys, channels)
        ray = jnp.concatenate([ray * mask.astype(BF16) for mask in masks], axis=0)
        values = jnp.concatenate([values * mask.astype(BF16) for mask in masks], axis=0)
        scores = dot(ray, query, 1, 1) * (float(head_dim) ** -0.5)
        scores = jnp.where((place < count_ref[m])[None], scores.reshape(HEADS, keys, queries), MASKED)
        raised = jnp.exp(scores - jnp.max(scores, axis=1, keepdims=True))
        probs = (raised * (1.0 / jnp.sum(raised, axis=1, keepdims=True))).astype(BF16)
        probs = probs.reshape(HEADS * keys, queries)
        pre_norm = base_ref[m] + dot(probs, values, 0, 0)
        centred = pre_norm - jnp.mean(pre_norm, axis=1, keepdims=True)
        scale = lax.rsqrt(jnp.mean(centred * centred, axis=1, keepdims=True) + NORM_EPS)
        unit = centred * scale
        out_ref[m] = (unit * gain).astype(BF16)
        pull = cotangent_ref[m].astype(F32) * gain
        pull = (
            pull
            - jnp.mean(pull, axis=1, keepdims=True)
            - unit * jnp.mean(pull * unit, axis=1, keepdims=True)
        )
        spread = dot(probs, (pull * scale).astype(BF16))
        total = spread[:keys] * masks[0]
        for h in range(1, HEADS):
            total = total + spread[h * keys : (h + 1) * keys] * masks[h]
        grad_ref[:, here, :] = total.astype(BF16).reshape(parts, step, channels)


def return_kernel(source_ref, grad_ref, lane_ref, sum_ref):
    sum_ref[...] = jnp.zeros(sum_ref.shape, F32)
    for e in range(grad_ref.shape[0]):
        lane = source_ref[e]
        sum_ref[lane] = sum_ref[lane] + grad_ref[e].astype(F32)
    lane_ref[...] = sum_ref[...].astype(BF16)


def neck_kernel(owner_ref, lane_ref, turned_ref, out_ref, grad_ref):
    quarter = lane_ref.shape[1]
    for s in range(grad_ref.shape[0] // quarter):
        grad_ref[s * quarter : (s + 1) * quarter, :] = lane_ref[owner_ref[s]]
    out_ref[...] = dot(turned_ref[...], grad_ref[...])


def on_device(
    cams,
    pack,
    visible,
    align,
    images,
    cam_keys,
    neck_weight,
    bev_query,
    prev_bev,
    point_weight,
    norm_gain,
    out_grad,
):
    owners = lax.axis_size("dp")
    bands = lax.axis_size("mp")
    owner_id = lax.axis_index("dp").astype(I32)
    band_id = lax.axis_index("mp").astype(I32)
    samples, max_cams, _ = visible.shape
    slots, quarter, depth = images.shape
    channels = neck_weight.shape[1]
    queries = bev_query.shape[0]
    rows = slots * quarter
    flat_images = images.reshape(rows, depth)
    lanes, owner = call(
        pack_kernel,
        (
            jax.ShapeDtypeStruct((owners * quarter, 2 * channels), BF16),
            jax.ShapeDtypeStruct((8, slots), I32),
        ),
        owner_id[None],
        cams.reshape(-1, min(128, cams.shape[0])),
        pack[None],
        flat_images,
        cam_keys.reshape(rows, channels),
        neck_weight,
        specs=[smem()] + [vmem()] * 2 + [pl.BlockSpec(memory_space=pl.ANY)] * 3,
        scratch=[
            pltpu.VMEM((rows, depth), BF16),
            pltpu.VMEM((rows, channels), BF16),
            pltpu.VMEM((depth, channels), BF16),
            pltpu.SemaphoreType.DMA((3,)),
        ],
        pinned=False,
    )
    got = lax.all_to_all(
        lanes.reshape(owners, quarter, 2 * channels), "dp", split_axis=0, concat_axis=0, tiled=True
    )
    cost = 1 << 30, 1 << 22
    chips = Y_CHIPS
    deep = owners // (CORES * chips)
    share = depth // (owners * bands)
    lanes_wide = min(128, rows)
    turned = call(
        functools.partial(turn_kernel, chips=chips, depth=deep, bands=bands, share=share),
        on_chip((depth, rows), BF16),
        flat_images,
        scratch=[pltpu.VMEM((rows // lanes_wide, depth, lanes_wide), F32)],
        cost=cost,
    )
    base = call(
        temporal_kernel,
        on_chip((samples, queries, channels), F32),
        band_id[None],
        bev_query,
        point_weight,
        prev_bev,
        align,
        specs=[smem()] + [vmem()] * 4,
        cost=cost,
    )
    first = owner_id * samples
    sample_ids = jnp.arange(cams.shape[0], dtype=I32)
    start = jnp.sum(jnp.where(sample_ids < first, cams, 0))
    local = lax.dynamic_slice(cams, (first,), (samples,))
    window = samples * max_cams
    padded = jnp.concatenate([pack, jnp.zeros((window,), I32)])
    bins = lax.dynamic_slice(padded, (start,), (window,)) // slots
    member = jnp.arange(samples, dtype=I32)
    offset = jnp.sum(jnp.where(member[None, :] < member[:, None], local[None, :], 0), axis=1)
    camera = jnp.arange(max_cams, dtype=I32)
    seen = (visible > 0).astype(I32)
    earlier = (camera[:, None] < camera[None, :]).astype(I32)
    rank = jnp.sum(seen[:, :, None, :] * earlier[None, :, :, None], axis=1)
    place = jnp.arange(SEEN, dtype=I32)
    chosen = (rank[:, :, :, None] == place) & (seen[:, :, :, None] > 0)
    position = jnp.sum(
        jnp.where(chosen, offset[:, None, None, None] + camera[None, :, None, None] + 1, 0), axis=1
    )
    in_window = position[..., None] == jnp.arange(1, window + 1, dtype=I32)
    lane_of = jnp.sum(jnp.where(in_window, bins + 1, 0), axis=-1) - 1
    lane_of = lane_of.transpose(1, 0, 2).reshape(bands * samples * SEEN)
    count = lax.dynamic_slice_in_dim(jnp.sum(seen, axis=1), band_id, 1, axis=1)[:, 0]
    source = jnp.maximum(lane_of, 0)
    got, base, turned, source, count, owner = lax.optimization_barrier(
        (got, base, turned, source, count, owner[0])
    )
    piece = samples * SEEN * quarter
    chosen_kv = call(
        select_kernel,
        on_chip((bands * samples * SEEN, quarter, 2 * channels), BF16),
        source,
        got,
        specs=[smem(), vmem()],
    )
    kv = lax.all_to_all(
        chosen_kv.reshape(bands, piece, 2 * channels), "mp", split_axis=0, concat_axis=0, tiled=True
    )
    bev_out, grads = call(
        attention_kernel,
        (
            jax.ShapeDtypeStruct((samples, queries, channels), BF16),
            on_chip((bands, piece, channels), BF16),
        ),
        count,
        kv,
        base,
        out_grad,
        bev_query,
        norm_gain[None],
        specs=[smem()] + [vmem()] * 5,
    )
    grads = lax.all_to_all(grads, "mp", split_axis=0, concat_axis=0, tiled=True)
    back = call(
        return_kernel,
        on_chip((owners, quarter, channels), BF16),
        source,
        grads.reshape(bands * samples * SEEN, quarter, channels),
        specs=[smem(), vmem()],
        scratch=[pltpu.VMEM((owners, quarter, channels), F32)],
    )
    back = lax.all_to_all(back, "dp", split_axis=0, concat_axis=0, tiled=True)
    neck = call(
        neck_kernel,
        on_chip((depth, channels), F32),
        owner,
        back,
        turned,
        specs=[smem(), vmem(), vmem()],
        scratch=[pltpu.VMEM((rows, channels), BF16)],
    )

    def device(y, z, c):
        return (y * deep + z) * CORES + c

    def exchange(part, axis, groups):
        return lax.all_to_all(
            part, axis, split_axis=0, concat_axis=0, tiled=True, axis_index_groups=groups
        )

    ys, zs, cs = range(chips), range(deep), range(CORES)
    pairs = [[device(y, z, c) for c in cs] for y in ys for z in zs]
    planes = [
        [device(y, z, c) * bands + x for y in ys for x in range(bands)] for z in zs for c in cs
    ]
    columns = [[device(y, z, c) for z in zs] for y in ys for c in cs]
    neck = exchange(neck.reshape(CORES, depth // CORES, channels), "dp", pairs)
    neck = jnp.sum(neck, axis=0).reshape(chips * bands, share * deep, channels)
    neck = exchange(neck, ("dp", "mp"), planes)
    neck = jnp.sum(neck, axis=0).reshape(share, deep, channels).transpose(1, 0, 2)
    neck = exchange(neck, "dp", columns)
    return bev_out, jnp.sum(neck, axis=0) / cams.shape[0]


def solution(mesh):
    return jax.shard_map(
        on_device,
        mesh=mesh,
        in_specs=(
            P(),
            P(),
            P("dp", None, None),
            P("dp", None, "mp"),
            P("dp", "mp", None),
            P("dp", "mp", None),
            P(),
            P("mp", None),
            P("dp", "mp", None),
            P(),
            P(),
            P("dp", "mp", None),
        ),
        out_specs=(P("dp", "mp", None), P(("dp", "mp"), None)),
        check_vma=False,
    )
```

time: 208 us -> 192 us (0.923)
  blocking collectives: 83.1 us -> 99.3 us
  waiting for transfers between devices: 56.1 us -> 42.8 us
  Pallas kernels: 25.7 us -> 15.4 us
  starting transfers between devices: 28.2 us -> 20.7 us
    all_to_all x4 -> x6, blocking collectives: 83.1 us -> 99.3 us  [the longest x1 45.5 us: on_device(): back = lax.all_to_all(back, 'dp', split_axis=0, concat_axis=0, tiled=True)]
    pallas_call x6 -> x7, Pallas kernels: 25.7 us -> 15.4 us  [call(): pl.pallas_call(body, out_shape=outs, in_specs=specs, out_specs=jax.tree.m...]
    all_to_all x2 -> x0, starting transfers between devices: 7.59 us -> none  [the longest x1 4.14 us: on_device(): lax.all_to_all(chosen_kv.reshape(bands, piece, 2 * channels), 'mp', split...]
    all_to_all x2 -> x0, waiting for transfers between devices: 7.35 us -> none  [the longest x1 5 us: on_device(): grads = lax.all_to_all(grads, 'mp', split_axis=0, concat_axis=0, tiled=True)]
    all_to_all x1, waiting for transfers between devices: 48.7 us -> 42.8 us  [on_device(): lax.all_to_all(lanes.reshape(owners, quarter, 2 * channels), 'dp', split_...]
  transfers between devices with their start and end apart: 3 -> 1, of which waited for: 3 -> 1; matrix products, arithmetic and copies ran while one was open for 3% -> 3% of each run, Pallas kernels for 2% -> 1%
where the time goes in v2:
time: 192 us; the launch traced here: 191 us
  blocking collectives  99.3 us (52%)
  waiting for transfers between devices  42.8 us (22%)
  starting transfers between devices  20.7 us (11%)
  Pallas kernels  15.4 us (8%)
  local copies, waits for them, and re-layouts  7 us (4%)
  other arithmetic  2.87 us (1%)
  between operations  2.75 us (1%)
    all_to_all x1, blocking collectives, on_device(): back = lax.all_to_all(back, 'dp', split_axis=0, concat_axis=0, tiled=True)  45.5 us
    all_to_all x1, waiting for transfers between devices, on_device(): lax.all_to_all(lanes.reshape(owners, quarter, 2 * channels), 'dp', split_...  42.8 us
    all_to_all x3, blocking collectives, exchange(): lax.all_to_all(part, axis, split_axis=0, concat_axis=0, tiled=True, axis_...  34.4 us
    all_to_all x1, starting transfers between devices, on_device(): lax.all_to_all(lanes.reshape(owners, quarter, 2 * channels), 'dp', split_...  20.7 us
    pallas_call x7, Pallas kernels, call(): pl.pallas_call(body, out_shape=outs, in_specs=specs, out_specs=jax.tree.m...  15.4 us
    all_to_all x1, blocking collectives, on_device(): lax.all_to_all(chosen_kv.reshape(bands, piece, 2 * channels), 'mp', split...  11.4 us
    all_to_all x1, blocking collectives, on_device(): grads = lax.all_to_all(grads, 'mp', split_axis=0, concat_axis=0, tiled=True)  8.05 us
    unnamed x25, local copies, waits for them, and re-layouts  4.04 us
  transfers between devices with their start and end apart: 1, of which 1 were waited for; matrix products, arithmetic and copies ran while one was open for 3% of the time, Pallas kernels for 1%

profile of v2, /device:TPU:1, one launch (start us, length us, event | category | flops | bytes accessed | tf_op | source)
XLA Modules:
  0.0 190.9 jit_solution(7612946916013872323)
XLA Ops:
  0.6 4.7 %shard_map.131 = (bf16[1024,512]{1,0:T(8,128)(2,1)}, s32[8,48]{1,0:T(8,128)}) custom-call(s32[1]{0:T(128)} %bitcast.bin_ref, s32[6,128]{1,0:T(8,128)} %bitcast.30, s32[1,6144]{1,0:T(1,128)} %bitcast.29, bf16[384,1024]{1,0:T(8,128)(2,1)} %bitcast.22, bf16[384,256]{1,0:T(8,128)(2,1)} %bitcast.27, bf16[1024,256]{1,0:T(8,128)(2,1)} %weight_hbm.1), custom_call_target="tpu_custom_call" | custom-call | flops 1048576 | bytes 1048576 | tf_op jit(solution)/shard_map/pallas_call | solution.py:49
  5.4 0.0 copy-start.10
  5.4 0.0 copy-start
  5.4 20.7 %all-to-all-start = ((bf16[128,8,512]{2,1,0:T(8,128)(2,1)}), bf16[128,8,512]{2,1,0:T(8,128)(2,1)S(1)}, u32[]{:S(2)}, u32[]{:S(2)}) async-start(bf16[128,8,512]{2,1,0:T(8,128)(2,1)} %bitcast.26), calls=%async_computation | async-start | bytes 2097152 | tf_op jit(solution)/shard_map/all_to_all | solution.py:259
  26.1 0.0 copy-start.9
  26.1 0.0 copy-done.10
  26.1 0.6 select_reduce_fusion.2
  28.1 0.1 dynamic_slice.9
  28.2 0.0 copy-done.9
  28.2 0.0 copy-start.8
  28.2 0.1 copy.28
  29.0 0.0 copy-done.8
  29.0 0.1 fusion.2
  29.1 0.1 select_reduce_fusion.3
  29.2 0.1 multiply_reduce_fusion
  29.3 0.1 add_add_fusion
  29.4 0.4 select_reduce_fusion.1
  29.8 0.5 select_reduce_fusion
  30.3 0.1 copy.29
  30.4 0.6 max.15.source_ref
  31.1 0.1 copy-done.11
  31.2 0.1 copy.27.point_ref
  31.3 0.2 fusion.3
  31.5 0.8 dynamic-slice_reduce_fusion.count_ref
  32.2 0.0 copy-done
  32.2 0.8 shard_map.133.turned_ref
  33.0 0.1 copy-done.4
  33.1 1.0 copy-done.6
  34.1 1.5 shard_map.132.base_ref
  35.6 0.9 copy-done.1
  36.5 1.2 slice_bitcast_fusion.owner_ref
  37.7 42.8 %all-to-all-done.lane_ref = bf16[128,8,512]{2,1,0:T(8,128)(2,1)S(1)} async-done(((bf16[128,8,512]{2,1,0:T(8,128)(2,1)}), bf16[128,8,512]{2,1,0:T(8,128)(2,1)S(1)}, u32[]{:S(2)}, u32[]{:S(2)}) %all-to-all-start) | async-done | bytes 1048608 | tf_op jit(solution)/shard_map/all_to_all | solution.py:259
  80.5 0.7 shard_map.134
  81.2 0.0 copy-start.3
  81.2 11.4 %all_to_all.35.kv_ref = bf16[4,144,512]{2,1,0:T(8,128)(2,1)S(1)} all-to-all(bf16[4,144,512]{2,1,0:T(8,128)(2,1)S(1)} %bitcast.20), channel_id=1, replica_groups=mesh['dp'=128,'mp'=4] {'mp'}, dimensions={0} | all-to-all | bytes 1179648 | tf_op jit(solution)/shard_map/all_to_all | solution.py:319
  92.6 0.0 copy-done.3
  92.6 0.7 copy-done.5
  93.3 1.1 copy-done.2
  94.4 5.5 %shard_map.135 = (bf16[6,128,256]{2,1,0:T(8,128)(2,1)}, bf16[4,144,256]{2,1,0:T(8,128)(2,1)S(1)}) custom-call(s32[6]{0:T(128)} %dynamic-slice_reduce_fusion.count_ref, bf16[4,144,512]{2,1,0:T(8,128)(2,1)S(1)} %all_to_all.35.kv_ref, f32[6,128,256]{2,1,0:T(8,128)S(1)} %copy-done.2, bf16[6,128,256]{2,1,0:T(8,128)(2,1)S(1)} %copy-done.3, ...), custom_call_target="tpu_custom_call" | custom-call | flops 1048576 | bytes 1048576 | tf_op jit(solution)/shard_map/pallas_call | solution.py:49
  99.9 8.1 %all_to_all.36 = bf16[4,144,256]{2,1,0:T(8,128)(2,1)S(1)} all-to-all(bf16[4,144,256]{2,1,0:T(8,128)(2,1)S(1)} %get-tuple-element.20), channel_id=1, replica_groups=mesh['dp'=128,'mp'=4] {'mp'}, dimensions={0} | all-to-all | bytes 589824 | tf_op jit(solution)/shard_map/all_to_all | solution.py:336
  108.0 1.1 shard_map.136
  109.1 45.5 %all_to_all.37.lane_ref = bf16[128,8,256]{2,1,0:T(8,128)(2,1)S(1)} all-to-all(bf16[128,8,256]{2,1,0:T(8,128)(2,1)S(1)} %shard_map.136), channel_id=1, replica_groups=mesh['dp'=128,'mp'=4] {'dp'}, dimensions={0} | all-to-all | bytes 1048576 | tf_op jit(solution)/shard_map/all_to_all | solution.py:345
  154.7 1.1 shard_map.137
  155.8 5.4 %all_to_all.38 = f32[2,512,256]{2,1,0:T(8,128)S(1)} all-to-all(f32[2,512,256]{2,1,0:T(8,128)S(1)} %bitcast.19), channel_id=1, replica_groups={{0,4},{8,12},{16,20},{24,28},{32,36},{40,44},{48,52},{56,60},{64,68},{7..., dimensions={0} | all-to-all | bytes 2097152 | tf_op jit(solution)/shard_map/all_to_all | solution.py:360
  161.2 0.1 reduce_sum.87
  161.3 15.0 %all_to_all.39 = f32[16,32,256]{2,1,0:T(8,128)S(1)} all-to-all(f32[16,32,256]{2,1,0:T(8,128)S(1)} %bitcast.25), channel_id=1, replica_groups={{0,1,2,3,128,129,130,131,256,257,258,259,384,385,386,387},{4,5,6,7,132,..., dimensions={0} | all-to-all | bytes 1048576 | tf_op jit(solution)/shard_map/all_to_all | solution.py:360
  176.3 14.0 %all_to_all.40 = f32[16,2,256]{2,1,0:T(2,128)S(1)} all-to-all(f32[16,2,256]{2,1,0:T(2,128)S(1)} %copy.30), channel_id=1, replica_groups={{0,8,16,24,32,40,48,56,64,72,80,88,96,104,112,120},{4,12,20,28,36,44,52..., dimensions={0} | all-to-all | bytes 65536 | tf_op jit(solution)/shard_map/all_to_all | solution.py:360
  190.3 0.6 broadcast_multiply_fusion
  (14 shorter events, 0.1 us)
Async XLA Ops:
  5.4 20.8 %copy-start.10 = (s32[768]{0:T(1024)S(1)}, s32[768]{0:T(1024)}, u32[]{:S(2)}) copy-start(s32[768]{0:T(1024)} %param.12) | copy-start | bytes 9220
  5.4 26.8 %copy-start = (bf16[48,8,1024]{2,1,0:T(8,128)(2,1)S(1)}, bf16[48,8,1024]{2,1,0:T(8,128)(2,1)}, u32[]{:S(2)}) copy-start(bf16[48,8,1024]{2,1,0:T(8,128)(2,1)} %param.16) | copy-start | bytes 2359300
  5.4 75.1 %all-to-all-start = ((bf16[128,8,512]{2,1,0:T(8,128)(2,1)}), bf16[128,8,512]{2,1,0:T(8,128)(2,1)S(1)}, u32[]{:S(2)}, u32[]{:S(2)}) async-start(bf16[128,8,512]{2,1,0:T(8,128)(2,1)} %bitcast.26), calls=%async_computation | async-start | bytes 2097152 | tf_op jit(solution)/shard_map/all_to_all | solution.py:259
  26.1 2.0 %copy-start.9 = (s32[6,11,4]{1,2,0:T(4,128)S(1)}, s32[6,11,4]{1,2,0:T(4,128)}, u32[]{:S(2)}) copy-start(s32[6,11,4]{1,2,0:T(4,128)} %param.14) | copy-start | bytes 3172
  28.2 0.8 copy-start.8
  30.4 0.7 copy-start.11
  32.2 0.8 copy-start.4
  32.2 0.8 copy-start.7
  33.1 1.0 copy-start.6
  35.6 0.9 copy-start.1
  81.2 11.4 %copy-start.3 = (bf16[6,128,256]{2,1,0:T(8,128)(2,1)S(1)}, bf16[6,128,256]{2,1,0:T(8,128)(2,1)}, u32[]{:S(2)}) copy-start(bf16[6,128,256]{2,1,0:T(8,128)(2,1)} %cotangent_ref.1) | copy-start | bytes 1179652
  92.6 0.7 copy-start.5
  93.3 1.1 copy-start.2

commit v3 on v2

--- a/solution.py
+++ b/solution.py
@@ -52,28 +52,39 @@
         in_specs=specs,
         out_specs=jax.tree.map(lambda _: vmem(), outs),
         scratch_shapes=scratch,
+        compiler_params=pltpu.CompilerParams(vmem_limit_bytes=24 << 20),
         cost_estimate=pl.CostEstimate(flops=cost[0], bytes_accessed=cost[1], transcendentals=0),
     )(*args)
 
 
 def pack_kernel(
     bin_ref,
-    cams_ref,
-    pack_ref,
+    cams_hbm,
+    pack_hbm,
     image_hbm,
     key_hbm,
     weight_hbm,
     lane_ref,
     owner_ref,
+    cams_ref,
+    pack_ref,
     image_ref,
     key_ref,
     weight_ref,
+    feature_ref,
+    index_ref,
     sems,
 ):
     moves = [
         pltpu.make_async_copy(source, target, sems.at[i])
         for i, (source, target) in enumerate(
-            ((image_hbm, image_ref), (weight_hbm, weight_ref), (key_hbm, key_ref))
+            (
+                (cams_hbm, cams_ref),
+                (pack_hbm, pack_ref),
+                (image_hbm, image_ref),
+                (weight_hbm, weight_ref),
+                (key_hbm, key_ref),
+            )
         )
     ]
     for move in moves:
@@ -81,35 +92,37 @@
     cameras = pack_ref.shape[1]
     rows, channels = key_ref.shape
     slots = owner_ref.shape[1]
-    quarter = rows // slots
-    lanes = lane_ref.shape[0]
-    owners = lanes // quarter
+    owners, quarter, _ = lane_ref.shape
     groups, width = cams_ref.shape
     spd = groups * width // owners
+    lane_ref[...] = jnp.zeros(lane_ref.shape, BF16)
+    moves[0].wait()
     first = iota((owners, width), 0) * spd
     before = jnp.zeros((owners, width), F32)
     for g in range(groups):
         counts = cams_ref[g : g + 1, :].astype(F32)
         before += jnp.where(iota((owners, width), 1) + g * width < first, counts, 0.0)
     start = jnp.sum(before, axis=1, keepdims=True)
+    moves[1].wait()
     here = (pack_ref[...] - bin_ref[0] * slots) == iota((slots, cameras), 0)
     here = here.astype(F32).astype(BF16)
-    number = iota((8, cameras), 1)
-    high = dot((number // 64).astype(F32).astype(BF16), here, 1, 1)
-    low = dot((number % 64).astype(F32).astype(BF16), here, 1, 1)
-    camera = (high * 64.0 + low)[:1]
+    number = iota((16, cameras), 1)
+    digits = jnp.where(iota((16, cameras), 0) < 8, number // 64, number % 64)
+    digits = dot(digits.astype(F32).astype(BF16), here, 1, 1)
+    camera = digits[:1] * 64.0 + digits[8:9]
     owner = jnp.sum((start <= camera).astype(F32), axis=0, keepdims=True) - 1.0
-    owner = jnp.broadcast_to(owner, (8, slots))
-    owner_ref[...] = owner.astype(I32)
-    spread = (iota((slots, rows), 1) // quarter == iota((slots, rows), 0)).astype(F32).astype(BF16)
-    target = dot(owner.astype(BF16), spread).astype(I32) * quarter + iota((8, rows), 1) % quarter
-    place = (iota((lanes, rows), 0) == target[:1]).astype(F32).astype(BF16)
-    moves[0].wait()
-    moves[1].wait()
-    features = dot(image_ref[...], weight_ref[...]).astype(BF16)
-    lane_ref[:, :channels] = dot(place, features).astype(BF16)
+    owner_ref[...] = jnp.broadcast_to(owner, owner_ref.shape).astype(I32)
+    index = pltpu.make_async_copy(owner_ref, index_ref, sems.at[5])
+    index.start()
     moves[2].wait()
-    lane_ref[:, channels:] = dot(place, key_ref[...]).astype(BF16)
+    moves[3].wait()
+    feature_ref[...] = dot(image_ref[...], weight_ref[...]).astype(BF16)
+    index.wait()
+    moves[4].wait()
+    for s in range(slots):
+        here = slice(s * quarter, (s + 1) * quarter)
+        lane_ref[index_ref[0, s], :, :channels] = feature_ref[here, :]
+        lane_ref[index_ref[0, s], :, channels:] = key_ref[here, :]
 
 
 def turn_kernel(image_ref, out_ref, turned_ref, *, chips, depth, bands, share):
@@ -119,8 +132,8 @@
         turned_ref[g] = turned[:, g * width : (g + 1) * width]
     step = CORES * bands * share
     at = 0
-    for c in range(CORES):
-        for y in range(chips):
+    for y in range(chips):
+        for c in range(CORES):
             for j in range(bands * share):
                 first = y * depth * step + c * bands * share + j
                 for g in range(turned_ref.shape[0]):
@@ -129,17 +142,34 @@
                 at += depth
 
 
-def temporal_kernel(band_ref, query_ref, point_ref, prev_ref, align_ref, base_ref):
+def temporal_kernel(
+    band_ref,
+    query_ref,
+    point_ref,
+    prev_ref,
+    align_ref,
+    cotangent_ref,
+    gain_ref,
+    base_ref,
+    pull_ref,
+    heads_ref,
+    scale_ref,
+):
     samples, cells, channels = prev_ref.shape
     query = query_ref[...]
     head_dim = channels // HEADS
     wide = query.astype(F32)
+    gain = gain_ref[...]
+    scale_ref[...] = gain
     gates = []
     for k in range(KT):
         shape = (HEADS * KT, channels)
         pick = iota(shape, 0) == (iota(shape, 1) // head_dim) * KT + k
         weight = dot(point_ref[...], pick.astype(F32).astype(BF16)).astype(BF16)
         gates.append(jax.nn.sigmoid(dot(query, weight)))
+    for h in range(HEADS):
+        mask = (iota((1, channels), 1) // head_dim == h).astype(F32).astype(BF16)
+        heads_ref[h * cells : (h + 1) * cells, :] = query * mask
     for m in range(samples):
         total = wide
         for k in range(KT):
@@ -147,6 +177,8 @@
             pick = (iota((cells, cells), 0) == cell).astype(F32).astype(BF16)
             total = total + gates[k] * dot(pick, prev_ref[m], 0, 0)
         base_ref[m] = total
+        pull = cotangent_ref[m].astype(F32) * gain
+        pull_ref[m] = pull - jnp.mean(pull, axis=1, keepdims=True)
 
 
 def select_kernel(source_ref, lane_ref, out_ref):
@@ -154,46 +186,39 @@
         out_ref[e] = lane_ref[source_ref[e]]
 
 
-def attention_kernel(
-    count_ref, kv_ref, base_ref, cotangent_ref, query_ref, gain_ref, out_ref, grad_ref
-):
+def attention_kernel(count_ref, kv_ref, base_ref, pull_ref, heads_ref, gain_ref, out_ref, grad_ref):
     parts, rows, width = kv_ref.shape
     samples, queries, channels = base_ref.shape
     step = rows // samples
     keys = parts * step
     head_dim = channels // HEADS
     quarter = step // SEEN
-    query, gain = query_ref[...], gain_ref[...]
+    gain = gain_ref[...]
     lane_head = iota((1, channels), 1) // head_dim
-    masks = [(lane_head == h).astype(F32) for h in range(HEADS)]
-    place = iota((keys, queries), 0) % step // quarter
+    masks = [(lane_head == h).astype(F32).astype(BF16) for h in range(HEADS)]
+    place = iota((keys, HEADS * queries), 0) % step // quarter
     for m in range(samples):
         here = slice(m * step, (m + 1) * step)
         values = kv_ref[:, here, :channels].reshape(keys, channels)
         ray = kv_ref[:, here, channels:].reshape(keys, channels)
-        ray = jnp.concatenate([ray * mask.astype(BF16) for mask in masks], axis=0)
-        values = jnp.concatenate([values * mask.astype(BF16) for mask in masks], axis=0)
-        scores = dot(ray, query, 1, 1) * (float(head_dim) ** -0.5)
-        scores = jnp.where((place < count_ref[m])[None], scores.reshape(HEADS, keys, queries), MASKED)
-        raised = jnp.exp(scores - jnp.max(scores, axis=1, keepdims=True))
-        probs = (raised * (1.0 / jnp.sum(raised, axis=1, keepdims=True))).astype(BF16)
-        probs = probs.reshape(HEADS * keys, queries)
-        pre_norm = base_ref[m] + dot(probs, values, 0, 0)
+        values = jnp.concatenate([values * mask for mask in masks], axis=0)
+        scores = dot(ray, heads_ref[...], 1, 1) * (float(head_dim) ** -0.5)
+        scores = jnp.where(place < count_ref[m], scores, MASKED)
+        raised = jnp.exp(scores - jnp.max(scores, axis=0, keepdims=True))
+        probs = (raised * (1.0 / jnp.sum(raised, axis=0, keepdims=True))).astype(BF16)
+        tall = jnp.concatenate(
+            [probs[:, h * queries : (h + 1) * queries] for h in range(HEADS)], axis=0
+        )
+        pre_norm = base_ref[m] + dot(tall, values, 0, 0)
         centred = pre_norm - jnp.mean(pre_norm, axis=1, keepdims=True)
         scale = lax.rsqrt(jnp.mean(centred * centred, axis=1, keepdims=True) + NORM_EPS)
         unit = centred * scale
         out_ref[m] = (unit * gain).astype(BF16)
-        pull = cotangent_ref[m].astype(F32) * gain
-        pull = (
-            pull
-            - jnp.mean(pull, axis=1, keepdims=True)
-            - unit * jnp.mean(pull * unit, axis=1, keepdims=True)
-        )
-        spread = dot(probs, (pull * scale).astype(BF16))
-        total = spread[:keys] * masks[0]
-        for h in range(1, HEADS):
-            total = total + spread[h * keys : (h + 1) * keys] * masks[h]
-        grad_ref[:, here, :] = total.astype(BF16).reshape(parts, step, channels)
+        pull = pull_ref[m]
+        pull = pull - unit * jnp.mean(pull * unit, axis=1, keepdims=True)
+        pull = (pull * scale).astype(BF16)
+        pull = jnp.concatenate([pull * mask for mask in masks], axis=0)
+        grad_ref[:, here, :] = dot(probs, pull).astype(BF16).reshape(parts, step, channels)
 
 
 def return_kernel(source_ref, grad_ref, lane_ref, sum_ref):
@@ -208,7 +233,7 @@
     quarter = lane_ref.shape[1]
     for s in range(grad_ref.shape[0] // quarter):
         grad_ref[s * quarter : (s + 1) * quarter, :] = lane_ref[owner_ref[s]]
-    out_ref[...] = dot(turned_ref[...], grad_ref[...])
+    out_ref[...] = dot(turned_ref[...], grad_ref[...]).astype(BF16)
 
 
 def on_device(
@@ -238,27 +263,34 @@
     lanes, owner = call(
         pack_kernel,
         (
-            jax.ShapeDtypeStruct((owners * quarter, 2 * channels), BF16),
+            jax.ShapeDtypeStruct((owners, quarter, 2 * channels), BF16),
             jax.ShapeDtypeStruct((8, slots), I32),
         ),
         owner_id[None],
-        cams.reshape(-1, min(128, cams.shape[0])),
-        pack[None],
-        flat_images,
-        cam_keys.reshape(rows, channels),
-        neck_weight,
-        specs=[smem()] + [vmem()] * 2 + [pl.BlockSpec(memory_space=pl.ANY)] * 3,
+        *(
+            pltpu.with_memory_space_constraint(arg, pltpu.HBM)
+            for arg in (
+                cams.reshape(-1, min(128, cams.shape[0])),
+                pack[None],
+                flat_images,
+                cam_keys.reshape(rows, channels),
+                neck_weight,
+            )
+        ),
+        specs=[smem()] + [pl.BlockSpec(memory_space=pltpu.HBM)] * 5,
         scratch=[
+            pltpu.VMEM((cams.shape[0] // min(128, cams.shape[0]), min(128, cams.shape[0])), I32),
+            pltpu.VMEM((1, pack.shape[0]), I32),
             pltpu.VMEM((rows, depth), BF16),
             pltpu.VMEM((rows, channels), BF16),
             pltpu.VMEM((depth, channels), BF16),
-            pltpu.SemaphoreType.DMA((3,)),
+            pltpu.VMEM((rows, channels), BF16),
+            pltpu.SMEM((8, slots), I32),
+            pltpu.SemaphoreType.DMA((6,)),
         ],
         pinned=False,
     )
-    got = lax.all_to_all(
-        lanes.reshape(owners, quarter, 2 * channels), "dp", split_axis=0, concat_axis=0, tiled=True
-    )
+    got = lax.all_to_all(lanes, "dp", split_axis=0, concat_axis=0, tiled=True)
     cost = 1 << 30, 1 << 22
     chips = Y_CHIPS
     deep = owners // (CORES * chips)
@@ -271,15 +303,22 @@
         scratch=[pltpu.VMEM((rows // lanes_wide, depth, lanes_wide), F32)],
         cost=cost,
     )
-    base = call(
+    base, pull, heads, gain = call(
         temporal_kernel,
-        on_chip((samples, queries, channels), F32),
+        (
+            on_chip((samples, queries, channels), F32),
+            on_chip((samples, queries, channels), F32),
+            on_chip((HEADS * queries, channels), BF16),
+            on_chip((1, channels), F32),
+        ),
         band_id[None],
         bev_query,
         point_weight,
         prev_bev,
         align,
-        specs=[smem()] + [vmem()] * 4,
+        out_grad,
+        norm_gain[None],
+        specs=[smem()] + [vmem()] * 6,
         cost=cost,
     )
     first = owner_id * samples
@@ -305,8 +344,8 @@
     lane_of = lane_of.transpose(1, 0, 2).reshape(bands * samples * SEEN)
     count = lax.dynamic_slice_in_dim(jnp.sum(seen, axis=1), band_id, 1, axis=1)[:, 0]
     source = jnp.maximum(lane_of, 0)
-    got, base, turned, source, count, owner = lax.optimization_barrier(
-        (got, base, turned, source, count, owner[0])
+    got, base, pull, heads, gain, turned, source, count, owner = lax.optimization_barrier(
+        (got, base, pull, heads, gain, turned, source, count, owner[0])
     )
     piece = samples * SEEN * quarter
     chosen_kv = call(
@@ -328,9 +367,9 @@
         count,
         kv,
         base,
-        out_grad,
-        bev_query,
-        norm_gain[None],
+        pull,
+        heads,
+        gain,
         specs=[smem()] + [vmem()] * 5,
     )
     grads = lax.all_to_all(grads, "mp", split_axis=0, concat_axis=0, tiled=True)
@@ -345,7 +384,7 @@
     back = lax.all_to_all(back, "dp", split_axis=0, concat_axis=0, tiled=True)
     neck = call(
         neck_kernel,
-        on_chip((depth, channels), F32),
+        on_chip((depth, channels), BF16),
         owner,
         back,
         turned,
@@ -362,14 +401,12 @@
         )
 
     ys, zs, cs = range(chips), range(deep), range(CORES)
-    pairs = [[device(y, z, c) for c in cs] for y in ys for z in zs]
     planes = [
-        [device(y, z, c) * bands + x for y in ys for x in range(bands)] for z in zs for c in cs
+        [device(y, z, c) * bands + x for y in ys for c in cs for x in range(bands)] for z in zs
     ]
     columns = [[device(y, z, c) for z in zs] for y in ys for c in cs]
-    neck = exchange(neck.reshape(CORES, depth // CORES, channels), "dp", pairs)
-    neck = jnp.sum(neck, axis=0).reshape(chips * bands, share * deep, channels)
-    neck = exchange(neck, ("dp", "mp"), planes)
+    neck = neck.reshape(chips * CORES * bands, share * deep, channels)
+    neck = exchange(neck, ("dp", "mp"), planes).astype(F32)
     neck = jnp.sum(neck, axis=0).reshape(share, deep, channels).transpose(1, 0, 2)
     neck = exchange(neck, "dp", columns)
     return bev_out, jnp.sum(neck, axis=0) / cams.shape[0]

time: 192 us -> 185 us (0.964)
  local copies, waits for them, and re-layouts: 7 us -> 3.51 us
  blocking collectives: 99.3 us -> 96.3 us
    all_to_all x3 -> x2, blocking collectives: 34.4 us -> 31.3 us  [exchange(): lax.all_to_all(part, axis, split_axis=0, concat_axis=0, tiled=True, axis_...]
  transfers between devices with their start and end apart: 1 -> 1, of which waited for: 1 -> 1; matrix products, arithmetic and copies ran while one was open for 3% -> 2% of each run, Pallas kernels for 1% -> 1%
where the time goes in v3:
time: 185 us
  blocking collectives  96.3 us (52%)
  waiting for transfers between devices  44.3 us (24%)
  starting transfers between devices  20.7 us (11%)
  Pallas kernels  14.2 us (8%)
  local copies, waits for them, and re-layouts  3.51 us (2%)
  other arithmetic  2.82 us (2%)
  between operations  2.8 us (2%)
    all_to_all x1, blocking collectives, on_device(): back = lax.all_to_all(back, 'dp', split_axis=0, concat_axis=0, tiled=True)  45.6 us
    all_to_all x1, waiting for transfers between devices, on_device(): got = lax.all_to_all(lanes, 'dp', split_axis=0, concat_axis=0, tiled=True)  44.3 us
    all_to_all x2, blocking collectives, exchange(): lax.all_to_all(part, axis, split_axis=0, concat_axis=0, tiled=True, axis_...  31.3 us
    all_to_all x1, starting transfers between devices, on_device(): got = lax.all_to_all(lanes, 'dp', split_axis=0, concat_axis=0, tiled=True)  20.7 us
    pallas_call x7, Pallas kernels, call(): pl.pallas_call(body, out_shape=outs, in_specs=specs, out_specs=jax.tree.m...  14.2 us
    all_to_all x1, blocking collectives, on_device(): lax.all_to_all(chosen_kv.reshape(bands, piece, 2 * channels), 'mp', split...  11.4 us
    all_to_all x1, blocking collectives, on_device(): grads = lax.all_to_all(grads, 'mp', split_axis=0, concat_axis=0, tiled=True)  8.05 us
  transfers between devices with their start and end apart: 1, of which 1 were waited for; matrix products, arithmetic and copies ran while one was open for 2% of the time, Pallas kernels for 1%

profile of v3, /device:TPU:1, one launch (start us, length us, event | category | flops | bytes accessed | tf_op | source)
XLA Modules:
  0.0 184.6 jit_solution(12897748077337766843)
XLA Ops:
  0.6 2.8 %shard_map.131 = (bf16[128,8,512]{2,1,0:T(8,128)(2,1)}, s32[8,48]{1,0:T(8,128)S(1)}) custom-call(s32[1]{0:T(128)} %bitcast.bin_ref, s32[6,128]{1,0:T(8,128)} %bitcast.26, s32[1,6144]{1,0:T(1,128)} %bitcast.25, bf16[384,1024]{1,0:T(8,128)(2,1)} %bitcast.20, bf16[384,256]{1,0:T(8,128)(2,1)} %bitcast.23, bf16[1024,256]{1,0:T(8,128)(2,1)} %weight_hbm.1), custom_call_target="tpu_custom_call" | custom-call | flops 1048576 | bytes 1048576 | tf_op jit(solution)/shard_map/pallas_call | solution.py:49
  3.4 0.0 copy-start
  3.5 20.7 %all-to-all-start = ((bf16[128,8,512]{2,1,0:T(8,128)(2,1)}), bf16[128,8,512]{2,1,0:T(8,128)(2,1)S(1)}, u32[]{:S(2)}, u32[]{:S(2)}) async-start(bf16[128,8,512]{2,1,0:T(8,128)(2,1)} %get-tuple-element.19), calls=%async_computation | async-start | bytes 2097152 | tf_op jit(solution)/shard_map/all_to_all | solution.py:293
  24.2 0.0 copy-start.10
  24.2 0.0 copy-start.9
  24.2 0.7 copy-done.10
  24.9 0.6 select_reduce_fusion.2
  26.8 0.1 dynamic_slice.9
  26.9 0.0 copy-done.9
  26.9 0.0 copy-start.8
  26.9 0.1 copy.28
  27.7 0.1 fusion.2
  27.8 0.1 select_reduce_fusion.3
  27.9 0.1 multiply_reduce_fusion
  28.1 0.1 add_add_fusion
  28.1 0.4 select_reduce_fusion.1
  28.5 0.5 select_reduce_fusion
  29.0 0.0 copy-start.11
  29.0 0.1 copy.29
  29.2 0.1 max.15.source_ref
  29.3 0.5 copy-done.11
  29.7 0.1 copy.27.point_ref
  29.9 0.2 fusion.3
  30.0 0.2 dynamic-slice_reduce_fusion.count_ref
  30.2 0.0 copy-start.3
  30.2 0.0 copy-start.4
  30.3 0.0 copy-start.5
  30.3 0.0 copy-start.6
  30.3 0.8 shard_map.133.turned_ref
  31.1 0.0 copy-start.7
  31.1 0.2 copy-done.3
  31.2 0.1 copy-done.4
  31.4 0.0 copy-done.6
  31.4 0.4 copy-done.7
  31.8 1.5 shard_map.132
  33.4 0.8 copy-done.1
  34.2 44.3 %all-to-all-done.lane_ref = bf16[128,8,512]{2,1,0:T(8,128)(2,1)S(1)} async-done(((bf16[128,8,512]{2,1,0:T(8,128)(2,1)}), bf16[128,8,512]{2,1,0:T(8,128)(2,1)S(1)}, u32[]{:S(2)}, u32[]{:S(2)}) %all-to-all-start) | async-done | bytes 1048608 | tf_op jit(solution)/shard_map/all_to_all | solution.py:293
  78.5 0.6 shard_map.134
  79.1 11.4 %all_to_all.30.kv_ref = bf16[4,144,512]{2,1,0:T(8,128)(2,1)S(1)} all-to-all(bf16[4,144,512]{2,1,0:T(8,128)(2,1)S(1)} %bitcast.17), channel_id=1, replica_groups=mesh['dp'=128,'mp'=4] {'mp'}, dimensions={0} | all-to-all | bytes 1179648 | tf_op jit(solution)/shard_map/all_to_all | solution.py:358
  90.5 6.5 %shard_map.135 = (bf16[6,128,256]{2,1,0:T(8,128)(2,1)}, bf16[4,144,256]{2,1,0:T(8,128)(2,1)S(1)}) custom-call(s32[6]{0:T(128)S(1)} %dynamic-slice_reduce_fusion.count_ref, bf16[4,144,512]{2,1,0:T(8,128)(2,1)S(1)} %all_to_all.30.kv_ref, f32[6,128,256]{2,1,0:T(8,128)S(1)} %get-tuple-element.28.base_ref, f32[6,128,256]{2,1,0:T(8,128)S(1)} %get-tuple-element.29.pull_ref, ...), custom_call_target="tpu_custom_call" | custom-call | flops 1048576 | bytes 1048576 | tf_op jit(solution)/shard_map/pallas_call | solution.py:49
  97.0 8.1 %all_to_all.31 = bf16[4,144,256]{2,1,0:T(8,128)(2,1)S(1)} all-to-all(bf16[4,144,256]{2,1,0:T(8,128)(2,1)S(1)} %get-tuple-element.34), channel_id=1, replica_groups=mesh['dp'=128,'mp'=4] {'mp'}, dimensions={0} | all-to-all | bytes 589824 | tf_op jit(solution)/shard_map/all_to_all | solution.py:375
  105.1 1.0 shard_map.136
  106.1 45.6 %all_to_all.32.lane_ref = bf16[128,8,256]{2,1,0:T(8,128)(2,1)S(1)} all-to-all(bf16[128,8,256]{2,1,0:T(8,128)(2,1)S(1)} %shard_map.136), channel_id=1, replica_groups=mesh['dp'=128,'mp'=4] {'dp'}, dimensions={0} | all-to-all | bytes 1048576 | tf_op jit(solution)/shard_map/all_to_all | solution.py:384
  151.6 1.0 shard_map.137
  152.6 17.2 %all_to_all.33 = bf16[32,32,256]{2,1,0:T(8,128)(2,1)S(1)} all-to-all(bf16[32,32,256]{2,1,0:T(8,128)(2,1)S(1)} %bitcast.18), channel_id=1, replica_groups={{0,1,2,3,4,5,6,7,128,129,130,131,132,133,134,135,256,257,258,259,260,26..., dimensions={0} | all-to-all | bytes 1048576 | tf_op jit(solution)/shard_map/all_to_all | solution.py:399
  169.8 0.1 convert_reduce_fusion
  169.9 14.1 %all_to_all.34 = f32[16,2,256]{2,1,0:T(2,128)S(1)} all-to-all(f32[16,2,256]{2,1,0:T(2,128)S(1)} %copy.30), channel_id=1, replica_groups={{0,8,16,24,32,40,48,56,64,72,80,88,96,104,112,120},{4,12,20,28,36,44,52..., dimensions={0} | all-to-all | bytes 65536 | tf_op jit(solution)/shard_map/all_to_all | solution.py:399
  184.1 0.6 broadcast_multiply_fusion
  (13 shorter events, 0.1 us)
Async XLA Ops:
  3.4 26.8 %copy-start = (bf16[48,8,1024]{2,1,0:T(8,128)(2,1)S(1)}, bf16[48,8,1024]{2,1,0:T(8,128)(2,1)}, u32[]{:S(2)}) copy-start(bf16[48,8,1024]{2,1,0:T(8,128)(2,1)} %param.16) | copy-start | bytes 2359300
  3.5 75.1 %all-to-all-start = ((bf16[128,8,512]{2,1,0:T(8,128)(2,1)}), bf16[128,8,512]{2,1,0:T(8,128)(2,1)S(1)}, u32[]{:S(2)}, u32[]{:S(2)}) async-start(bf16[128,8,512]{2,1,0:T(8,128)(2,1)} %get-tuple-element.19), calls=%async_computation | async-start | bytes 2097152 | tf_op jit(solution)/shard_map/all_to_all | solution.py:293
  24.2 0.7 copy-start.10
  24.2 2.7 %copy-start.9 = (s32[6,11,4]{1,2,0:T(4,128)S(1)}, s32[6,11,4]{1,2,0:T(4,128)}, u32[]{:S(2)}) copy-start(s32[6,11,4]{1,2,0:T(4,128)} %param.14) | copy-start | bytes 3172
  26.9 0.8 copy-start.8
  29.0 0.7 copy-start.11
  30.2 1.0 copy-start.3
  30.2 1.1 copy-start.4
  30.3 1.1 copy-start.5
  30.3 1.1 copy-start.6
  31.1 0.7 copy-start.7
  33.4 0.8 copy-start.1
  79.1 11.4 %copy-start.2 = (bf16[1024,256]{1,0:T(8,128)(2,1)S(1)}, bf16[1024,256]{1,0:T(8,128)(2,1)}, u32[]{:S(2)}) copy-start(bf16[1024,256]{1,0:T(8,128)(2,1)} %copy-done.1) | copy-start | bytes 1572868

commit v4 on v3

--- a/solution.py
+++ b/solution.py
@@ -15,6 +15,7 @@
 
 NORM_EPS = 1e-05
 MASKED = -1e30
+LOG2_E = 1.4426950408889634
 BF16 = jnp.bfloat16
 F32 = jnp.float32
 I32 = jnp.int32
@@ -186,7 +187,20 @@
         out_ref[e] = lane_ref[source_ref[e]]
 
 
-def attention_kernel(count_ref, kv_ref, base_ref, pull_ref, heads_ref, gain_ref, out_ref, grad_ref):
+def attention_kernel(
+    count_ref,
+    kv_ref,
+    base_ref,
+    pull_ref,
+    heads_ref,
+    gain_ref,
+    out_ref,
+    grad_ref,
+    score_ref,
+    prob_ref,
+    norm_ref,
+    cross_ref,
+):
     parts, rows, width = kv_ref.shape
     samples, queries, channels = base_ref.shape
     step = rows // samples
@@ -196,29 +210,37 @@
     gain = gain_ref[...]
     lane_head = iota((1, channels), 1) // head_dim
     masks = [(lane_head == h).astype(F32).astype(BF16) for h in range(HEADS)]
+    factor = float(head_dim) ** -0.5 * LOG2_E
     place = iota((keys, HEADS * queries), 0) % step // quarter
+    spans = [slice(m * step, (m + 1) * step) for m in range(samples)]
+    ray = kv_ref[:, :, channels:].reshape(parts * rows, channels)
+    score_ref[...] = dot(ray, heads_ref[...], 1, 1).reshape(score_ref.shape)
     for m in range(samples):
-        here = slice(m * step, (m + 1) * step)
-        values = kv_ref[:, here, :channels].reshape(keys, channels)
-        ray = kv_ref[:, here, channels:].reshape(keys, channels)
+        scores = score_ref[:, spans[m], :].reshape(keys, HEADS * queries)
+        scores = jnp.where(place < count_ref[m], scores, MASKED)
+        raised = jnp.exp2((scores - jnp.max(scores, axis=0, keepdims=True)) * factor)
+        prob_ref[m] = (raised * (1.0 / jnp.sum(raised, axis=0, keepdims=True))).astype(BF16)
+    for m in range(samples):
+        values = kv_ref[:, spans[m], :channels].reshape(keys, channels)
         values = jnp.concatenate([values * mask for mask in masks], axis=0)
-        scores = dot(ray, heads_ref[...], 1, 1) * (float(head_dim) ** -0.5)
-        scores = jnp.where(place < count_ref[m], scores, MASKED)
-        raised = jnp.exp(scores - jnp.max(scores, axis=0, keepdims=True))
-        probs = (raised * (1.0 / jnp.sum(raised, axis=0, keepdims=True))).astype(BF16)
+        probs = prob_ref[m]
         tall = jnp.concatenate(
             [probs[:, h * queries : (h + 1) * queries] for h in range(HEADS)], axis=0
         )
-        pre_norm = base_ref[m] + dot(tall, values, 0, 0)
+        norm_ref[m] = base_ref[m] + dot(tall, values, 0, 0)
+    for m in range(samples):
+        pre_norm = norm_ref[m]
         centred = pre_norm - jnp.mean(pre_norm, axis=1, keepdims=True)
         scale = lax.rsqrt(jnp.mean(centred * centred, axis=1, keepdims=True) + NORM_EPS)
         unit = centred * scale
         out_ref[m] = (unit * gain).astype(BF16)
         pull = pull_ref[m]
         pull = pull - unit * jnp.mean(pull * unit, axis=1, keepdims=True)
-        pull = (pull * scale).astype(BF16)
+        cross_ref[m] = (pull * scale).astype(BF16)
+    for m in range(samples):
+        pull = cross_ref[m]
         pull = jnp.concatenate([pull * mask for mask in masks], axis=0)
-        grad_ref[:, here, :] = dot(probs, pull).astype(BF16).reshape(parts, step, channels)
+        grad_ref[:, spans[m], :] = dot(prob_ref[m], pull).astype(BF16).reshape(parts, step, channels)
 
 
 def return_kernel(source_ref, grad_ref, lane_ref, sum_ref):
@@ -229,11 +251,11 @@
     lane_ref[...] = sum_ref[...].astype(BF16)
 
 
-def neck_kernel(owner_ref, lane_ref, turned_ref, out_ref, grad_ref):
+def neck_kernel(owner_ref, lane_ref, turned_ref, out_ref, grad_ref, *, samples):
     quarter = lane_ref.shape[1]
     for s in range(grad_ref.shape[0] // quarter):
         grad_ref[s * quarter : (s + 1) * quarter, :] = lane_ref[owner_ref[s]]
-    out_ref[...] = dot(turned_ref[...], grad_ref[...]).astype(BF16)
+    out_ref[...] = (dot(turned_ref[...], grad_ref[...]) * (1.0 / samples)).astype(BF16)
 
 
 def on_device(
@@ -371,6 +393,12 @@
         heads,
         gain,
         specs=[smem()] + [vmem()] * 5,
+        scratch=[
+            pltpu.VMEM((bands, piece, HEADS * queries), F32),
+            pltpu.VMEM((samples, bands * SEEN * quarter, HEADS * queries), BF16),
+            pltpu.VMEM((samples, queries, channels), F32),
+            pltpu.VMEM((samples, queries, channels), BF16),
+        ],
     )
     grads = lax.all_to_all(grads, "mp", split_axis=0, concat_axis=0, tiled=True)
     back = call(
@@ -383,7 +411,7 @@
     )
     back = lax.all_to_all(back, "dp", split_axis=0, concat_axis=0, tiled=True)
     neck = call(
-        neck_kernel,
+        functools.partial(neck_kernel, samples=cams.shape[0]),
         on_chip((depth, channels), BF16),
         owner,
         back,
@@ -409,7 +437,7 @@
     neck = exchange(neck, ("dp", "mp"), planes).astype(F32)
     neck = jnp.sum(neck, axis=0).reshape(share, deep, channels).transpose(1, 0, 2)
     neck = exchange(neck, "dp", columns)
-    return bev_out, jnp.sum(neck, axis=0) / cams.shape[0]
+    return bev_out, jnp.sum(neck, axis=0)
 
 
 def solution(mesh):

time: 185 us -> 182 us (0.984)
  Pallas kernels: 14.2 us -> 10.9 us
    pallas_call x7, Pallas kernels: 14.2 us -> 10.9 us  [call(): pl.pallas_call(body, out_shape=outs, in_specs=specs, out_specs=jax.tree.m...]
where the time goes in v4:
time: 182 us; the launch traced here: 181 us
  blocking collectives  96.3 us (53%)
  waiting for transfers between devices  44.3 us (24%)
  starting transfers between devices  20.7 us (11%)
  Pallas kernels  10.9 us (6%)
  local copies, waits for them, and re-layouts  3.51 us (2%)
  other arithmetic  2.81 us (2%)
  between operations  2.8 us (2%)
    all_to_all x1, blocking collectives, on_device(): back = lax.all_to_all(back, 'dp', split_axis=0, concat_axis=0, tiled=True)  45.5 us
    all_to_all x1, waiting for transfers between devices, on_device(): got = lax.all_to_all(lanes, 'dp', split_axis=0, concat_axis=0, tiled=True)  44.3 us
    all_to_all x2, blocking collectives, exchange(): lax.all_to_all(part, axis, split_axis=0, concat_axis=0, tiled=True, axis_...  31.3 us
    all_to_all x1, starting transfers between devices, on_device(): got = lax.all_to_all(lanes, 'dp', split_axis=0, concat_axis=0, tiled=True)  20.7 us
    all_to_all x1, blocking collectives, on_device(): lax.all_to_all(chosen_kv.reshape(bands, piece, 2 * channels), 'mp', split...  11.4 us
    pallas_call x7, Pallas kernels, call(): pl.pallas_call(body, out_shape=outs, in_specs=specs, out_specs=jax.tree.m...  10.9 us
    all_to_all x1, blocking collectives, on_device(): grads = lax.all_to_all(grads, 'mp', split_axis=0, concat_axis=0, tiled=True)  8.05 us
  transfers between devices with their start and end apart: 1, of which 1 were waited for; matrix products, arithmetic and copies ran while one was open for 2% of the time, Pallas kernels for 1%

profile of v4, /device:TPU:1, one launch (start us, length us, event | category | flops | bytes accessed | tf_op | source)
XLA Modules:
  0.0 181.4 jit_solution(1702956834544312156)
XLA Ops:
  0.6 2.8 %shard_map.131 = (bf16[128,8,512]{2,1,0:T(8,128)(2,1)}, s32[8,48]{1,0:T(8,128)S(1)}) custom-call(s32[1]{0:T(128)} %bitcast.bin_ref, s32[6,128]{1,0:T(8,128)} %bitcast.26, s32[1,6144]{1,0:T(1,128)} %bitcast.25, bf16[384,1024]{1,0:T(8,128)(2,1)} %bitcast.20, bf16[384,256]{1,0:T(8,128)(2,1)} %bitcast.23, bf16[1024,256]{1,0:T(8,128)(2,1)} %weight_hbm.1), custom_call_target="tpu_custom_call" | custom-call | flops 1048576 | bytes 1048576 | tf_op jit(solution)/shard_map/pallas_call | solution.py:50
  3.4 0.0 copy-start
  3.5 20.7 %all-to-all-start = ((bf16[128,8,512]{2,1,0:T(8,128)(2,1)}), bf16[128,8,512]{2,1,0:T(8,128)(2,1)S(1)}, u32[]{:S(2)}, u32[]{:S(2)}) async-start(bf16[128,8,512]{2,1,0:T(8,128)(2,1)} %get-tuple-element.19), calls=%async_computation | async-start | bytes 2097152 | tf_op jit(solution)/shard_map/all_to_all | solution.py:315
  24.2 0.0 copy-start.10
  24.2 0.0 copy-start.9
  24.2 0.7 copy-done.10
  24.9 0.6 select_reduce_fusion.2
  26.8 0.1 dynamic_slice.9
  26.9 0.0 copy-done.9
  26.9 0.0 copy-start.8
  26.9 0.1 copy.28
  27.7 0.0 copy-done.8
  27.7 0.1 fusion.2
  27.8 0.1 select_reduce_fusion.3
  27.9 0.1 multiply_reduce_fusion
  28.1 0.1 add_add_fusion
  28.1 0.4 select_reduce_fusion.1
  28.5 0.5 select_reduce_fusion
  29.0 0.0 copy-start.11
  29.0 0.1 copy.29
  29.2 0.1 max.15.source_ref
  29.3 0.5 copy-done.11
  29.7 0.1 copy.27.point_ref
  29.9 0.2 fusion.3
  30.0 0.2 dynamic-slice_reduce_fusion.count_ref
  30.2 0.0 copy-start.3
  30.2 0.0 copy-start.4
  30.3 0.0 copy-start.5
  30.3 0.0 copy-start.6
  30.3 0.8 shard_map.133.turned_ref
  31.1 0.0 copy-start.7
  31.1 0.2 copy-done.3
  31.2 0.1 copy-done.4
  31.4 0.4 copy-done.7
  31.8 1.5 shard_map.132
  33.4 0.8 copy-done.1
  34.2 44.3 %all-to-all-done.lane_ref = bf16[128,8,512]{2,1,0:T(8,128)(2,1)S(1)} async-done(((bf16[128,8,512]{2,1,0:T(8,128)(2,1)}), bf16[128,8,512]{2,1,0:T(8,128)(2,1)S(1)}, u32[]{:S(2)}, u32[]{:S(2)}) %all-to-all-start) | async-done | bytes 1048608 | tf_op jit(solution)/shard_map/all_to_all | solution.py:315
  78.5 0.6 shard_map.134
  79.1 11.4 %all_to_all.30.kv_ref = bf16[4,144,512]{2,1,0:T(8,128)(2,1)S(1)} all-to-all(bf16[4,144,512]{2,1,0:T(8,128)(2,1)S(1)} %bitcast.17), channel_id=1, replica_groups=mesh['dp'=128,'mp'=4] {'mp'}, dimensions={0} | all-to-all | bytes 1179648 | tf_op jit(solution)/shard_map/all_to_all | solution.py:380
  90.5 3.2 %shard_map.135 = (bf16[6,128,256]{2,1,0:T(8,128)(2,1)}, bf16[4,144,256]{2,1,0:T(8,128)(2,1)S(1)}) custom-call(s32[6]{0:T(128)S(1)} %dynamic-slice_reduce_fusion.count_ref, bf16[4,144,512]{2,1,0:T(8,128)(2,1)S(1)} %all_to_all.30.kv_ref, f32[6,128,256]{2,1,0:T(8,128)S(1)} %get-tuple-element.28.base_ref, f32[6,128,256]{2,1,0:T(8,128)S(1)} %get-tuple-element.29.pull_ref, ...), custom_call_target="tpu_custom_call" | custom-call | flops 1048576 | bytes 1048576 | tf_op jit(solution)/shard_map/pallas_call | solution.py:50
  93.8 8.1 %all_to_all.31 = bf16[4,144,256]{2,1,0:T(8,128)(2,1)S(1)} all-to-all(bf16[4,144,256]{2,1,0:T(8,128)(2,1)S(1)} %get-tuple-element.34), channel_id=1, replica_groups=mesh['dp'=128,'mp'=4] {'mp'}, dimensions={0} | all-to-all | bytes 589824 | tf_op jit(solution)/shard_map/all_to_all | solution.py:403
  101.8 1.0 shard_map.136
  102.8 45.5 %all_to_all.32.lane_ref = bf16[128,8,256]{2,1,0:T(8,128)(2,1)S(1)} all-to-all(bf16[128,8,256]{2,1,0:T(8,128)(2,1)S(1)} %shard_map.136), channel_id=1, replica_groups=mesh['dp'=128,'mp'=4] {'dp'}, dimensions={0} | all-to-all | bytes 1048576 | tf_op jit(solution)/shard_map/all_to_all | solution.py:412
  148.3 1.0 shard_map.137
  149.3 17.2 %all_to_all.33 = bf16[32,32,256]{2,1,0:T(8,128)(2,1)S(1)} all-to-all(bf16[32,32,256]{2,1,0:T(8,128)(2,1)S(1)} %bitcast.18), channel_id=1, replica_groups={{0,1,2,3,4,5,6,7,128,129,130,131,132,133,134,135,256,257,258,259,260,26..., dimensions={0} | all-to-all | bytes 1048576 | tf_op jit(solution)/shard_map/all_to_all | solution.py:427
  166.5 0.1 convert_reduce_fusion
  166.7 14.1 %all_to_all.34 = f32[16,2,256]{2,1,0:T(2,128)S(1)} all-to-all(f32[16,2,256]{2,1,0:T(2,128)S(1)} %copy.30), channel_id=1, replica_groups={{0,8,16,24,32,40,48,56,64,72,80,88,96,104,112,120},{4,12,20,28,36,44,52..., dimensions={0} | all-to-all | bytes 65536 | tf_op jit(solution)/shard_map/all_to_all | solution.py:427
  180.7 0.6 reduce_sum.79
  (12 shorter events, 0.1 us)
Async XLA Ops:
  3.4 26.8 %copy-start = (bf16[48,8,1024]{2,1,0:T(8,128)(2,1)S(1)}, bf16[48,8,1024]{2,1,0:T(8,128)(2,1)}, u32[]{:S(2)}) copy-start(bf16[48,8,1024]{2,1,0:T(8,128)(2,1)} %param.16) | copy-start | bytes 2359300
  3.5 75.1 %all-to-all-start = ((bf16[128,8,512]{2,1,0:T(8,128)(2,1)}), bf16[128,8,512]{2,1,0:T(8,128)(2,1)S(1)}, u32[]{:S(2)}, u32[]{:S(2)}) async-start(bf16[128,8,512]{2,1,0:T(8,128)(2,1)} %get-tuple-element.19), calls=%async_computation | async-start | bytes 2097152 | tf_op jit(solution)/shard_map/all_to_all | solution.py:315
  24.2 0.7 copy-start.10
  24.2 2.7 %copy-start.9 = (s32[6,11,4]{1,2,0:T(4,128)S(1)}, s32[6,11,4]{1,2,0:T(4,128)}, u32[]{:S(2)}) copy-start(s32[6,11,4]{1,2,0:T(4,128)} %param.14) | copy-start | bytes 3172
  26.9 0.8 copy-start.8
  29.0 0.7 copy-start.11
  30.2 1.0 copy-start.3
  30.2 1.1 copy-start.4
  30.3 1.1 copy-start.5
  30.3 1.1 copy-start.6
  31.1 0.7 copy-start.7
  33.3 0.8 copy-start.1
  79.1 11.4 %copy-start.2 = (bf16[1024,256]{1,0:T(8,128)(2,1)S(1)}, bf16[1024,256]{1,0:T(8,128)(2,1)}, u32[]{:S(2)}) copy-start(bf16[1024,256]{1,0:T(8,128)(2,1)} %copy-done.1) | copy-start | bytes 1572868

commit v5 on v4

--- a/solution.py
+++ b/solution.py
@@ -126,21 +126,34 @@
         lane_ref[index_ref[0, s], :, channels:] = key_ref[here, :]
 
 
-def turn_kernel(image_ref, out_ref, turned_ref, *, chips, depth, bands, share):
-    turned = image_ref[...].astype(F32).T
-    width = turned_ref.shape[2]
-    for g in range(turned_ref.shape[0]):
-        turned_ref[g] = turned[:, g * width : (g + 1) * width]
+def deal_kernel(lane_ref, image_ref, out_ref):
+    quarter = out_ref.shape[1]
+    out_ref[...] = jnp.zeros(out_ref.shape, BF16)
+    for s in range(image_ref.shape[0] // quarter):
+        out_ref[lane_ref[s]] = image_ref[s * quarter : (s + 1) * quarter, :]
+
+
+def turn_kernel(*refs, bands, share):
+    out_ref, block_ref, turned_ref = refs[-3:]
+    pieces = refs[:-3]
+    deep, quarter, _ = pieces[0].shape
+    for z in range(deep):
+        for p, piece in enumerate(pieces):
+            at = (z * len(pieces) + p) * quarter
+            block_ref[at : at + quarter, :] = piece[z]
+    groups, _, width = turned_ref.shape
+    for g in range(groups):
+        turned_ref[g] = block_ref[g * width : (g + 1) * width, :].astype(F32).T
     step = CORES * bands * share
     at = 0
-    for y in range(chips):
+    for y in range(len(pieces) // CORES):
         for c in range(CORES):
             for j in range(bands * share):
-                first = y * depth * step + c * bands * share + j
-                for g in range(turned_ref.shape[0]):
-                    part = turned_ref.at[g][pl.ds(first, depth, stride=step), :]
-                    out_ref[at : at + depth, g * width : (g + 1) * width] = part.astype(BF16)
-                at += depth
+                first = y * deep * step + c * bands * share + j
+                for g in range(groups):
+                    part = turned_ref.at[g][pl.ds(first, deep, stride=step), :]
+                    out_ref[at : at + deep, g * width : (g + 1) * width] = part.astype(BF16)
+                at += deep
 
 
 def temporal_kernel(
@@ -251,10 +264,7 @@
     lane_ref[...] = sum_ref[...].astype(BF16)
 
 
-def neck_kernel(owner_ref, lane_ref, turned_ref, out_ref, grad_ref, *, samples):
-    quarter = lane_ref.shape[1]
-    for s in range(grad_ref.shape[0] // quarter):
-        grad_ref[s * quarter : (s + 1) * quarter, :] = lane_ref[owner_ref[s]]
+def neck_kernel(grad_ref, turned_ref, out_ref, *, samples):
     out_ref[...] = (dot(turned_ref[...], grad_ref[...]) * (1.0 / samples)).astype(BF16)
 
 
@@ -317,13 +327,45 @@
     chips = Y_CHIPS
     deep = owners // (CORES * chips)
     share = depth // (owners * bands)
-    lanes_wide = min(128, rows)
+
+    def device(y, z, c):
+        return (y * deep + z) * CORES + c
+
+    def place_of(device_id):
+        return device_id // (deep * CORES), device_id // CORES % deep, device_id % CORES
+
+    ys, zs, cs = range(chips), range(deep), range(CORES)
+    my_y, _, my_core = place_of(owner_id)
+    owner_y, owner_z, owner_core = place_of(owner[0])
+    column = (owner_y - my_y) % chips * CORES + (owner_core + my_core) % CORES
+    dealt = call(
+        deal_kernel,
+        jax.ShapeDtypeStruct((owners, quarter, depth), BF16),
+        column * deep + owner_z,
+        flat_images,
+        specs=[smem(), vmem()],
+        cost=cost,
+    ).reshape(chips * CORES, deep, quarter, depth)
+    pieces = [dealt[0]]
+    for p in range(1, chips * CORES):
+        moves = [
+            (device(y, z, c), device((y + p // CORES) % chips, z, (c + p) % CORES))
+            for y in ys
+            for z in zs
+            for c in cs
+        ]
+        pieces.append(lax.ppermute(dealt[p], "dp", moves))
+    tokens = owners * quarter
     turned = call(
-        functools.partial(turn_kernel, chips=chips, depth=deep, bands=bands, share=share),
-        on_chip((depth, rows), BF16),
-        flat_images,
-        scratch=[pltpu.VMEM((rows // lanes_wide, depth, lanes_wide), F32)],
+        functools.partial(turn_kernel, bands=bands, share=share),
+        on_chip((depth, tokens), BF16),
+        *pieces,
+        scratch=[
+            pltpu.VMEM((tokens, depth), BF16),
+            pltpu.VMEM((tokens // 128, depth, 128), F32),
+        ],
         cost=cost,
+        pinned=False,
     )
     base, pull, heads, gain = call(
         temporal_kernel,
@@ -366,8 +408,10 @@
     lane_of = lane_of.transpose(1, 0, 2).reshape(bands * samples * SEEN)
     count = lax.dynamic_slice_in_dim(jnp.sum(seen, axis=1), band_id, 1, axis=1)[:, 0]
     source = jnp.maximum(lane_of, 0)
-    got, base, pull, heads, gain, turned, source, count, owner = lax.optimization_barrier(
-        (got, base, pull, heads, gain, turned, source, count, owner[0])
+    bin_y, bin_z, bin_core = place_of(source)
+    back_lane = (bin_z * chips + (my_y - bin_y) % chips) * CORES + (bin_core + my_core) % CORES
+    got, base, pull, heads, gain, turned, source, back_lane, count = lax.optimization_barrier(
+        (got, base, pull, heads, gain, turned, source, back_lane, count)
     )
     piece = samples * SEEN * quarter
     chosen_kv = call(
@@ -404,35 +448,28 @@
     back = call(
         return_kernel,
         on_chip((owners, quarter, channels), BF16),
-        source,
+        back_lane,
         grads.reshape(bands * samples * SEEN, quarter, channels),
         specs=[smem(), vmem()],
         scratch=[pltpu.VMEM((owners, quarter, channels), F32)],
     )
-    back = lax.all_to_all(back, "dp", split_axis=0, concat_axis=0, tiled=True)
-    neck = call(
-        functools.partial(neck_kernel, samples=cams.shape[0]),
-        on_chip((depth, channels), BF16),
-        owner,
-        back,
-        turned,
-        specs=[smem(), vmem(), vmem()],
-        scratch=[pltpu.VMEM((rows, channels), BF16)],
-    )
-
-    def device(y, z, c):
-        return (y * deep + z) * CORES + c
 
     def exchange(part, axis, groups):
         return lax.all_to_all(
             part, axis, split_axis=0, concat_axis=0, tiled=True, axis_index_groups=groups
         )
 
-    ys, zs, cs = range(chips), range(deep), range(CORES)
+    columns = [[device(y, z, c) for z in zs] for y in ys for c in cs]
+    back = exchange(back.reshape(deep, tokens // deep, channels), "dp", columns)
+    neck = call(
+        functools.partial(neck_kernel, samples=cams.shape[0]),
+        on_chip((depth, channels), BF16),
+        back.reshape(tokens, channels),
+        turned,
+    )
     planes = [
         [device(y, z, c) * bands + x for y in ys for c in cs for x in range(bands)] for z in zs
     ]
-    columns = [[device(y, z, c) for z in zs] for y in ys for c in cs]
     neck = neck.reshape(chips * CORES * bands, share * deep, channels)
     neck = exchange(neck, ("dp", "mp"), planes).astype(F32)
     neck = jnp.sum(neck, axis=0).reshape(share, deep, channels).transpose(1, 0, 2)

time: 182 us -> 184 us (1.011)
  waiting for transfers between devices: 44.3 us -> 7.52 us
  starting transfers between devices: 20.7 us -> 42.7 us
  local copies, waits for them, and re-layouts: 3.51 us -> 16.7 us
    all_to_all x2 -> x3, blocking collectives: 31.3 us -> 77.3 us  [exchange(): lax.all_to_all(part, axis, split_axis=0, concat_axis=0, tiled=True, axis_...]
    all_to_all x1 -> x0, blocking collectives: 45.5 us -> none  [on_device(): back = lax.all_to_all(back, 'dp', split_axis=0, concat_axis=0, tiled=True)]
    all_to_all x1, waiting for transfers between devices: 44.3 us -> 0.01 us  [on_device(): got = lax.all_to_all(lanes, 'dp', split_axis=0, concat_axis=0, tiled=True)]
    ppermute x0 -> x7, starting transfers between devices: none -> 22.1 us  [on_device(): pieces.append(lax.ppermute(dealt[p], 'dp', moves))]
    unnamed x25 -> x61, local copies, waits for them, and re-layouts: 2.85 us -> 14.9 us
    ppermute x0 -> x7, waiting for transfers between devices: none -> 7.52 us  [on_device(): pieces.append(lax.ppermute(dealt[p], 'dp', moves))]
    pallas_call x7 -> x8, Pallas kernels: 10.9 us -> 12.7 us  [call(): pl.pallas_call(body, out_shape=outs, in_specs=specs, out_specs=jax.tree.m...]
  transfers between devices with their start and end apart: 1 -> 8, of which waited for: 1 -> 2; matrix products, arithmetic and copies ran while one was open for 2% -> 2% of each run, Pallas kernels for 1% -> 2%
where the time goes in v5:
time: 184 us; the launch traced here: 183 us
  blocking collectives  97.3 us (53%)
  starting transfers between devices  42.7 us (23%)
  local copies, waits for them, and re-layouts  16.7 us (9%)
  Pallas kernels  12.7 us (7%)
  waiting for transfers between devices  7.52 us (4%)
  between operations  3.01 us (2%)
  other arithmetic  2.85 us (2%)
    all_to_all x3, blocking collectives, exchange(): lax.all_to_all(part, axis, split_axis=0, concat_axis=0, tiled=True, axis_...  77.3 us
    ppermute x7, starting transfers between devices, on_device(): pieces.append(lax.ppermute(dealt[p], 'dp', moves))  22.1 us
    all_to_all x1, starting transfers between devices, on_device(): got = lax.all_to_all(lanes, 'dp', split_axis=0, concat_axis=0, tiled=True)  20.6 us
    unnamed x61, local copies, waits for them, and re-layouts  14.9 us
    pallas_call x8, Pallas kernels, call(): pl.pallas_call(body, out_shape=outs, in_specs=specs, out_specs=jax.tree.m...  12.7 us
    all_to_all x1, blocking collectives, on_device(): lax.all_to_all(chosen_kv.reshape(bands, piece, 2 * channels), 'mp', split...  12 us
    all_to_all x1, blocking collectives, on_device(): grads = lax.all_to_all(grads, 'mp', split_axis=0, concat_axis=0, tiled=True)  8.05 us
    ppermute x7, waiting for transfers between devices, on_device(): pieces.append(lax.ppermute(dealt[p], 'dp', moves))  7.52 us
  transfers between devices with their start and end apart: 8, of which 2 were waited for; matrix products, arithmetic and copies ran while one was open for 2% of the time, Pallas kernels for 2%

profile of v5, /device:TPU:1, one launch (start us, length us, event | category | flops | bytes accessed | tf_op | source)
XLA Modules:
  0.0 182.8 jit_solution(13572508798155859564)
XLA Ops:
  0.6 2.9 %shard_map.131 = (bf16[128,8,512]{2,1,0:T(8,128)(2,1)}, s32[8,48]{1,0:T(8,128)S(1)}) custom-call(s32[1]{0:T(128)} %bitcast.bin_ref, s32[6,128]{1,0:T(8,128)} %bitcast.44, s32[1,6144]{1,0:T(1,128)} %bitcast.43, bf16[384,1024]{1,0:T(8,128)(2,1)} %bitcast.38, bf16[384,256]{1,0:T(8,128)(2,1)} %bitcast.41, bf16[1024,256]{1,0:T(8,128)(2,1)} %weight_hbm.1), custom_call_target="tpu_custom_call" | custom-call | flops 1048576 | bytes 1048576 | tf_op jit(solution)/shard_map/pallas_call | solution.py:50
  3.5 20.6 %all-to-all-start = ((bf16[128,8,512]{2,1,0:T(8,128)(2,1)}), bf16[128,8,512]{2,1,0:T(8,128)(2,1)S(1)}, u32[]{:S(2)}, u32[]{:S(2)}) async-start(bf16[128,8,512]{2,1,0:T(8,128)(2,1)} %get-tuple-element.19), calls=%async_computation | async-start | bytes 2097152 | tf_op jit(solution)/shard_map/all_to_all | solution.py:325
  24.2 0.7 shard_map.133
  25.0 1.1 fusion.18
  26.0 2.8 %collective-permute-start = (bf16[16,8,1024]{2,1,0:T(8,128)(2,1)S(1)}, bf16[16,8,1024]{2,1,0:T(8,128)(2,1)S(1)}, u32[]{:S(2)}, u32[]{:S(2)}) collective-permute-start(bf16[16,8,1024]{2,1,0:T(8,128)(2,1)S(1)} %get-tuple-element.42), channel_id=1, source_target_pairs={{0,4},{4,0},{8,12},{12,8},{16,20},{20,16},{24,28},{28,24},{32,36},... | collective-permute-start | bytes 786440 | tf_op jit(solution)/shard_map/ppermute | solution.py:357
  28.8 2.9 %collective-permute-start.1 = (bf16[16,8,1024]{2,1,0:T(8,128)(2,1)S(1)}, bf16[16,8,1024]{2,1,0:T(8,128)(2,1)S(1)}, u32[]{:S(2)}, u32[]{:S(2)}) collective-permute-start(bf16[16,8,1024]{2,1,0:T(8,128)(2,1)S(1)} %get-tuple-element.41), channel_id=1, source_target_pairs={{0,128},{4,132},{8,136},{12,140},{16,144},{20,148},{24,152},{28,15... | collective-permute-start | bytes 786440 | tf_op jit(solution)/shard_map/ppermute | solution.py:357
  31.7 3.6 %collective-permute-start.2 = (bf16[16,8,1024]{2,1,0:T(8,128)(2,1)}, bf16[16,8,1024]{2,1,0:T(8,128)(2,1)S(1)}, u32[]{:S(2)}, u32[]{:S(2)}) collective-permute-start(bf16[16,8,1024]{2,1,0:T(8,128)(2,1)} %get-tuple-element.40), channel_id=1, source_target_pairs={{0,132},{4,128},{8,140},{12,136},{16,148},{20,144},{24,156},{28,15... | collective-permute-start | bytes 786440 | tf_op jit(solution)/shard_map/ppermute | solution.py:357
  35.4 3.3 %collective-permute-start.3 = (bf16[16,8,1024]{2,1,0:T(8,128)(2,1)}, bf16[16,8,1024]{2,1,0:T(8,128)(2,1)S(1)}, u32[]{:S(2)}, u32[]{:S(2)}) collective-permute-start(bf16[16,8,1024]{2,1,0:T(8,128)(2,1)} %get-tuple-element.39), channel_id=1, source_target_pairs={{0,256},{4,260},{8,264},{12,268},{16,272},{20,276},{24,280},{28,28... | collective-permute-start | bytes 786440 | tf_op jit(solution)/shard_map/ppermute | solution.py:357
  38.6 3.8 %collective-permute-start.4 = (bf16[16,8,1024]{2,1,0:T(8,128)(2,1)}, bf16[16,8,1024]{2,1,0:T(8,128)(2,1)S(1)}, u32[]{:S(2)}, u32[]{:S(2)}) collective-permute-start(bf16[16,8,1024]{2,1,0:T(8,128)(2,1)} %get-tuple-element.38), channel_id=1, source_target_pairs={{0,260},{4,256},{8,268},{12,264},{16,276},{20,272},{24,284},{28,28... | collective-permute-start | bytes 786440 | tf_op jit(solution)/shard_map/ppermute | solution.py:357
  42.4 0.6 select_reduce_fusion.2
  45.4 0.1 multiply_reduce_fusion
  45.7 0.4 select_reduce_fusion.1
  46.1 0.5 select_reduce_fusion
  46.5 0.2 fusion.17
  46.9 3.2 %collective-permute-start.5 = (bf16[16,8,1024]{2,1,0:T(8,128)(2,1)}, bf16[16,8,1024]{2,1,0:T(8,128)(2,1)S(1)}, u32[]{:S(2)}, u32[]{:S(2)}) collective-permute-start(bf16[16,8,1024]{2,1,0:T(8,128)(2,1)} %get-tuple-element.37), channel_id=1, source_target_pairs={{0,384},{4,388},{8,392},{12,396},{16,400},{20,404},{24,408},{28,41... | collective-permute-start | bytes 786440 | tf_op jit(solution)/shard_map/ppermute | solution.py:357
  50.1 2.6 %collective-permute-start.6 = (bf16[16,8,1024]{2,1,0:T(8,128)(2,1)}, bf16[16,8,1024]{2,1,0:T(8,128)(2,1)S(1)}, u32[]{:S(2)}, u32[]{:S(2)}) collective-permute-start(bf16[16,8,1024]{2,1,0:T(8,128)(2,1)} %get-tuple-element.36), channel_id=1, source_target_pairs={{0,388},{4,384},{8,396},{12,392},{16,404},{20,400},{24,412},{28,40... | collective-permute-start | bytes 786440 | tf_op jit(solution)/shard_map/ppermute | solution.py:357
  52.7 1.0 copy-done.21
  53.7 1.0 copy-done.22
  54.7 1.5 shard_map.132
  56.3 0.9 copy-done.1
  57.2 0.9 copy-done.3
  58.1 0.8 copy-done.5
  59.1 0.2 dynamic-slice_reduce_fusion.count_ref
  59.4 0.7 copy-done.11
  60.1 0.7 copy-done.13
  60.8 4.8 %collective-permute-done.4.refs_5_ = bf16[16,8,1024]{2,1,0:T(8,128)(2,1)S(1)} collective-permute-done((bf16[16,8,1024]{2,1,0:T(8,128)(2,1)}, bf16[16,8,1024]{2,1,0:T(8,128)(2,1)S(1)}, u32[]{:S(2)}, u32[]{:S(2)}) %collective-permute-start.4) | collective-permute-done | bytes 262176 | tf_op jit(solution)/shard_map/ppermute | solution.py:357
  65.6 0.7 copy-done.15
  66.3 0.7 copy-done.17
  67.0 2.7 %collective-permute-done.6.refs_7_ = bf16[16,8,1024]{2,1,0:T(8,128)(2,1)S(1)} collective-permute-done((bf16[16,8,1024]{2,1,0:T(8,128)(2,1)}, bf16[16,8,1024]{2,1,0:T(8,128)(2,1)S(1)}, u32[]{:S(2)}, u32[]{:S(2)}) %collective-permute-start.6) | collective-permute-done | bytes 262176 | tf_op jit(solution)/shard_map/ppermute | solution.py:357
  69.7 0.7 copy-done.19
  70.4 0.9 copy-done.8
  71.3 0.9 copy-done.10
  72.3 0.9 copy-done.12
  73.2 0.9 copy-done.14
  74.2 0.9 copy-done.16
  75.1 0.9 copy-done.18
  76.1 0.9 copy-done.20
  77.0 2.0 %shard_map.134.turned_ref = bf16[1024,1024]{1,0:T(8,128)(2,1)S(1)} custom-call(bf16[16,8,1024]{2,1,0:T(8,128)(2,1)S(1)} %get-tuple-element.43.refs_0_, bf16[16,8,1024]{2,1,0:T(8,128)(2,1)S(1)} %copy-done.8, bf16[16,8,1024]{2,1,0:T(8,128)(2,1)S(1)} %copy-done.10, bf16[16,8,1024]{2,1,0:T(8,128)(2,1)S(1)} %copy-done.12, bf16[16,8,1024]{2,1,0:T(8,128)(2,1)S(1)} %copy-done.14, ...), custom_call_target="tpu_custom_call" | custom-call | flops 1073741824 | bytes 4194304 | tf_op jit(solution)/shard_map/pallas_call | solution.py:50
  79.1 0.6 shard_map.135
  79.7 12.0 %all_to_all.30.kv_ref = bf16[4,144,512]{2,1,0:T(8,128)(2,1)S(1)} all-to-all(bf16[4,144,512]{2,1,0:T(8,128)(2,1)S(1)} %bitcast.33), channel_id=1, replica_groups=mesh['dp'=128,'mp'=4] {'mp'}, dimensions={0} | all-to-all | bytes 1179648 | tf_op jit(solution)/shard_map/all_to_all | solution.py:424
  91.7 3.3 %shard_map.136 = (bf16[6,128,256]{2,1,0:T(8,128)(2,1)}, bf16[4,144,256]{2,1,0:T(8,128)(2,1)S(1)}) custom-call(s32[6]{0:T(128)S(1)} %dynamic-slice_reduce_fusion.count_ref, bf16[4,144,512]{2,1,0:T(8,128)(2,1)S(1)} %all_to_all.30.kv_ref, f32[6,128,256]{2,1,0:T(8,128)S(1)} %copy-done.2, f32[6,128,256]{2,1,0:T(8,128)S(1)} %copy-done.4, ...), custom_call_target="tpu_custom_call" | custom-call | flops 1048576 | bytes 1048576 | tf_op jit(solution)/shard_map/pallas_call | solution.py:50
  95.0 8.1 %all_to_all.31 = bf16[4,144,256]{2,1,0:T(8,128)(2,1)S(1)} all-to-all(bf16[4,144,256]{2,1,0:T(8,128)(2,1)S(1)} %get-tuple-element.34), channel_id=1, replica_groups=mesh['dp'=128,'mp'=4] {'mp'}, dimensions={0} | all-to-all | bytes 589824 | tf_op jit(solution)/shard_map/all_to_all | solution.py:447
  103.1 1.0 shard_map.137
  104.0 35.0 %all_to_all.32 = bf16[16,64,256]{2,1,0:T(8,128)(2,1)S(1)} all-to-all(bf16[16,64,256]{2,1,0:T(8,128)(2,1)S(1)} %bitcast.34), channel_id=1, replica_groups={{0,8,16,24,32,40,48,56,64,72,80,88,96,104,112,120},{4,12,20,28,36,44,52..., dimensions={0} | all-to-all | bytes 1048576 | tf_op jit(solution)/shard_map/all_to_all | solution.py:458
  139.1 0.7 shard_map.138
  139.8 24.3 %all_to_all.33 = bf16[32,32,256]{2,1,0:T(8,128)(2,1)S(1)} all-to-all(bf16[32,32,256]{2,1,0:T(8,128)(2,1)S(1)} %bitcast.36), channel_id=1, replica_groups={{0,1,2,3,4,5,6,7,128,129,130,131,132,133,134,135,256,257,258,259,260,26..., dimensions={0} | all-to-all | bytes 1048576 | tf_op jit(solution)/shard_map/all_to_all | solution.py:458
  164.2 18.0 %all_to_all.34 = f32[16,2,256]{2,1,0:T(2,128)S(1)} all-to-all(f32[16,2,256]{2,1,0:T(2,128)S(1)} %copy.30), channel_id=1, replica_groups={{0,8,16,24,32,40,48,56,64,72,80,88,96,104,112,120},{4,12,20,28,36,44,52..., dimensions={0} | all-to-all | bytes 65536 | tf_op jit(solution)/shard_map/all_to_all | solution.py:458
  182.1 0.6 reduce_sum.79
  (65 shorter events, 1.1 us)
Async XLA Ops:
  0.6 23.5 %copy-start = (bf16[48,8,1024]{2,1,0:T(8,128)(2,1)S(1)}, bf16[48,8,1024]{2,1,0:T(8,128)(2,1)}, u32[]{:S(2)}) copy-start(bf16[48,8,1024]{2,1,0:T(8,128)(2,1)} %param.16) | copy-start | bytes 2359300
  3.5 75.5 %all-to-all-start = ((bf16[128,8,512]{2,1,0:T(8,128)(2,1)}), bf16[128,8,512]{2,1,0:T(8,128)(2,1)S(1)}, u32[]{:S(2)}, u32[]{:S(2)}) async-start(bf16[128,8,512]{2,1,0:T(8,128)(2,1)} %get-tuple-element.19), calls=%async_computation | async-start | bytes 2097152 | tf_op jit(solution)/shard_map/all_to_all | solution.py:325
  24.9 17.5 %copy-start.28 = (s32[768]{0:T(1024)S(1)}, s32[768]{0:T(1024)}, u32[]{:S(2)}) copy-start(s32[768]{0:T(1024)} %param.12) | copy-start | bytes 9220
  24.9 19.5 %copy-start.27 = (s32[6,11,4]{1,2,0:T(4,128)S(1)}, s32[6,11,4]{1,2,0:T(4,128)}, u32[]{:S(2)}) copy-start(s32[6,11,4]{1,2,0:T(4,128)} %param.14) | copy-start | bytes 3172
  24.9 20.3 %copy-start.26 = (s32[6144]{0:T(1024)S(1)}, s32[6144]{0:T(1024)}, u32[]{:S(2)}) copy-start(s32[6144]{0:T(1024)} %param.13) | copy-start | bytes 73732
  24.9 21.8 %copy-start.29 = (bf16[256,32]{0,1:T(8,128)(2,1)S(1)}, bf16[256,32]{0,1:T(8,128)(2,1)}, u32[]{:S(2)}) copy-start(bf16[256,32]{0,1:T(8,128)(2,1)} %param.21) | copy-start | bytes 49156
  24.9 27.8 %copy-start.23 = (bf16[128,256]{1,0:T(8,128)(2,1)S(1)}, bf16[128,256]{1,0:T(8,128)(2,1)}, u32[]{:S(2)}) copy-start(bf16[128,256]{1,0:T(8,128)(2,1)} %query_ref.1) | copy-start | bytes 196612
  25.0 27.8 %copy-start.24 = (s32[6,4,128]{2,1,0:T(4,128)S(1)}, s32[6,4,128]{2,1,0:T(4,128)}, u32[]{:S(2)}) copy-start(s32[6,4,128]{2,1,0:T(4,128)} %align_ref.1) | copy-start | bytes 36868
  25.0 27.7 %copy-start.25 = (f32[256]{0:T(256)S(1)}, f32[256]{0:T(256)}, u32[]{:S(2)}) copy-start(f32[256]{0:T(256)} %param.22) | copy-start | bytes 3076
  26.0 20.8 %collective-permute-start = (bf16[16,8,1024]{2,1,0:T(8,128)(2,1)S(1)}, bf16[16,8,1024]{2,1,0:T(8,128)(2,1)S(1)}, u32[]{:S(2)}, u32[]{:S(2)}) collective-permute-start(bf16[16,8,1024]{2,1,0:T(8,128)(2,1)S(1)} %get-tuple-element.42), channel_id=1, source_target_pairs={{0,4},{4,0},{8,12},{12,8},{16,20},{20,16},{24,28},{28,24},{32,36},... | collective-permute-start | bytes 786440 | tf_op jit(solution)/shard_map/ppermute | solution.py:357
  28.8 21.2 %collective-permute-start.1 = (bf16[16,8,1024]{2,1,0:T(8,128)(2,1)S(1)}, bf16[16,8,1024]{2,1,0:T(8,128)(2,1)S(1)}, u32[]{:S(2)}, u32[]{:S(2)}) collective-permute-start(bf16[16,8,1024]{2,1,0:T(8,128)(2,1)S(1)} %get-tuple-element.41), channel_id=1, source_target_pairs={{0,128},{4,132},{8,136},{12,140},{16,144},{20,148},{24,152},{28,15... | collective-permute-start | bytes 786440 | tf_op jit(solution)/shard_map/ppermute | solution.py:357
  31.7 27.6 %collective-permute-start.2 = (bf16[16,8,1024]{2,1,0:T(8,128)(2,1)}, bf16[16,8,1024]{2,1,0:T(8,128)(2,1)S(1)}, u32[]{:S(2)}, u32[]{:S(2)}) collective-permute-start(bf16[16,8,1024]{2,1,0:T(8,128)(2,1)} %get-tuple-element.40), channel_id=1, source_target_pairs={{0,132},{4,128},{8,140},{12,136},{16,148},{20,144},{24,156},{28,15... | collective-permute-start | bytes 786440 | tf_op jit(solution)/shard_map/ppermute | solution.py:357
  35.4 24.7 %collective-permute-start.3 = (bf16[16,8,1024]{2,1,0:T(8,128)(2,1)}, bf16[16,8,1024]{2,1,0:T(8,128)(2,1)S(1)}, u32[]{:S(2)}, u32[]{:S(2)}) collective-permute-start(bf16[16,8,1024]{2,1,0:T(8,128)(2,1)} %get-tuple-element.39), channel_id=1, source_target_pairs={{0,256},{4,260},{8,264},{12,268},{16,272},{20,276},{24,280},{28,28... | collective-permute-start | bytes 786440 | tf_op jit(solution)/shard_map/ppermute | solution.py:357
  38.6 27.0 %collective-permute-start.4 = (bf16[16,8,1024]{2,1,0:T(8,128)(2,1)}, bf16[16,8,1024]{2,1,0:T(8,128)(2,1)S(1)}, u32[]{:S(2)}, u32[]{:S(2)}) collective-permute-start(bf16[16,8,1024]{2,1,0:T(8,128)(2,1)} %get-tuple-element.38), channel_id=1, source_target_pairs={{0,260},{4,256},{8,268},{12,264},{16,276},{20,272},{24,284},{28,28... | collective-permute-start | bytes 786440 | tf_op jit(solution)/shard_map/ppermute | solution.py:357
  46.9 22.8 %copy-start.7 = (bf16[16,8,1024]{2,1,0:T(8,128)(2,1)}, bf16[16,8,1024]{2,1,0:T(8,128)(2,1)S(1)}, u32[]{:S(2)}) copy-start(bf16[16,8,1024]{2,1,0:T(8,128)(2,1)S(1)} %collective-permute-done.refs_1_) | copy-start | bytes 786436
  46.9 19.4 %collective-permute-start.5 = (bf16[16,8,1024]{2,1,0:T(8,128)(2,1)}, bf16[16,8,1024]{2,1,0:T(8,128)(2,1)S(1)}, u32[]{:S(2)}, u32[]{:S(2)}) collective-permute-start(bf16[16,8,1024]{2,1,0:T(8,128)(2,1)} %get-tuple-element.37), channel_id=1, source_target_pairs={{0,384},{4,388},{8,392},{12,396},{16,400},{20,404},{24,408},{28,41... | collective-permute-start | bytes 786440 | tf_op jit(solution)/shard_map/ppermute | solution.py:357
  50.1 19.6 %copy-start.9 = (bf16[16,8,1024]{2,1,0:T(8,128)(2,1)}, bf16[16,8,1024]{2,1,0:T(8,128)(2,1)S(1)}, u32[]{:S(2)}) copy-start(bf16[16,8,1024]{2,1,0:T(8,128)(2,1)S(1)} %collective-permute-done.1.refs_2_) | copy-start | bytes 786436
  50.1 19.6 %collective-permute-start.6 = (bf16[16,8,1024]{2,1,0:T(8,128)(2,1)}, bf16[16,8,1024]{2,1,0:T(8,128)(2,1)S(1)}, u32[]{:S(2)}, u32[]{:S(2)}) collective-permute-start(bf16[16,8,1024]{2,1,0:T(8,128)(2,1)} %get-tuple-element.36), channel_id=1, source_target_pairs={{0,388},{4,384},{8,396},{12,392},{16,404},{20,400},{24,412},{28,40... | collective-permute-start | bytes 786440 | tf_op jit(solution)/shard_map/ppermute | solution.py:357
  52.7 1.0 copy-start.21
  53.7 1.0 copy-start.22
  56.3 0.9 copy-start.1
  57.2 0.9 copy-start.3
  58.1 0.8 copy-start.5
  59.4 0.7 copy-start.11
  60.1 0.7 copy-start.13
  65.6 0.7 copy-start.15
  66.3 0.7 copy-start.17
  69.7 0.7 copy-start.19
  70.4 0.9 copy-start.8
  71.3 0.9 copy-start.10
  72.3 0.9 copy-start.12
  73.2 0.9 copy-start.14
  74.2 0.9 copy-start.16
  75.1 0.9 copy-start.18
  76.1 0.9 copy-start.20
  79.0 12.7 %copy-start.2 = (f32[6,128,256]{2,1,0:T(8,128)S(1)}, f32[6,128,256]{2,1,0:T(8,128)}, u32[]{:S(2)}) copy-start(f32[6,128,256]{2,1,0:T(8,128)} %copy-done.1) | copy-start | bytes 2359300
  79.1 12.7 %copy-start.4 = (f32[6,128,256]{2,1,0:T(8,128)S(1)}, f32[6,128,256]{2,1,0:T(8,128)}, u32[]{:S(2)}) copy-start(f32[6,128,256]{2,1,0:T(8,128)} %copy-done.3) | copy-start | bytes 2359300
  79.1 12.7 %copy-start.6 = (bf16[1024,256]{1,0:T(8,128)(2,1)S(1)}, bf16[1024,256]{1,0:T(8,128)(2,1)}, u32[]{:S(2)}) copy-start(bf16[1024,256]{1,0:T(8,128)(2,1)} %copy-done.5) | copy-start | bytes 1572868

commit v6 on v5

--- a/solution.py
+++ b/solution.py
@@ -134,16 +134,21 @@
 
 
 def turn_kernel(*refs, bands, share):
-    out_ref, block_ref, turned_ref = refs[-3:]
-    pieces = refs[:-3]
+    out_ref, block_ref, turned_ref, sems = refs[-4:]
+    pieces = refs[:-4]
     deep, quarter, _ = pieces[0].shape
-    for z in range(deep):
-        for p, piece in enumerate(pieces):
-            at = (z * len(pieces) + p) * quarter
-            block_ref[at : at + quarter, :] = piece[z]
-    groups, _, width = turned_ref.shape
+    moves = [
+        pltpu.make_async_copy(piece, block_ref.at[:, p], sems.at[p]) for p, piece in enumerate(pieces)
+    ]
+    for move in moves:
+        move.start()
+    for move in moves:
+        move.wait()
+    groups, depth, width = turned_ref.shape
+    some = width // (len(pieces) * quarter)
     for g in range(groups):
-        turned_ref[g] = block_ref[g * width : (g + 1) * width, :].astype(F32).T
+        block = block_ref[g * some : (g + 1) * some].reshape(width, depth)
+        turned_ref[g] = block.astype(F32).T
     step = CORES * bands * share
     at = 0
     for y in range(len(pieces) // CORES):
@@ -166,7 +171,6 @@
     gain_ref,
     base_ref,
     pull_ref,
-    heads_ref,
     scale_ref,
 ):
     samples, cells, channels = prev_ref.shape
@@ -181,9 +185,6 @@
         pick = iota(shape, 0) == (iota(shape, 1) // head_dim) * KT + k
         weight = dot(point_ref[...], pick.astype(F32).astype(BF16)).astype(BF16)
         gates.append(jax.nn.sigmoid(dot(query, weight)))
-    for h in range(HEADS):
-        mask = (iota((1, channels), 1) // head_dim == h).astype(F32).astype(BF16)
-        heads_ref[h * cells : (h + 1) * cells, :] = query * mask
     for m in range(samples):
         total = wide
         for k in range(KT):
@@ -203,17 +204,27 @@
 def attention_kernel(
     count_ref,
     kv_ref,
-    base_ref,
-    pull_ref,
-    heads_ref,
+    base_hbm,
+    pull_hbm,
+    query_ref,
     gain_ref,
     out_ref,
     grad_ref,
+    base_ref,
+    pull_ref,
+    sems,
+    heads_ref,
     score_ref,
     prob_ref,
     norm_ref,
     cross_ref,
 ):
+    moves = [
+        pltpu.make_async_copy(base_hbm, base_ref, sems.at[0]),
+        pltpu.make_async_copy(pull_hbm, pull_ref, sems.at[1]),
+    ]
+    for move in moves:
+        move.start()
     parts, rows, width = kv_ref.shape
     samples, queries, channels = base_ref.shape
     step = rows // samples
@@ -225,6 +236,8 @@
     masks = [(lane_head == h).astype(F32).astype(BF16) for h in range(HEADS)]
     factor = float(head_dim) ** -0.5 * LOG2_E
     place = iota((keys, HEADS * queries), 0) % step // quarter
+    for h in range(HEADS):
+        heads_ref[h * queries : (h + 1) * queries, :] = query_ref[...] * masks[h]
     spans = [slice(m * step, (m + 1) * step) for m in range(samples)]
     ray = kv_ref[:, :, channels:].reshape(parts * rows, channels)
     score_ref[...] = dot(ray, heads_ref[...], 1, 1).reshape(score_ref.shape)
@@ -233,6 +246,7 @@
         scores = jnp.where(place < count_ref[m], scores, MASKED)
         raised = jnp.exp2((scores - jnp.max(scores, axis=0, keepdims=True)) * factor)
         prob_ref[m] = (raised * (1.0 / jnp.sum(raised, axis=0, keepdims=True))).astype(BF16)
+    moves[0].wait()
     for m in range(samples):
         values = kv_ref[:, spans[m], :channels].reshape(keys, channels)
         values = jnp.concatenate([values * mask for mask in masks], axis=0)
@@ -241,6 +255,7 @@
             [probs[:, h * queries : (h + 1) * queries] for h in range(HEADS)], axis=0
         )
         norm_ref[m] = base_ref[m] + dot(tall, values, 0, 0)
+    moves[1].wait()
     for m in range(samples):
         pre_norm = norm_ref[m]
         centred = pre_norm - jnp.mean(pre_norm, axis=1, keepdims=True)
@@ -355,24 +370,11 @@
             for c in cs
         ]
         pieces.append(lax.ppermute(dealt[p], "dp", moves))
-    tokens = owners * quarter
-    turned = call(
-        functools.partial(turn_kernel, bands=bands, share=share),
-        on_chip((depth, tokens), BF16),
-        *pieces,
-        scratch=[
-            pltpu.VMEM((tokens, depth), BF16),
-            pltpu.VMEM((tokens // 128, depth, 128), F32),
-        ],
-        cost=cost,
-        pinned=False,
-    )
-    base, pull, heads, gain = call(
+    base, pull, gain = call(
         temporal_kernel,
         (
-            on_chip((samples, queries, channels), F32),
-            on_chip((samples, queries, channels), F32),
-            on_chip((HEADS * queries, channels), BF16),
+            pltpu.HBM((samples, queries, channels), F32),
+            pltpu.HBM((samples, queries, channels), F32),
             on_chip((1, channels), F32),
         ),
         band_id[None],
@@ -410,8 +412,8 @@
     source = jnp.maximum(lane_of, 0)
     bin_y, bin_z, bin_core = place_of(source)
     back_lane = (bin_z * chips + (my_y - bin_y) % chips) * CORES + (bin_core + my_core) % CORES
-    got, base, pull, heads, gain, turned, source, back_lane, count = lax.optimization_barrier(
-        (got, base, pull, heads, gain, turned, source, back_lane, count)
+    got, base, pull, gain, pieces, source, back_lane, count = lax.optimization_barrier(
+        (got, base, pull, gain, pieces, source, back_lane, count)
     )
     piece = samples * SEEN * quarter
     chosen_kv = call(
@@ -424,6 +426,20 @@
     kv = lax.all_to_all(
         chosen_kv.reshape(bands, piece, 2 * channels), "mp", split_axis=0, concat_axis=0, tiled=True
     )
+    tokens = owners * quarter
+    turned = call(
+        functools.partial(turn_kernel, bands=bands, share=share),
+        pltpu.HBM((depth, tokens), BF16),
+        *pieces,
+        specs=[pl.BlockSpec(memory_space=pltpu.HBM)] * len(pieces),
+        scratch=[
+            pltpu.VMEM((deep, len(pieces), quarter, depth), BF16),
+            pltpu.VMEM((tokens // 128, depth, 128), F32),
+            pltpu.SemaphoreType.DMA((len(pieces),)),
+        ],
+        cost=cost,
+    )
+    kv, turned = lax.optimization_barrier((kv, turned))
     bev_out, grads = call(
         attention_kernel,
         (
@@ -434,10 +450,14 @@
         kv,
         base,
         pull,
-        heads,
+        bev_query,
         gain,
-        specs=[smem()] + [vmem()] * 5,
+        specs=[smem(), vmem()] + [pl.BlockSpec(memory_space=pltpu.HBM)] * 2 + [vmem()] * 2,
         scratch=[
+            pltpu.VMEM((samples, queries, channels), F32),
+            pltpu.VMEM((samples, queries, channels), F32),
+            pltpu.SemaphoreType.DMA((2,)),
+            pltpu.VMEM((HEADS * queries, channels), BF16),
             pltpu.VMEM((bands, piece, HEADS * queries), F32),
             pltpu.VMEM((samples, bands * SEEN * quarter, HEADS * queries), BF16),
             pltpu.VMEM((samples, queries, channels), F32),

time: 184 us -> 177 us (0.962)
  blocking collectives: 97.3 us -> 78.2 us
  waiting for transfers between devices: 7.52 us -> 24.2 us
  local copies, waits for them, and re-layouts: 16.7 us -> 2.18 us
  Pallas kernels: 12.7 us -> 18.2 us
  starting transfers between devices: 42.7 us -> 47.3 us
    unnamed x61 -> x33, local copies, waits for them, and re-layouts: 14.9 us -> 0.21 us
    all_to_all x1 -> x0, blocking collectives: 12 us -> none  [on_device(): lax.all_to_all(chosen_kv.reshape(bands, piece, 2 * channels), 'mp', split...]
    all_to_all x1, waiting for transfers between devices: 0.01 us -> 8.71 us  [on_device(): got = lax.all_to_all(lanes, 'dp', split_axis=0, concat_axis=0, tiled=True)]
    all_to_all x3, blocking collectives: 77.3 us -> 70.1 us  [exchange(): lax.all_to_all(part, axis, split_axis=0, concat_axis=0, tiled=True, axis_...]
    pallas_call x8, Pallas kernels: 12.7 us -> 18.2 us  [call(): pl.pallas_call(body, out_shape=outs, in_specs=specs, out_specs=jax.tree.m...]
    ppermute x7, waiting for transfers between devices: 7.52 us -> 13 us  [on_device(): pieces.append(lax.ppermute(dealt[p], 'dp', moves))]
    all_to_all x0 -> x1, starting transfers between devices: none -> 4.03 us  [on_device(): lax.all_to_all(chosen_kv.reshape(bands, piece, 2 * channels), 'mp', split...]
    all_to_all x0 -> x1, waiting for transfers between devices: none -> 2.52 us  [on_device(): lax.all_to_all(chosen_kv.reshape(bands, piece, 2 * channels), 'mp', split...]
  transfers between devices with their start and end apart: 8 -> 9, of which waited for: 2 -> 4; matrix products, arithmetic and copies ran while one was open for 2% -> 2% of each run, Pallas kernels for 2% -> 5%
where the time goes in v6:
time: 177 us; the launch traced here: 176 us
  blocking collectives  78.2 us (44%)
  starting transfers between devices  47.3 us (27%)
  waiting for transfers between devices  24.2 us (14%)
  Pallas kernels  18.2 us (10%)
  between operations  3.01 us (2%)
  other arithmetic  2.85 us (2%)
  local copies, waits for them, and re-layouts  2.18 us (1%)
    all_to_all x3, blocking collectives, exchange(): lax.all_to_all(part, axis, split_axis=0, concat_axis=0, tiled=True, axis_...  70.1 us
    ppermute x7, starting transfers between devices, on_device(): pieces.append(lax.ppermute(dealt[p], 'dp', moves))  22.7 us
    all_to_all x1, starting transfers between devices, on_device(): got = lax.all_to_all(lanes, 'dp', split_axis=0, concat_axis=0, tiled=True)  20.6 us
    pallas_call x8, Pallas kernels, call(): pl.pallas_call(body, out_shape=outs, in_specs=specs, out_specs=jax.tree.m...  18.2 us
    ppermute x7, waiting for transfers between devices, on_device(): pieces.append(lax.ppermute(dealt[p], 'dp', moves))  13 us
    all_to_all x1, waiting for transfers between devices, on_device(): got = lax.all_to_all(lanes, 'dp', split_axis=0, concat_axis=0, tiled=True)  8.71 us
    all_to_all x1, blocking collectives, on_device(): grads = lax.all_to_all(grads, 'mp', split_axis=0, concat_axis=0, tiled=True)  8.07 us
    all_to_all x1, starting transfers between devices, on_device(): lax.all_to_all(chosen_kv.reshape(bands, piece, 2 * channels), 'mp', split...  4.03 us
  transfers between devices with their start and end apart: 9, of which 4 were waited for; matrix products, arithmetic and copies ran while one was open for 2% of the time, Pallas kernels for 5%

profile of v6, /device:TPU:1, one launch (start us, length us, event | category | flops | bytes accessed | tf_op | source)
XLA Modules:
  0.0 175.9 jit_solution(7914303044719480266)
XLA Ops:
  0.6 2.8 %shard_map.131 = (bf16[128,8,512]{2,1,0:T(8,128)(2,1)}, s32[8,48]{1,0:T(8,128)S(1)}) custom-call(s32[1]{0:T(128)} %bitcast.bin_ref, s32[6,128]{1,0:T(8,128)} %bitcast.43, s32[1,6144]{1,0:T(1,128)} %bitcast.42, bf16[384,1024]{1,0:T(8,128)(2,1)} %bitcast.37, bf16[384,256]{1,0:T(8,128)(2,1)} %bitcast.40, bf16[1024,256]{1,0:T(8,128)(2,1)} %weight_hbm.1), custom_call_target="tpu_custom_call" | custom-call | flops 1048576 | bytes 1048576 | tf_op jit(solution)/shard_map/pallas_call | solution.py:50
  3.5 20.6 %all-to-all-start = ((bf16[128,8,512]{2,1,0:T(8,128)(2,1)}), bf16[128,8,512]{2,1,0:T(8,128)(2,1)S(1)}, u32[]{:S(2)}, u32[]{:S(2)}) async-start(bf16[128,8,512]{2,1,0:T(8,128)(2,1)} %get-tuple-element.26), calls=%async_computation | async-start | bytes 2097152 | tf_op jit(solution)/shard_map/all_to_all | solution.py:340
  24.1 0.7 shard_map.133
  24.9 0.0 copy-start.14
  24.9 0.0 copy-start.15
  24.9 0.0 copy-start.2
  25.0 0.0 copy-start.4
  25.0 0.0 copy-start.5
  25.0 1.3 fusion.18
  26.3 5.3 %collective-permute-start.6 = (bf16[16,8,1024]{2,1,0:T(8,128)(2,1)}, bf16[16,8,1024]{2,1,0:T(8,128)(2,1)S(1)}, u32[]{:S(2)}, u32[]{:S(2)}) collective-permute-start(bf16[16,8,1024]{2,1,0:T(8,128)(2,1)} %get-tuple-element.50), channel_id=1, source_target_pairs={{0,388},{4,384},{8,396},{12,392},{16,404},{20,400},{24,412},{28,40... | collective-permute-start | bytes 786440 | tf_op jit(solution)/shard_map/ppermute | solution.py:372
  31.6 2.3 %collective-permute-start.5 = (bf16[16,8,1024]{2,1,0:T(8,128)(2,1)}, bf16[16,8,1024]{2,1,0:T(8,128)(2,1)S(1)}, u32[]{:S(2)}, u32[]{:S(2)}) collective-permute-start(bf16[16,8,1024]{2,1,0:T(8,128)(2,1)} %get-tuple-element.51), channel_id=1, source_target_pairs={{0,384},{4,388},{8,392},{12,396},{16,400},{20,404},{24,408},{28,41... | collective-permute-start | bytes 786440 | tf_op jit(solution)/shard_map/ppermute | solution.py:372
  33.9 2.0 %collective-permute-start.4 = (bf16[16,8,1024]{2,1,0:T(8,128)(2,1)}, bf16[16,8,1024]{2,1,0:T(8,128)(2,1)S(1)}, u32[]{:S(2)}, u32[]{:S(2)}) collective-permute-start(bf16[16,8,1024]{2,1,0:T(8,128)(2,1)} %get-tuple-element.52), channel_id=1, source_target_pairs={{0,260},{4,256},{8,268},{12,264},{16,276},{20,272},{24,284},{28,28... | collective-permute-start | bytes 786440 | tf_op jit(solution)/shard_map/ppermute | solution.py:372
  35.9 5.1 %collective-permute-start.3 = (bf16[16,8,1024]{2,1,0:T(8,128)(2,1)}, bf16[16,8,1024]{2,1,0:T(8,128)(2,1)S(1)}, u32[]{:S(2)}, u32[]{:S(2)}) collective-permute-start(bf16[16,8,1024]{2,1,0:T(8,128)(2,1)} %get-tuple-element.53), channel_id=1, source_target_pairs={{0,256},{4,260},{8,264},{12,268},{16,272},{20,276},{24,280},{28,28... | collective-permute-start | bytes 786440 | tf_op jit(solution)/shard_map/ppermute | solution.py:372
  41.0 3.2 %collective-permute-start.2 = (bf16[16,8,1024]{2,1,0:T(8,128)(2,1)}, bf16[16,8,1024]{2,1,0:T(8,128)(2,1)S(1)}, u32[]{:S(2)}, u32[]{:S(2)}) collective-permute-start(bf16[16,8,1024]{2,1,0:T(8,128)(2,1)} %get-tuple-element.54), channel_id=1, source_target_pairs={{0,132},{4,128},{8,140},{12,136},{16,148},{20,144},{24,156},{28,15... | collective-permute-start | bytes 786440 | tf_op jit(solution)/shard_map/ppermute | solution.py:372
  44.3 0.6 select_reduce_fusion.2
  46.2 0.1 dynamic_slice.9
  46.3 0.1 copy.28
  47.1 0.1 fusion.16
  47.2 0.1 select_reduce_fusion.3
  47.3 0.1 multiply_reduce_fusion
  47.4 0.1 add_add_fusion
  47.5 0.4 select_reduce_fusion.1
  47.9 0.5 select_reduce_fusion
  48.4 0.2 fusion.17
  48.6 0.1 copy.27.point_ref
  48.7 1.9 %collective-permute-start.1 = (bf16[16,8,1024]{2,1,0:T(8,128)(2,1)}, bf16[16,8,1024]{2,1,0:T(8,128)(2,1)}, u32[]{:S(2)}, u32[]{:S(2)}) collective-permute-start(bf16[16,8,1024]{2,1,0:T(8,128)(2,1)} %get-tuple-element.55), channel_id=1, source_target_pairs={{0,128},{4,132},{8,136},{12,140},{16,144},{20,148},{24,152},{28,15... | collective-permute-start | bytes 786440 | tf_op jit(solution)/shard_map/ppermute | solution.py:372
  50.7 10.4 %collective-permute-done.5.refs_6_ = bf16[16,8,1024]{2,1,0:T(8,128)(2,1)S(1)} collective-permute-done((bf16[16,8,1024]{2,1,0:T(8,128)(2,1)}, bf16[16,8,1024]{2,1,0:T(8,128)(2,1)S(1)}, u32[]{:S(2)}, u32[]{:S(2)}) %collective-permute-start.5) | collective-permute-done | bytes 262176 | tf_op jit(solution)/shard_map/ppermute | solution.py:372
  61.1 2.9 %collective-permute-start = (bf16[16,8,1024]{2,1,0:T(8,128)(2,1)}, bf16[16,8,1024]{2,1,0:T(8,128)(2,1)}, u32[]{:S(2)}, u32[]{:S(2)}) collective-permute-start(bf16[16,8,1024]{2,1,0:T(8,128)(2,1)} %get-tuple-element.56), channel_id=1, source_target_pairs={{0,4},{4,0},{8,12},{12,8},{16,20},{20,16},{24,28},{28,24},{32,36},... | collective-permute-start | bytes 786440 | tf_op jit(solution)/shard_map/ppermute | solution.py:372
  64.0 2.7 %shard_map.132 = (f32[6,128,256]{2,1,0:T(8,128)}, f32[6,128,256]{2,1,0:T(8,128)}, f32[1,256]{1,0:T(1,128)S(1)}) custom-call(s32[1]{0:T(128)} %bitcast.5.band_ref, bf16[128,256]{1,0:T(8,128)(2,1)S(1)} %copy-done.2, bf16[256,32]{1,0:T(8,128)(2,1)S(1)} %copy.27.point_ref, bf16[6,128,256]{2,1,0:T(8,128)(2,1)S(1)} %copy-done.3, s32[6,4,128]{2,1,0:T(4,128)S(1)} %copy-done.5, ...), custom_call_target="tpu_custom_call" | custom-call | flops 1073741824 | bytes 4194304 | tf_op jit(solution)/shard_map/pallas_call | solution.py:50
  66.7 0.1 copy.29
  66.8 0.1 max.17.source_ref
  66.9 0.2 dynamic-slice_reduce_fusion.count_ref
  67.2 0.0 copy-start.11
  67.2 2.5 %collective-permute-done.1.refs_2_ = bf16[16,8,1024]{2,1,0:T(8,128)(2,1)} collective-permute-done((bf16[16,8,1024]{2,1,0:T(8,128)(2,1)}, bf16[16,8,1024]{2,1,0:T(8,128)(2,1)}, u32[]{:S(2)}, u32[]{:S(2)}) %collective-permute-start.1) | collective-permute-done | bytes 262176 | tf_op jit(solution)/shard_map/ppermute | solution.py:372
  69.7 8.7 %all-to-all-done.lane_ref = bf16[128,8,512]{2,1,0:T(8,128)(2,1)S(1)} async-done(((bf16[128,8,512]{2,1,0:T(8,128)(2,1)}), bf16[128,8,512]{2,1,0:T(8,128)(2,1)S(1)}, u32[]{:S(2)}, u32[]{:S(2)}) %all-to-all-start) | async-done | bytes 1048608 | tf_op jit(solution)/shard_map/all_to_all | solution.py:340
  78.4 1.4 shard_map.134
  79.9 4.0 %all-to-all-start.1 = ((bf16[4,144,512]{2,1,0:T(8,128)(2,1)}), bf16[4,144,512]{2,1,0:T(8,128)(2,1)S(1)}, u32[]{:S(2)}, u32[]{:S(2)}) async-start(bf16[4,144,512]{2,1,0:T(8,128)(2,1)} %bitcast.9), calls=%async_computation.1 | async-start | bytes 1179648 | tf_op jit(solution)/shard_map/all_to_all | solution.py:426
  83.9 4.9 %shard_map.135.turned_ref = bf16[1024,1024]{1,0:T(8,128)(2,1)} custom-call(bf16[16,8,1024]{2,1,0:T(8,128)(2,1)} %get-tuple-element.34.refs_0_, bf16[16,8,1024]{2,1,0:T(8,128)(2,1)} %collective-permute-done.refs_1_, bf16[16,8,1024]{2,1,0:T(8,128)(2,1)} %collective-permute-done.1.refs_2_, bf16[16,8,1024]{2,1,0:T(8,128)(2,1)} %copy-done.11, ...), custom_call_target="tpu_custom_call" | custom-call | flops 1073741824 | bytes 4194304 | tf_op jit(solution)/shard_map/pallas_call | solution.py:50
  88.8 2.5 %all-to-all-done.1.kv_ref = bf16[4,144,512]{2,1,0:T(8,128)(2,1)S(1)} async-done(((bf16[4,144,512]{2,1,0:T(8,128)(2,1)}), bf16[4,144,512]{2,1,0:T(8,128)(2,1)S(1)}, u32[]{:S(2)}, u32[]{:S(2)}) %all-to-all-start.1) | async-done | bytes 589856 | tf_op jit(solution)/shard_map/all_to_all | solution.py:426
  91.3 3.9 %shard_map.136 = (bf16[6,128,256]{2,1,0:T(8,128)(2,1)}, bf16[4,144,256]{2,1,0:T(8,128)(2,1)S(1)}) custom-call(s32[6]{0:T(128)S(1)} %dynamic-slice_reduce_fusion.count_ref, bf16[4,144,512]{2,1,0:T(8,128)(2,1)S(1)} %all-to-all-done.1.kv_ref, f32[6,128,256]{2,1,0:T(8,128)} %get-tuple-element.43.base_hbm, f32[6,128,256]{2,1,0:T(8,128)} %get-tuple-element.44.pull_hbm, ...), custom_call_target="tpu_custom_call" | custom-call | flops 1048576 | bytes 1048576 | tf_op jit(solution)/shard_map/pallas_call | solution.py:50
  95.3 8.1 %all_to_all.30 = bf16[4,144,256]{2,1,0:T(8,128)(2,1)S(1)} all-to-all(bf16[4,144,256]{2,1,0:T(8,128)(2,1)S(1)} %get-tuple-element.48), channel_id=1, replica_groups=mesh['dp'=128,'mp'=4] {'mp'}, dimensions={0} | all-to-all | bytes 589824 | tf_op jit(solution)/shard_map/all_to_all | solution.py:467
  103.4 1.0 shard_map.137
  104.3 31.3 %all_to_all.31 = bf16[16,64,256]{2,1,0:T(8,128)(2,1)S(1)} all-to-all(bf16[16,64,256]{2,1,0:T(8,128)(2,1)S(1)} %bitcast.33), channel_id=1, replica_groups={{0,8,16,24,32,40,48,56,64,72,80,88,96,104,112,120},{4,12,20,28,36,44,52..., dimensions={0} | all-to-all | bytes 1048576 | tf_op jit(solution)/shard_map/all_to_all | solution.py:478
  135.6 0.7 shard_map.138
  136.3 21.1 %all_to_all.32 = bf16[32,32,256]{2,1,0:T(8,128)(2,1)S(1)} all-to-all(bf16[32,32,256]{2,1,0:T(8,128)(2,1)S(1)} %bitcast.35), channel_id=1, replica_groups={{0,1,2,3,4,5,6,7,128,129,130,131,132,133,134,135,256,257,258,259,260,26..., dimensions={0} | all-to-all | bytes 1048576 | tf_op jit(solution)/shard_map/all_to_all | solution.py:478
  157.4 0.1 convert_reduce_fusion
  157.6 17.7 %all_to_all.33 = f32[16,2,256]{2,1,0:T(2,128)S(1)} all-to-all(f32[16,2,256]{2,1,0:T(2,128)S(1)} %copy.30), channel_id=1, replica_groups={{0,8,16,24,32,40,48,56,64,72,80,88,96,104,112,120},{4,12,20,28,36,44,52..., dimensions={0} | all-to-all | bytes 65536 | tf_op jit(solution)/shard_map/all_to_all | solution.py:478
  175.3 0.6 reduce_sum.79
  (38 shorter events, 0.2 us)
Async XLA Ops:
  0.6 23.5 %copy-start.1 = (bf16[48,8,1024]{2,1,0:T(8,128)(2,1)S(1)}, bf16[48,8,1024]{2,1,0:T(8,128)(2,1)}, u32[]{:S(2)}) copy-start(bf16[48,8,1024]{2,1,0:T(8,128)(2,1)} %param.16) | copy-start | bytes 2359300
  3.5 74.9 %all-to-all-start = ((bf16[128,8,512]{2,1,0:T(8,128)(2,1)}), bf16[128,8,512]{2,1,0:T(8,128)(2,1)S(1)}, u32[]{:S(2)}, u32[]{:S(2)}) async-start(bf16[128,8,512]{2,1,0:T(8,128)(2,1)} %get-tuple-element.26), calls=%async_computation | async-start | bytes 2097152 | tf_op jit(solution)/shard_map/all_to_all | solution.py:340
  24.9 19.4 %copy-start.14 = (s32[768]{0:T(1024)S(1)}, s32[768]{0:T(1024)}, u32[]{:S(2)}) copy-start(s32[768]{0:T(1024)} %param.12) | copy-start | bytes 9220
  24.9 21.4 %copy-start.13 = (s32[6,11,4]{1,2,0:T(4,128)S(1)}, s32[6,11,4]{1,2,0:T(4,128)}, u32[]{:S(2)}) copy-start(s32[6,11,4]{1,2,0:T(4,128)} %param.14) | copy-start | bytes 3172
  24.9 22.2 %copy-start.12 = (s32[6144]{0:T(1024)S(1)}, s32[6144]{0:T(1024)}, u32[]{:S(2)}) copy-start(s32[6144]{0:T(1024)} %param.13) | copy-start | bytes 73732
  24.9 23.7 %copy-start.15 = (bf16[256,32]{0,1:T(8,128)(2,1)S(1)}, bf16[256,32]{0,1:T(8,128)(2,1)}, u32[]{:S(2)}) copy-start(bf16[256,32]{0,1:T(8,128)(2,1)} %param.21) | copy-start | bytes 49156
  24.9 39.1 %copy-start.2 = (bf16[128,256]{1,0:T(8,128)(2,1)S(1)}, bf16[128,256]{1,0:T(8,128)(2,1)}, u32[]{:S(2)}) copy-start(bf16[128,256]{1,0:T(8,128)(2,1)} %query_ref.3) | copy-start | bytes 196612
  24.9 39.1 %copy-start.3 = (bf16[6,128,256]{2,1,0:T(8,128)(2,1)S(1)}, bf16[6,128,256]{2,1,0:T(8,128)(2,1)}, u32[]{:S(2)}) copy-start(bf16[6,128,256]{2,1,0:T(8,128)(2,1)} %prev_ref.1) | copy-start | bytes 1179652
  25.0 39.1 %copy-start.4 = (bf16[6,128,256]{2,1,0:T(8,128)(2,1)S(1)}, bf16[6,128,256]{2,1,0:T(8,128)(2,1)}, u32[]{:S(2)}) copy-start(bf16[6,128,256]{2,1,0:T(8,128)(2,1)} %cotangent_ref.1) | copy-start | bytes 1179652
  25.0 39.1 %copy-start.5 = (s32[6,4,128]{2,1,0:T(4,128)S(1)}, s32[6,4,128]{2,1,0:T(4,128)}, u32[]{:S(2)}) copy-start(s32[6,4,128]{2,1,0:T(4,128)} %align_ref.1) | copy-start | bytes 36868
  25.0 39.1 %copy-start.6 = (f32[256]{0:T(256)S(1)}, f32[256]{0:T(256)}, u32[]{:S(2)}) copy-start(f32[256]{0:T(256)} %param.22) | copy-start | bytes 3076
  26.3 22.4 %collective-permute-start.6 = (bf16[16,8,1024]{2,1,0:T(8,128)(2,1)}, bf16[16,8,1024]{2,1,0:T(8,128)(2,1)S(1)}, u32[]{:S(2)}, u32[]{:S(2)}) collective-permute-start(bf16[16,8,1024]{2,1,0:T(8,128)(2,1)} %get-tuple-element.50), channel_id=1, source_target_pairs={{0,388},{4,384},{8,396},{12,392},{16,404},{20,400},{24,412},{28,40... | collective-permute-start | bytes 786440 | tf_op jit(solution)/shard_map/ppermute | solution.py:372
  31.6 29.5 %collective-permute-start.5 = (bf16[16,8,1024]{2,1,0:T(8,128)(2,1)}, bf16[16,8,1024]{2,1,0:T(8,128)(2,1)S(1)}, u32[]{:S(2)}, u32[]{:S(2)}) collective-permute-start(bf16[16,8,1024]{2,1,0:T(8,128)(2,1)} %get-tuple-element.51), channel_id=1, source_target_pairs={{0,384},{4,388},{8,392},{12,396},{16,400},{20,404},{24,408},{28,41... | collective-permute-start | bytes 786440 | tf_op jit(solution)/shard_map/ppermute | solution.py:372
  33.9 33.3 %collective-permute-start.4 = (bf16[16,8,1024]{2,1,0:T(8,128)(2,1)}, bf16[16,8,1024]{2,1,0:T(8,128)(2,1)S(1)}, u32[]{:S(2)}, u32[]{:S(2)}) collective-permute-start(bf16[16,8,1024]{2,1,0:T(8,128)(2,1)} %get-tuple-element.52), channel_id=1, source_target_pairs={{0,260},{4,256},{8,268},{12,264},{16,276},{20,272},{24,284},{28,28... | collective-permute-start | bytes 786440 | tf_op jit(solution)/shard_map/ppermute | solution.py:372
  35.9 31.3 %collective-permute-start.3 = (bf16[16,8,1024]{2,1,0:T(8,128)(2,1)}, bf16[16,8,1024]{2,1,0:T(8,128)(2,1)S(1)}, u32[]{:S(2)}, u32[]{:S(2)}) collective-permute-start(bf16[16,8,1024]{2,1,0:T(8,128)(2,1)} %get-tuple-element.53), channel_id=1, source_target_pairs={{0,256},{4,260},{8,264},{12,268},{16,272},{20,276},{24,280},{28,28... | collective-permute-start | bytes 786440 | tf_op jit(solution)/shard_map/ppermute | solution.py:372
  41.0 26.2 %collective-permute-start.2 = (bf16[16,8,1024]{2,1,0:T(8,128)(2,1)}, bf16[16,8,1024]{2,1,0:T(8,128)(2,1)S(1)}, u32[]{:S(2)}, u32[]{:S(2)}) collective-permute-start(bf16[16,8,1024]{2,1,0:T(8,128)(2,1)} %get-tuple-element.54), channel_id=1, source_target_pairs={{0,132},{4,128},{8,140},{12,136},{16,148},{20,144},{24,156},{28,15... | collective-permute-start | bytes 786440 | tf_op jit(solution)/shard_map/ppermute | solution.py:372
  48.7 31.1 %copy-start.7 = (bf16[16,8,1024]{2,1,0:T(8,128)(2,1)}, bf16[16,8,1024]{2,1,0:T(8,128)(2,1)S(1)}, u32[]{:S(2)}) copy-start(bf16[16,8,1024]{2,1,0:T(8,128)(2,1)S(1)} %collective-permute-done.6.refs_7_) | copy-start | bytes 786436
  48.7 21.0 %collective-permute-start.1 = (bf16[16,8,1024]{2,1,0:T(8,128)(2,1)}, bf16[16,8,1024]{2,1,0:T(8,128)(2,1)}, u32[]{:S(2)}, u32[]{:S(2)}) collective-permute-start(bf16[16,8,1024]{2,1,0:T(8,128)(2,1)} %get-tuple-element.55), channel_id=1, source_target_pairs={{0,128},{4,132},{8,136},{12,140},{16,144},{20,148},{24,152},{28,15... | collective-permute-start | bytes 786440 | tf_op jit(solution)/shard_map/ppermute | solution.py:372
  61.1 18.7 %copy-start.8 = (bf16[16,8,1024]{2,1,0:T(8,128)(2,1)}, bf16[16,8,1024]{2,1,0:T(8,128)(2,1)S(1)}, u32[]{:S(2)}) copy-start(bf16[16,8,1024]{2,1,0:T(8,128)(2,1)S(1)} %collective-permute-done.5.refs_6_) | copy-start | bytes 786436
  61.1 8.6 %collective-permute-start = (bf16[16,8,1024]{2,1,0:T(8,128)(2,1)}, bf16[16,8,1024]{2,1,0:T(8,128)(2,1)}, u32[]{:S(2)}, u32[]{:S(2)}) collective-permute-start(bf16[16,8,1024]{2,1,0:T(8,128)(2,1)} %get-tuple-element.56), channel_id=1, source_target_pairs={{0,4},{4,0},{8,12},{12,8},{16,20},{20,16},{24,28},{28,24},{32,36},... | collective-permute-start | bytes 786440 | tf_op jit(solution)/shard_map/ppermute | solution.py:372
  67.2 16.7 %copy-start.9 = (bf16[16,8,1024]{2,1,0:T(8,128)(2,1)}, bf16[16,8,1024]{2,1,0:T(8,128)(2,1)S(1)}, u32[]{:S(2)}) copy-start(bf16[16,8,1024]{2,1,0:T(8,128)(2,1)S(1)} %collective-permute-done.4.refs_5_) | copy-start | bytes 786436
  67.2 12.7 %copy-start.10 = (bf16[16,8,1024]{2,1,0:T(8,128)(2,1)}, bf16[16,8,1024]{2,1,0:T(8,128)(2,1)S(1)}, u32[]{:S(2)}) copy-start(bf16[16,8,1024]{2,1,0:T(8,128)(2,1)S(1)} %collective-permute-done.3.refs_4_) | copy-start | bytes 786436
  67.2 12.7 %copy-start.11 = (bf16[16,8,1024]{2,1,0:T(8,128)(2,1)}, bf16[16,8,1024]{2,1,0:T(8,128)(2,1)S(1)}, u32[]{:S(2)}) copy-start(bf16[16,8,1024]{2,1,0:T(8,128)(2,1)S(1)} %collective-permute-done.2.refs_3_) | copy-start | bytes 786436
  79.9 11.5 %all-to-all-start.1 = ((bf16[4,144,512]{2,1,0:T(8,128)(2,1)}), bf16[4,144,512]{2,1,0:T(8,128)(2,1)S(1)}, u32[]{:S(2)}, u32[]{:S(2)}) async-start(bf16[4,144,512]{2,1,0:T(8,128)(2,1)} %bitcast.9), calls=%async_computation.1 | async-start | bytes 1179648 | tf_op jit(solution)/shard_map/all_to_all | solution.py:426
  88.8 46.8 %copy-start = (bf16[1024,1024]{1,0:T(8,128)(2,1)S(1)}, bf16[1024,1024]{1,0:T(8,128)(2,1)}, u32[]{:S(2)}) copy-start(bf16[1024,1024]{1,0:T(8,128)(2,1)} %shard_map.135.turned_ref) | copy-start | bytes 6291460

commit v7 on v6

--- a/solution.py
+++ b/solution.py
@@ -75,6 +75,8 @@
     feature_ref,
     index_ref,
     sems,
+    *,
+    pack_slots,
 ):
     moves = [
         pltpu.make_async_copy(source, target, sems.at[i])
@@ -92,7 +94,7 @@
         move.start()
     cameras = pack_ref.shape[1]
     rows, channels = key_ref.shape
-    slots = owner_ref.shape[1]
+    slots = pack_slots
     owners, quarter, _ = lane_ref.shape
     groups, width = cams_ref.shape
     spd = groups * width // owners
@@ -104,14 +106,16 @@
         counts = cams_ref[g : g + 1, :].astype(F32)
         before += jnp.where(iota((owners, width), 1) + g * width < first, counts, 0.0)
     start = jnp.sum(before, axis=1, keepdims=True)
+    start = jnp.sum(
+        jnp.where(iota((owners, owners), 0) == iota((owners, owners), 1), start, 0.0), axis=0, keepdims=True
+    )
     moves[1].wait()
     here = (pack_ref[...] - bin_ref[0] * slots) == iota((slots, cameras), 0)
-    here = here.astype(F32).astype(BF16)
-    number = iota((16, cameras), 1)
-    digits = jnp.where(iota((16, cameras), 0) < 8, number // 64, number % 64)
-    digits = dot(digits.astype(F32).astype(BF16), here, 1, 1)
-    camera = digits[:1] * 64.0 + digits[8:9]
-    owner = jnp.sum((start <= camera).astype(F32), axis=0, keepdims=True) - 1.0
+    number = iota((1, cameras), 1).astype(F32)
+    camera = jnp.sum(jnp.where(here, number, 0.0), axis=1, keepdims=True)
+    owner = jnp.sum((start <= camera).astype(F32), axis=1, keepdims=True) - 1.0
+    across = (slots, owner_ref.shape[1])
+    owner = jnp.sum(jnp.where(iota(across, 0) == iota(across, 1), owner, 0.0), axis=0, keepdims=True)
     owner_ref[...] = jnp.broadcast_to(owner, owner_ref.shape).astype(I32)
     index = pltpu.make_async_copy(owner_ref, index_ref, sems.at[5])
     index.start()
@@ -308,10 +312,10 @@
     rows = slots * quarter
     flat_images = images.reshape(rows, depth)
     lanes, owner = call(
-        pack_kernel,
+        functools.partial(pack_kernel, pack_slots=slots),
         (
             jax.ShapeDtypeStruct((owners, quarter, 2 * channels), BF16),
-            jax.ShapeDtypeStruct((8, slots), I32),
+            jax.ShapeDtypeStruct((8, 128), I32),
         ),
         owner_id[None],
         *(
@@ -332,7 +336,7 @@
             pltpu.VMEM((rows, channels), BF16),
             pltpu.VMEM((depth, channels), BF16),
             pltpu.VMEM((rows, channels), BF16),
-            pltpu.SMEM((8, slots), I32),
+            pltpu.SMEM((8, 128), I32),
             pltpu.SemaphoreType.DMA((6,)),
         ],
         pinned=False,
@@ -351,7 +355,7 @@
 
     ys, zs, cs = range(chips), range(deep), range(CORES)
     my_y, _, my_core = place_of(owner_id)
-    owner_y, owner_z, owner_core = place_of(owner[0])
+    owner_y, owner_z, owner_core = place_of(owner[0, :slots])
     column = (owner_y - my_y) % chips * CORES + (owner_core + my_core) % CORES
     dealt = call(
         deal_kernel,
@@ -426,20 +430,6 @@
     kv = lax.all_to_all(
         chosen_kv.reshape(bands, piece, 2 * channels), "mp", split_axis=0, concat_axis=0, tiled=True
     )
-    tokens = owners * quarter
-    turned = call(
-        functools.partial(turn_kernel, bands=bands, share=share),
-        pltpu.HBM((depth, tokens), BF16),
-        *pieces,
-        specs=[pl.BlockSpec(memory_space=pltpu.HBM)] * len(pieces),
-        scratch=[
-            pltpu.VMEM((deep, len(pieces), quarter, depth), BF16),
-            pltpu.VMEM((tokens // 128, depth, 128), F32),
-            pltpu.SemaphoreType.DMA((len(pieces),)),
-        ],
-        cost=cost,
-    )
-    kv, turned = lax.optimization_barrier((kv, turned))
     bev_out, grads = call(
         attention_kernel,
         (
@@ -465,6 +455,7 @@
         ],
     )
     grads = lax.all_to_all(grads, "mp", split_axis=0, concat_axis=0, tiled=True)
+    grads, pieces = lax.optimization_barrier((grads, pieces))
     back = call(
         return_kernel,
         on_chip((owners, quarter, channels), BF16),
@@ -480,6 +471,19 @@
         )
 
     columns = [[device(y, z, c) for z in zs] for y in ys for c in cs]
+    tokens = owners * quarter
+    turned = call(
+        functools.partial(turn_kernel, bands=bands, share=share),
+        on_chip((depth, tokens), BF16),
+        *pieces,
+        specs=[pl.BlockSpec(memory_space=pltpu.HBM)] * len(pieces),
+        scratch=[
+            pltpu.VMEM((deep, len(pieces), quarter, depth), BF16),
+            pltpu.VMEM((tokens // 128, depth, 128), F32),
+            pltpu.SemaphoreType.DMA((len(pieces),)),
+        ],
+        cost=cost,
+    )
     back = exchange(back.reshape(deep, tokens // deep, channels), "dp", columns)
     neck = call(
         functools.partial(neck_kernel, samples=cams.shape[0]),

time: 177 us -> 177 us (level)
  blocking collectives: 78.2 us -> 58.1 us
  waiting for transfers between devices: 24.2 us -> 41.5 us
  starting transfers between devices: 47.3 us -> 51.3 us
    all_to_all x3 -> x2, blocking collectives: 70.1 us -> 38.8 us  [exchange(): lax.all_to_all(part, axis, split_axis=0, concat_axis=0, tiled=True, axis_...]
    all_to_all x1, waiting for transfers between devices: 2.52 us -> 19.2 us  [exchange(): lax.all_to_all(part, axis, split_axis=0, concat_axis=0, tiled=True, axis_...]
    all_to_all x0 -> x1, blocking collectives: none -> 11.3 us  [on_device(): lax.all_to_all(chosen_kv.reshape(bands, piece, 2 * channels), 'mp', split...]
    all_to_all x1, starting transfers between devices: 4.03 us -> 8.66 us  [exchange(): lax.all_to_all(part, axis, split_axis=0, concat_axis=0, tiled=True, axis_...]
  transfers between devices with their start and end apart: 9 -> 9, of which waited for: 4 -> 5; matrix products, arithmetic and copies ran while one was open for 2% -> 2% of each run, Pallas kernels for 5% -> 4%
where the time goes in v7:
time: 177 us; the launch traced here: 176 us
  blocking collectives  58.1 us (33%)
  starting transfers between devices  51.3 us (29%)
  waiting for transfers between devices  41.5 us (23%)
  Pallas kernels  16.9 us (10%)
  between operations  3.02 us (2%)
  other arithmetic  2.86 us (2%)
  local copies, waits for them, and re-layouts  2.17 us (1%)
    all_to_all x2, blocking collectives, exchange(): lax.all_to_all(part, axis, split_axis=0, concat_axis=0, tiled=True, axis_...  38.8 us
    ppermute x7, starting transfers between devices, on_device(): pieces.append(lax.ppermute(dealt[p], 'dp', moves))  22.1 us
    all_to_all x1, starting transfers between devices, on_device(): got = lax.all_to_all(lanes, 'dp', split_axis=0, concat_axis=0, tiled=True)  20.6 us
    all_to_all x1, waiting for transfers between devices, exchange(): lax.all_to_all(part, axis, split_axis=0, concat_axis=0, tiled=True, axis_...  19.2 us
    pallas_call x8, Pallas kernels, call(): pl.pallas_call(body, out_shape=outs, in_specs=specs, out_specs=jax.tree.m...  16.9 us
    ppermute x7, waiting for transfers between devices, on_device(): pieces.append(lax.ppermute(dealt[p], 'dp', moves))  13.8 us
    all_to_all x1, blocking collectives, on_device(): lax.all_to_all(chosen_kv.reshape(bands, piece, 2 * channels), 'mp', split...  11.3 us
    all_to_all x1, starting transfers between devices, exchange(): lax.all_to_all(part, axis, split_axis=0, concat_axis=0, tiled=True, axis_...  8.66 us
  transfers between devices with their start and end apart: 9, of which 5 were waited for; matrix products, arithmetic and copies ran while one was open for 2% of the time, Pallas kernels for 4%

profile of v7, /device:TPU:1, one launch (start us, length us, event | category | flops | bytes accessed | tf_op | source)
XLA Modules:
  0.0 175.9 jit_solution(13378012683027204601)
XLA Ops:
  0.6 2.9 %shard_map.131 = (bf16[128,8,512]{2,1,0:T(8,128)(2,1)}, s32[8,128]{1,0:T(8,128)S(1)}) custom-call(s32[1]{0:T(128)} %bitcast.bin_ref, s32[6,128]{1,0:T(8,128)} %bitcast.43, s32[1,6144]{1,0:T(1,128)} %bitcast.42, bf16[384,1024]{1,0:T(8,128)(2,1)} %bitcast.37, bf16[384,256]{1,0:T(8,128)(2,1)} %bitcast.40, bf16[1024,256]{1,0:T(8,128)(2,1)} %weight_hbm.1), custom_call_target="tpu_custom_call" | custom-call | flops 1048576 | bytes 1048576 | tf_op jit(solution)/shard_map/pallas_call | solution.py:50
  3.5 20.6 %all-to-all-start = ((bf16[128,8,512]{2,1,0:T(8,128)(2,1)}), bf16[128,8,512]{2,1,0:T(8,128)(2,1)S(1)}, u32[]{:S(2)}, u32[]{:S(2)}) async-start(bf16[128,8,512]{2,1,0:T(8,128)(2,1)} %get-tuple-element.33), calls=%async_computation | async-start | bytes 2097152 | tf_op jit(solution)/shard_map/all_to_all | solution.py:344
  24.2 0.7 shard_map.133
  24.9 0.0 copy-start.13
  24.9 0.0 copy-start.11
  24.9 0.0 copy-start.14
  25.0 0.0 copy-start.3
  25.0 0.0 copy-start.4
  25.0 1.3 fusion.18
  26.3 2.8 %collective-permute-start = (bf16[16,8,1024]{2,1,0:T(8,128)(2,1)}, bf16[16,8,1024]{2,1,0:T(8,128)(2,1)S(1)}, u32[]{:S(2)}, u32[]{:S(2)}) collective-permute-start(bf16[16,8,1024]{2,1,0:T(8,128)(2,1)} %get-tuple-element.70), channel_id=1, source_target_pairs={{0,4},{4,0},{8,12},{12,8},{16,20},{20,16},{24,28},{28,24},{32,36},... | collective-permute-start | bytes 786440 | tf_op jit(solution)/shard_map/ppermute | solution.py:376
  29.1 2.9 %collective-permute-start.1 = (bf16[16,8,1024]{2,1,0:T(8,128)(2,1)}, bf16[16,8,1024]{2,1,0:T(8,128)(2,1)S(1)}, u32[]{:S(2)}, u32[]{:S(2)}) collective-permute-start(bf16[16,8,1024]{2,1,0:T(8,128)(2,1)} %get-tuple-element.69), channel_id=1, source_target_pairs={{0,128},{4,132},{8,136},{12,140},{16,144},{20,148},{24,152},{28,15... | collective-permute-start | bytes 786440 | tf_op jit(solution)/shard_map/ppermute | solution.py:376
  32.0 3.6 %collective-permute-start.2 = (bf16[16,8,1024]{2,1,0:T(8,128)(2,1)}, bf16[16,8,1024]{2,1,0:T(8,128)(2,1)S(1)}, u32[]{:S(2)}, u32[]{:S(2)}) collective-permute-start(bf16[16,8,1024]{2,1,0:T(8,128)(2,1)} %get-tuple-element.68), channel_id=1, source_target_pairs={{0,132},{4,128},{8,140},{12,136},{16,148},{20,144},{24,156},{28,15... | collective-permute-start | bytes 786440 | tf_op jit(solution)/shard_map/ppermute | solution.py:376
  35.7 3.3 %collective-permute-start.3 = (bf16[16,8,1024]{2,1,0:T(8,128)(2,1)}, bf16[16,8,1024]{2,1,0:T(8,128)(2,1)S(1)}, u32[]{:S(2)}, u32[]{:S(2)}) collective-permute-start(bf16[16,8,1024]{2,1,0:T(8,128)(2,1)} %get-tuple-element.67), channel_id=1, source_target_pairs={{0,256},{4,260},{8,264},{12,268},{16,272},{20,276},{24,280},{28,28... | collective-permute-start | bytes 786440 | tf_op jit(solution)/shard_map/ppermute | solution.py:376
  38.9 3.8 %collective-permute-start.4 = (bf16[16,8,1024]{2,1,0:T(8,128)(2,1)}, bf16[16,8,1024]{2,1,0:T(8,128)(2,1)S(1)}, u32[]{:S(2)}, u32[]{:S(2)}) collective-permute-start(bf16[16,8,1024]{2,1,0:T(8,128)(2,1)} %get-tuple-element.66), channel_id=1, source_target_pairs={{0,260},{4,256},{8,268},{12,264},{16,276},{20,272},{24,284},{28,28... | collective-permute-start | bytes 786440 | tf_op jit(solution)/shard_map/ppermute | solution.py:376
  42.7 0.6 select_reduce_fusion.2
  44.6 0.1 dynamic_slice.9
  44.7 0.1 copy.28
  45.5 0.1 fusion.16
  45.6 0.1 select_reduce_fusion.3
  45.7 0.1 multiply_reduce_fusion
  45.9 0.1 add_add_fusion
  46.0 0.4 select_reduce_fusion.1
  46.4 0.5 select_reduce_fusion
  46.8 0.2 fusion.17
  47.0 0.1 copy.27.point_ref
  47.2 3.2 %collective-permute-start.5 = (bf16[16,8,1024]{2,1,0:T(8,128)(2,1)}, bf16[16,8,1024]{2,1,0:T(8,128)(2,1)}, u32[]{:S(2)}, u32[]{:S(2)}) collective-permute-start(bf16[16,8,1024]{2,1,0:T(8,128)(2,1)} %get-tuple-element.65), channel_id=1, source_target_pairs={{0,384},{4,388},{8,392},{12,396},{16,400},{20,404},{24,408},{28,41... | collective-permute-start | bytes 786440 | tf_op jit(solution)/shard_map/ppermute | solution.py:376
  50.4 2.6 %collective-permute-start.6 = (bf16[16,8,1024]{2,1,0:T(8,128)(2,1)}, bf16[16,8,1024]{2,1,0:T(8,128)(2,1)}, u32[]{:S(2)}, u32[]{:S(2)}) collective-permute-start(bf16[16,8,1024]{2,1,0:T(8,128)(2,1)} %get-tuple-element.64), channel_id=1, source_target_pairs={{0,388},{4,384},{8,396},{12,392},{16,404},{20,400},{24,412},{28,40... | collective-permute-start | bytes 786440 | tf_op jit(solution)/shard_map/ppermute | solution.py:376
  53.0 2.7 %shard_map.132 = (f32[6,128,256]{2,1,0:T(8,128)}, f32[6,128,256]{2,1,0:T(8,128)}, f32[1,256]{1,0:T(1,128)S(1)}) custom-call(s32[1]{0:T(128)} %bitcast.5.band_ref, bf16[128,256]{1,0:T(8,128)(2,1)S(1)} %copy-done.1, bf16[256,32]{1,0:T(8,128)(2,1)S(1)} %copy.27.point_ref, bf16[6,128,256]{2,1,0:T(8,128)(2,1)S(1)} %copy-done.2, s32[6,4,128]{2,1,0:T(4,128)S(1)} %copy-done.4, ...), custom_call_target="tpu_custom_call" | custom-call | flops 1073741824 | bytes 4194304 | tf_op jit(solution)/shard_map/pallas_call | solution.py:50
  55.7 0.1 copy.29
  55.9 0.1 max.17.source_ref
  56.0 0.2 dynamic-slice_reduce_fusion.count_ref
  56.2 1.6 collective-permute-done.3.refs_4_
  57.8 8.0 %collective-permute-done.4.refs_5_ = bf16[16,8,1024]{2,1,0:T(8,128)(2,1)S(1)} collective-permute-done((bf16[16,8,1024]{2,1,0:T(8,128)(2,1)}, bf16[16,8,1024]{2,1,0:T(8,128)(2,1)S(1)}, u32[]{:S(2)}, u32[]{:S(2)}) %collective-permute-start.4) | collective-permute-done | bytes 262176 | tf_op jit(solution)/shard_map/ppermute | solution.py:376
  65.8 4.1 %collective-permute-done.6.refs_7_ = bf16[16,8,1024]{2,1,0:T(8,128)(2,1)} collective-permute-done((bf16[16,8,1024]{2,1,0:T(8,128)(2,1)}, bf16[16,8,1024]{2,1,0:T(8,128)(2,1)}, u32[]{:S(2)}, u32[]{:S(2)}) %collective-permute-start.6) | collective-permute-done | bytes 262176 | tf_op jit(solution)/shard_map/ppermute | solution.py:376
  70.0 8.5 %all-to-all-done.lane_ref = bf16[128,8,512]{2,1,0:T(8,128)(2,1)S(1)} async-done(((bf16[128,8,512]{2,1,0:T(8,128)(2,1)}), bf16[128,8,512]{2,1,0:T(8,128)(2,1)S(1)}, u32[]{:S(2)}, u32[]{:S(2)}) %all-to-all-start) | async-done | bytes 1048608 | tf_op jit(solution)/shard_map/all_to_all | solution.py:344
  78.5 0.6 shard_map.134
  79.1 11.3 %all_to_all.30.kv_ref = bf16[4,144,512]{2,1,0:T(8,128)(2,1)S(1)} all-to-all(bf16[4,144,512]{2,1,0:T(8,128)(2,1)S(1)} %bitcast.33), channel_id=1, replica_groups=mesh['dp'=128,'mp'=4] {'mp'}, dimensions={0} | all-to-all | bytes 1179648 | tf_op jit(solution)/shard_map/all_to_all | solution.py:430
  90.4 3.9 %shard_map.135 = (bf16[6,128,256]{2,1,0:T(8,128)(2,1)}, bf16[4,144,256]{2,1,0:T(8,128)(2,1)S(1)}) custom-call(s32[6]{0:T(128)S(1)} %dynamic-slice_reduce_fusion.count_ref, bf16[4,144,512]{2,1,0:T(8,128)(2,1)S(1)} %all_to_all.30.kv_ref, f32[6,128,256]{2,1,0:T(8,128)} %get-tuple-element.41.base_hbm, f32[6,128,256]{2,1,0:T(8,128)} %get-tuple-element.42.pull_hbm, ...), custom_call_target="tpu_custom_call" | custom-call | flops 1048576 | bytes 1048576 | tf_op jit(solution)/shard_map/pallas_call | solution.py:50
  94.3 8.1 %all_to_all.31 = bf16[4,144,256]{2,1,0:T(8,128)(2,1)S(1)} all-to-all(bf16[4,144,256]{2,1,0:T(8,128)(2,1)S(1)} %get-tuple-element.46), channel_id=1, replica_groups=mesh['dp'=128,'mp'=4] {'mp'}, dimensions={0} | all-to-all | bytes 589824 | tf_op jit(solution)/shard_map/all_to_all | solution.py:457
  102.4 1.8 %shard_map.136 = bf16[128,8,256]{2,1,0:T(8,128)(2,1)} custom-call(s32[72]{0:T(128)S(1)} %fusion.5.source_ref, bf16[72,8,256]{2,1,0:T(8,128)(2,1)S(1)} %bitcast.36), custom_call_target="tpu_custom_call" | custom-call | flops 1048576 | bytes 1048576 | tf_op jit(solution)/shard_map/pallas_call | solution.py:50
  104.2 8.7 %all-to-all-start.3 = ((bf16[16,64,256]{2,1,0:T(8,128)(2,1)}), bf16[16,64,256]{2,1,0:T(8,128)(2,1)S(1)}, u32[]{:S(2)}, u32[]{:S(2)}) async-start(bf16[16,64,256]{2,1,0:T(8,128)(2,1)} %bitcast.11), calls=%async_computation.3 | async-start | bytes 1048576 | tf_op jit(solution)/shard_map/all_to_all | solution.py:469
  112.8 3.6 %shard_map.137.turned_ref = bf16[1024,1024]{1,0:T(8,128)(2,1)S(1)} custom-call(bf16[16,8,1024]{2,1,0:T(8,128)(2,1)} %get-tuple-element.56.refs_0_, bf16[16,8,1024]{2,1,0:T(8,128)(2,1)} %copy-done.6, bf16[16,8,1024]{2,1,0:T(8,128)(2,1)} %copy-done.7, bf16[16,8,1024]{2,1,0:T(8,128)(2,1)} %copy-done.8, bf16[16,8,1024]{2,1,0:T(8,128)(2,1)} %copy-done.9, ...), custom_call_target="tpu_custom_call" | custom-call | flops 1073741824 | bytes 4194304 | tf_op jit(solution)/shard_map/pallas_call | solution.py:50
  116.4 19.2 %all-to-all-done.3 = bf16[16,64,256]{2,1,0:T(8,128)(2,1)S(1)} async-done(((bf16[16,64,256]{2,1,0:T(8,128)(2,1)}), bf16[16,64,256]{2,1,0:T(8,128)(2,1)S(1)}, u32[]{:S(2)}, u32[]{:S(2)}) %all-to-all-start.3) | async-done | bytes 524320 | tf_op jit(solution)/shard_map/all_to_all | solution.py:469
  135.7 0.7 shard_map.138
  136.4 21.1 %all_to_all.32 = bf16[32,32,256]{2,1,0:T(8,128)(2,1)S(1)} all-to-all(bf16[32,32,256]{2,1,0:T(8,128)(2,1)S(1)} %bitcast.35), channel_id=1, replica_groups={{0,1,2,3,4,5,6,7,128,129,130,131,132,133,134,135,256,257,258,259,260,26..., dimensions={0} | all-to-all | bytes 1048576 | tf_op jit(solution)/shard_map/all_to_all | solution.py:469
  157.5 0.1 convert_reduce_fusion
  157.6 17.7 %all_to_all.33 = f32[16,2,256]{2,1,0:T(2,128)S(1)} all-to-all(f32[16,2,256]{2,1,0:T(2,128)S(1)} %copy.30), channel_id=1, replica_groups={{0,8,16,24,32,40,48,56,64,72,80,88,96,104,112,120},{4,12,20,28,36,44,52..., dimensions={0} | all-to-all | bytes 65536 | tf_op jit(solution)/shard_map/all_to_all | solution.py:469
  175.3 0.6 reduce_sum.79
  (36 shorter events, 0.2 us)
Async XLA Ops:
  0.6 23.5 %copy-start = (bf16[48,8,1024]{2,1,0:T(8,128)(2,1)S(1)}, bf16[48,8,1024]{2,1,0:T(8,128)(2,1)}, u32[]{:S(2)}) copy-start(bf16[48,8,1024]{2,1,0:T(8,128)(2,1)} %param.16) | copy-start | bytes 2359300
  3.5 74.9 %all-to-all-start = ((bf16[128,8,512]{2,1,0:T(8,128)(2,1)}), bf16[128,8,512]{2,1,0:T(8,128)(2,1)S(1)}, u32[]{:S(2)}, u32[]{:S(2)}) async-start(bf16[128,8,512]{2,1,0:T(8,128)(2,1)} %get-tuple-element.33), calls=%async_computation | async-start | bytes 2097152 | tf_op jit(solution)/shard_map/all_to_all | solution.py:344
  24.9 17.8 %copy-start.13 = (s32[768]{0:T(1024)S(1)}, s32[768]{0:T(1024)}, u32[]{:S(2)}) copy-start(s32[768]{0:T(1024)} %param.12) | copy-start | bytes 9220
  24.9 19.8 %copy-start.12 = (s32[6,11,4]{1,2,0:T(4,128)S(1)}, s32[6,11,4]{1,2,0:T(4,128)}, u32[]{:S(2)}) copy-start(s32[6,11,4]{1,2,0:T(4,128)} %param.14) | copy-start | bytes 3172
  24.9 20.6 %copy-start.11 = (s32[6144]{0:T(1024)S(1)}, s32[6144]{0:T(1024)}, u32[]{:S(2)}) copy-start(s32[6144]{0:T(1024)} %param.13) | copy-start | bytes 73732
  24.9 22.1 %copy-start.14 = (bf16[256,32]{0,1:T(8,128)(2,1)S(1)}, bf16[256,32]{0,1:T(8,128)(2,1)}, u32[]{:S(2)}) copy-start(bf16[256,32]{0,1:T(8,128)(2,1)} %param.21) | copy-start | bytes 49156
  25.0 28.0 %copy-start.1 = (bf16[128,256]{1,0:T(8,128)(2,1)S(1)}, bf16[128,256]{1,0:T(8,128)(2,1)}, u32[]{:S(2)}) copy-start(bf16[128,256]{1,0:T(8,128)(2,1)} %query_ref.3) | copy-start | bytes 196612
  25.0 28.0 %copy-start.2 = (bf16[6,128,256]{2,1,0:T(8,128)(2,1)S(1)}, bf16[6,128,256]{2,1,0:T(8,128)(2,1)}, u32[]{:S(2)}) copy-start(bf16[6,128,256]{2,1,0:T(8,128)(2,1)} %prev_ref.1) | copy-start | bytes 1179652
  25.0 28.0 %copy-start.3 = (bf16[6,128,256]{2,1,0:T(8,128)(2,1)S(1)}, bf16[6,128,256]{2,1,0:T(8,128)(2,1)}, u32[]{:S(2)}) copy-start(bf16[6,128,256]{2,1,0:T(8,128)(2,1)} %cotangent_ref.1) | copy-start | bytes 1179652
  25.0 28.0 %copy-start.4 = (s32[6,4,128]{2,1,0:T(4,128)S(1)}, s32[6,4,128]{2,1,0:T(4,128)}, u32[]{:S(2)}) copy-start(s32[6,4,128]{2,1,0:T(4,128)} %align_ref.1) | copy-start | bytes 36868
  25.0 28.0 %copy-start.5 = (f32[256]{0:T(256)S(1)}, f32[256]{0:T(256)}, u32[]{:S(2)}) copy-start(f32[256]{0:T(256)} %param.22) | copy-start | bytes 3076
  26.3 20.8 %collective-permute-start = (bf16[16,8,1024]{2,1,0:T(8,128)(2,1)}, bf16[16,8,1024]{2,1,0:T(8,128)(2,1)S(1)}, u32[]{:S(2)}, u32[]{:S(2)}) collective-permute-start(bf16[16,8,1024]{2,1,0:T(8,128)(2,1)} %get-tuple-element.70), channel_id=1, source_target_pairs={{0,4},{4,0},{8,12},{12,8},{16,20},{20,16},{24,28},{28,24},{32,36},... | collective-permute-start | bytes 786440 | tf_op jit(solution)/shard_map/ppermute | solution.py:376
  29.1 21.2 %collective-permute-start.1 = (bf16[16,8,1024]{2,1,0:T(8,128)(2,1)}, bf16[16,8,1024]{2,1,0:T(8,128)(2,1)S(1)}, u32[]{:S(2)}, u32[]{:S(2)}) collective-permute-start(bf16[16,8,1024]{2,1,0:T(8,128)(2,1)} %get-tuple-element.69), channel_id=1, source_target_pairs={{0,128},{4,132},{8,136},{12,140},{16,144},{20,148},{24,152},{28,15... | collective-permute-start | bytes 786440 | tf_op jit(solution)/shard_map/ppermute | solution.py:376
  32.0 24.2 %collective-permute-start.2 = (bf16[16,8,1024]{2,1,0:T(8,128)(2,1)}, bf16[16,8,1024]{2,1,0:T(8,128)(2,1)S(1)}, u32[]{:S(2)}, u32[]{:S(2)}) collective-permute-start(bf16[16,8,1024]{2,1,0:T(8,128)(2,1)} %get-tuple-element.68), channel_id=1, source_target_pairs={{0,132},{4,128},{8,140},{12,136},{16,148},{20,144},{24,156},{28,15... | collective-permute-start | bytes 786440 | tf_op jit(solution)/shard_map/ppermute | solution.py:376
  35.7 22.2 %collective-permute-start.3 = (bf16[16,8,1024]{2,1,0:T(8,128)(2,1)}, bf16[16,8,1024]{2,1,0:T(8,128)(2,1)S(1)}, u32[]{:S(2)}, u32[]{:S(2)}) collective-permute-start(bf16[16,8,1024]{2,1,0:T(8,128)(2,1)} %get-tuple-element.67), channel_id=1, source_target_pairs={{0,256},{4,260},{8,264},{12,268},{16,272},{20,276},{24,280},{28,28... | collective-permute-start | bytes 786440 | tf_op jit(solution)/shard_map/ppermute | solution.py:376
  38.9 26.9 %collective-permute-start.4 = (bf16[16,8,1024]{2,1,0:T(8,128)(2,1)}, bf16[16,8,1024]{2,1,0:T(8,128)(2,1)S(1)}, u32[]{:S(2)}, u32[]{:S(2)}) collective-permute-start(bf16[16,8,1024]{2,1,0:T(8,128)(2,1)} %get-tuple-element.66), channel_id=1, source_target_pairs={{0,260},{4,256},{8,268},{12,264},{16,276},{20,272},{24,284},{28,28... | collective-permute-start | bytes 786440 | tf_op jit(solution)/shard_map/ppermute | solution.py:376
  47.2 31.9 %copy-start.6 = (bf16[16,8,1024]{2,1,0:T(8,128)(2,1)}, bf16[16,8,1024]{2,1,0:T(8,128)(2,1)S(1)}, u32[]{:S(2)}) copy-start(bf16[16,8,1024]{2,1,0:T(8,128)(2,1)S(1)} %collective-permute-done.refs_1_) | copy-start | bytes 786436
  47.2 18.7 %collective-permute-start.5 = (bf16[16,8,1024]{2,1,0:T(8,128)(2,1)}, bf16[16,8,1024]{2,1,0:T(8,128)(2,1)}, u32[]{:S(2)}, u32[]{:S(2)}) collective-permute-start(bf16[16,8,1024]{2,1,0:T(8,128)(2,1)} %get-tuple-element.65), channel_id=1, source_target_pairs={{0,384},{4,388},{8,392},{12,396},{16,400},{20,404},{24,408},{28,41... | collective-permute-start | bytes 786440 | tf_op jit(solution)/shard_map/ppermute | solution.py:376
  50.4 28.7 %copy-start.7 = (bf16[16,8,1024]{2,1,0:T(8,128)(2,1)}, bf16[16,8,1024]{2,1,0:T(8,128)(2,1)S(1)}, u32[]{:S(2)}) copy-start(bf16[16,8,1024]{2,1,0:T(8,128)(2,1)S(1)} %collective-permute-done.1.refs_2_) | copy-start | bytes 786436
  50.4 19.6 %collective-permute-start.6 = (bf16[16,8,1024]{2,1,0:T(8,128)(2,1)}, bf16[16,8,1024]{2,1,0:T(8,128)(2,1)}, u32[]{:S(2)}, u32[]{:S(2)}) collective-permute-start(bf16[16,8,1024]{2,1,0:T(8,128)(2,1)} %get-tuple-element.64), channel_id=1, source_target_pairs={{0,388},{4,384},{8,396},{12,392},{16,404},{20,400},{24,412},{28,40... | collective-permute-start | bytes 786440 | tf_op jit(solution)/shard_map/ppermute | solution.py:376
  56.2 38.1 %copy-start.8 = (bf16[16,8,1024]{2,1,0:T(8,128)(2,1)}, bf16[16,8,1024]{2,1,0:T(8,128)(2,1)S(1)}, u32[]{:S(2)}) copy-start(bf16[16,8,1024]{2,1,0:T(8,128)(2,1)S(1)} %collective-permute-done.2.refs_3_) | copy-start | bytes 786436
  57.8 36.5 %copy-start.9 = (bf16[16,8,1024]{2,1,0:T(8,128)(2,1)}, bf16[16,8,1024]{2,1,0:T(8,128)(2,1)S(1)}, u32[]{:S(2)}) copy-start(bf16[16,8,1024]{2,1,0:T(8,128)(2,1)S(1)} %collective-permute-done.3.refs_4_) | copy-start | bytes 786436
  65.8 28.5 %copy-start.10 = (bf16[16,8,1024]{2,1,0:T(8,128)(2,1)}, bf16[16,8,1024]{2,1,0:T(8,128)(2,1)S(1)}, u32[]{:S(2)}) copy-start(bf16[16,8,1024]{2,1,0:T(8,128)(2,1)S(1)} %collective-permute-done.4.refs_5_) | copy-start | bytes 786436
  104.2 31.5 %all-to-all-start.3 = ((bf16[16,64,256]{2,1,0:T(8,128)(2,1)}), bf16[16,64,256]{2,1,0:T(8,128)(2,1)S(1)}, u32[]{:S(2)}, u32[]{:S(2)}) async-start(bf16[16,64,256]{2,1,0:T(8,128)(2,1)} %bitcast.11), calls=%async_computation.3 | async-start | bytes 1048576 | tf_op jit(solution)/shard_map/all_to_all | solution.py:469

commit v8 on v7

--- a/solution.py
+++ b/solution.py
@@ -98,7 +98,6 @@
     owners, quarter, _ = lane_ref.shape
     groups, width = cams_ref.shape
     spd = groups * width // owners
-    lane_ref[...] = jnp.zeros(lane_ref.shape, BF16)
     moves[0].wait()
     first = iota((owners, width), 0) * spd
     before = jnp.zeros((owners, width), F32)
@@ -175,6 +174,7 @@
     gain_ref,
     base_ref,
     pull_ref,
+    heads_ref,
     scale_ref,
 ):
     samples, cells, channels = prev_ref.shape
@@ -183,6 +183,9 @@
     wide = query.astype(F32)
     gain = gain_ref[...]
     scale_ref[...] = gain
+    for h in range(HEADS):
+        mask = (iota((1, channels), 1) // head_dim == h).astype(F32).astype(BF16)
+        heads_ref[h * cells : (h + 1) * cells, :] = query * mask
     gates = []
     for k in range(KT):
         shape = (HEADS * KT, channels)
@@ -208,27 +211,21 @@
 def attention_kernel(
     count_ref,
     kv_ref,
-    base_hbm,
+    base_ref,
     pull_hbm,
-    query_ref,
+    heads_ref,
     gain_ref,
     out_ref,
     grad_ref,
-    base_ref,
     pull_ref,
-    sems,
-    heads_ref,
+    sem,
     score_ref,
     prob_ref,
     norm_ref,
     cross_ref,
 ):
-    moves = [
-        pltpu.make_async_copy(base_hbm, base_ref, sems.at[0]),
-        pltpu.make_async_copy(pull_hbm, pull_ref, sems.at[1]),
-    ]
-    for move in moves:
-        move.start()
+    move = pltpu.make_async_copy(pull_hbm, pull_ref, sem)
+    move.start()
     parts, rows, width = kv_ref.shape
     samples, queries, channels = base_ref.shape
     step = rows // samples
@@ -240,8 +237,6 @@
     masks = [(lane_head == h).astype(F32).astype(BF16) for h in range(HEADS)]
     factor = float(head_dim) ** -0.5 * LOG2_E
     place = iota((keys, HEADS * queries), 0) % step // quarter
-    for h in range(HEADS):
-        heads_ref[h * queries : (h + 1) * queries, :] = query_ref[...] * masks[h]
     spans = [slice(m * step, (m + 1) * step) for m in range(samples)]
     ray = kv_ref[:, :, channels:].reshape(parts * rows, channels)
     score_ref[...] = dot(ray, heads_ref[...], 1, 1).reshape(score_ref.shape)
@@ -250,7 +245,6 @@
         scores = jnp.where(place < count_ref[m], scores, MASKED)
         raised = jnp.exp2((scores - jnp.max(scores, axis=0, keepdims=True)) * factor)
         prob_ref[m] = (raised * (1.0 / jnp.sum(raised, axis=0, keepdims=True))).astype(BF16)
-    moves[0].wait()
     for m in range(samples):
         values = kv_ref[:, spans[m], :channels].reshape(keys, channels)
         values = jnp.concatenate([values * mask for mask in masks], axis=0)
@@ -259,7 +253,7 @@
             [probs[:, h * queries : (h + 1) * queries] for h in range(HEADS)], axis=0
         )
         norm_ref[m] = base_ref[m] + dot(tall, values, 0, 0)
-    moves[1].wait()
+    move.wait()
     for m in range(samples):
         pre_norm = norm_ref[m]
         centred = pre_norm - jnp.mean(pre_norm, axis=1, keepdims=True)
@@ -374,11 +368,12 @@
             for c in cs
         ]
         pieces.append(lax.ppermute(dealt[p], "dp", moves))
-    base, pull, gain = call(
+    base, pull, heads, gain = call(
         temporal_kernel,
         (
+            on_chip((samples, queries, channels), F32),
             pltpu.HBM((samples, queries, channels), F32),
-            pltpu.HBM((samples, queries, channels), F32),
+            on_chip((HEADS * queries, channels), BF16),
             on_chip((1, channels), F32),
         ),
         band_id[None],
@@ -411,13 +406,14 @@
     )
     in_window = position[..., None] == jnp.arange(1, window + 1, dtype=I32)
     lane_of = jnp.sum(jnp.where(in_window, bins + 1, 0), axis=-1) - 1
+    lane_of = jnp.where(lane_of >= 0, lane_of, lane_of[:, :, :1])
     lane_of = lane_of.transpose(1, 0, 2).reshape(bands * samples * SEEN)
     count = lax.dynamic_slice_in_dim(jnp.sum(seen, axis=1), band_id, 1, axis=1)[:, 0]
     source = jnp.maximum(lane_of, 0)
     bin_y, bin_z, bin_core = place_of(source)
     back_lane = (bin_z * chips + (my_y - bin_y) % chips) * CORES + (bin_core + my_core) % CORES
-    got, base, pull, gain, pieces, source, back_lane, count = lax.optimization_barrier(
-        (got, base, pull, gain, pieces, source, back_lane, count)
+    got, base, pull, heads, gain, pieces, source, back_lane, count = lax.optimization_barrier(
+        (got, base, pull, heads, gain, pieces, source, back_lane, count)
     )
     piece = samples * SEEN * quarter
     chosen_kv = call(
@@ -440,37 +436,20 @@
         kv,
         base,
         pull,
-        bev_query,
+        heads,
         gain,
-        specs=[smem(), vmem()] + [pl.BlockSpec(memory_space=pltpu.HBM)] * 2 + [vmem()] * 2,
+        specs=[smem(), vmem(), vmem(), pl.BlockSpec(memory_space=pltpu.HBM), vmem(), vmem()],
         scratch=[
             pltpu.VMEM((samples, queries, channels), F32),
-            pltpu.VMEM((samples, queries, channels), F32),
-            pltpu.SemaphoreType.DMA((2,)),
-            pltpu.VMEM((HEADS * queries, channels), BF16),
+            pltpu.SemaphoreType.DMA,
             pltpu.VMEM((bands, piece, HEADS * queries), F32),
             pltpu.VMEM((samples, bands * SEEN * quarter, HEADS * queries), BF16),
             pltpu.VMEM((samples, queries, channels), F32),
             pltpu.VMEM((samples, queries, channels), BF16),
         ],
     )
+    grads, pieces = lax.optimization_barrier((grads, pieces))
     grads = lax.all_to_all(grads, "mp", split_axis=0, concat_axis=0, tiled=True)
-    grads, pieces = lax.optimization_barrier((grads, pieces))
-    back = call(
-        return_kernel,
-        on_chip((owners, quarter, channels), BF16),
-        back_lane,
-        grads.reshape(bands * samples * SEEN, quarter, channels),
-        specs=[smem(), vmem()],
-        scratch=[pltpu.VMEM((owners, quarter, channels), F32)],
-    )
-
-    def exchange(part, axis, groups):
-        return lax.all_to_all(
-            part, axis, split_axis=0, concat_axis=0, tiled=True, axis_index_groups=groups
-        )
-
-    columns = [[device(y, z, c) for z in zs] for y in ys for c in cs]
     tokens = owners * quarter
     turned = call(
         functools.partial(turn_kernel, bands=bands, share=share),
@@ -484,6 +463,22 @@
         ],
         cost=cost,
     )
+    grads, turned = lax.optimization_barrier((grads, turned))
+    back = call(
+        return_kernel,
+        on_chip((owners, quarter, channels), BF16),
+        back_lane,
+        grads.reshape(bands * samples * SEEN, quarter, channels),
+        specs=[smem(), vmem()],
+        scratch=[pltpu.VMEM((owners, quarter, channels), F32)],
+    )
+
+    def exchange(part, axis, groups):
+        return lax.all_to_all(
+            part, axis, split_axis=0, concat_axis=0, tiled=True, axis_index_groups=groups
+        )
+
+    columns = [[device(y, z, c) for z in zs] for y in ys for c in cs]
     back = exchange(back.reshape(deep, tokens // deep, channels), "dp", columns)
     neck = call(
         functools.partial(neck_kernel, samples=cams.shape[0]),

time: 177 us -> 176 us (level)
  blocking collectives: 58.1 us -> 81.3 us
  waiting for transfers between devices: 41.5 us -> 24.5 us
  starting transfers between devices: 51.3 us -> 46.1 us
    all_to_all x2 -> x3, blocking collectives: 38.8 us -> 70 us  [exchange(): lax.all_to_all(part, axis, split_axis=0, concat_axis=0, tiled=True, axis_...]
    all_to_all x1, waiting for transfers between devices: 19.2 us -> 2.08 us  [on_device(): grads = lax.all_to_all(grads, 'mp', split_axis=0, concat_axis=0, tiled=True)]
    all_to_all x1 -> x0, blocking collectives: 8.07 us -> none  [on_device(): grads = lax.all_to_all(grads, 'mp', split_axis=0, concat_axis=0, tiled=True)]
    all_to_all x1, starting transfers between devices: 8.66 us -> 3.46 us  [on_device(): grads = lax.all_to_all(grads, 'mp', split_axis=0, concat_axis=0, tiled=True)]
where the time goes in v8:
time: 176 us
  blocking collectives  81.3 us (46%)
  starting transfers between devices  46.1 us (26%)
  waiting for transfers between devices  24.5 us (14%)
  Pallas kernels  15.8 us (9%)
  between operations  3 us (2%)
  other arithmetic  2.86 us (2%)
  local copies, waits for them, and re-layouts  2.18 us (1%)
    all_to_all x3, blocking collectives, exchange(): lax.all_to_all(part, axis, split_axis=0, concat_axis=0, tiled=True, axis_...  70 us
    ppermute x7, starting transfers between devices, on_device(): pieces.append(lax.ppermute(dealt[p], 'dp', moves))  22.1 us
    all_to_all x1, starting transfers between devices, on_device(): got = lax.all_to_all(lanes, 'dp', split_axis=0, concat_axis=0, tiled=True)  20.6 us
    pallas_call x8, Pallas kernels, call(): pl.pallas_call(body, out_shape=outs, in_specs=specs, out_specs=jax.tree.m...  15.8 us
    ppermute x7, waiting for transfers between devices, on_device(): pieces.append(lax.ppermute(dealt[p], 'dp', moves))  13.8 us
    all_to_all x1, blocking collectives, on_device(): lax.all_to_all(chosen_kv.reshape(bands, piece, 2 * channels), 'mp', split...  11.3 us
    all_to_all x1, waiting for transfers between devices, on_device(): got = lax.all_to_all(lanes, 'dp', split_axis=0, concat_axis=0, tiled=True)  8.64 us
  transfers between devices with their start and end apart: 9, of which 5 were waited for; matrix products, arithmetic and copies ran while one was open for 2% of the time, Pallas kernels for 4%

profile of v8, /device:TPU:1, one launch (start us, length us, event | category | flops | bytes accessed | tf_op | source)
XLA Modules:
  0.0 175.8 jit_solution(14167469074201049255)
XLA Ops:
  0.6 2.9 %shard_map.131 = (bf16[128,8,512]{2,1,0:T(8,128)(2,1)}, s32[8,128]{1,0:T(8,128)S(1)}) custom-call(s32[1]{0:T(128)} %bitcast.bin_ref, s32[6,128]{1,0:T(8,128)} %bitcast.47, s32[1,6144]{1,0:T(1,128)} %bitcast.46, bf16[384,1024]{1,0:T(8,128)(2,1)} %bitcast.41, bf16[384,256]{1,0:T(8,128)(2,1)} %bitcast.44, bf16[1024,256]{1,0:T(8,128)(2,1)} %weight_hbm.1), custom_call_target="tpu_custom_call" | custom-call | flops 1048576 | bytes 1048576 | tf_op jit(solution)/shard_map/pallas_call | solution.py:50
  3.5 20.6 %all-to-all-start = ((bf16[128,8,512]{2,1,0:T(8,128)(2,1)}), bf16[128,8,512]{2,1,0:T(8,128)(2,1)S(1)}, u32[]{:S(2)}, u32[]{:S(2)}) async-start(bf16[128,8,512]{2,1,0:T(8,128)(2,1)} %get-tuple-element.37), calls=%async_computation | async-start | bytes 2097152 | tf_op jit(solution)/shard_map/all_to_all | solution.py:338
  24.2 0.7 shard_map.133
  24.9 0.0 copy-start.8
  25.0 0.0 copy-start.11
  25.0 0.0 copy-start.3
  25.0 1.2 fusion.19
  26.2 2.8 %collective-permute-start = (bf16[16,8,1024]{2,1,0:T(8,128)(2,1)S(1)}, bf16[16,8,1024]{2,1,0:T(8,128)(2,1)S(1)}, u32[]{:S(2)}, u32[]{:S(2)}) collective-permute-start(bf16[16,8,1024]{2,1,0:T(8,128)(2,1)S(1)} %get-tuple-element.78), channel_id=1, source_target_pairs={{0,4},{4,0},{8,12},{12,8},{16,20},{20,16},{24,28},{28,24},{32,36},... | collective-permute-start | bytes 786440 | tf_op jit(solution)/shard_map/ppermute | solution.py:370
  29.0 2.9 %collective-permute-start.1 = (bf16[16,8,1024]{2,1,0:T(8,128)(2,1)S(1)}, bf16[16,8,1024]{2,1,0:T(8,128)(2,1)S(1)}, u32[]{:S(2)}, u32[]{:S(2)}) collective-permute-start(bf16[16,8,1024]{2,1,0:T(8,128)(2,1)S(1)} %get-tuple-element.77), channel_id=1, source_target_pairs={{0,128},{4,132},{8,136},{12,140},{16,144},{20,148},{24,152},{28,15... | collective-permute-start | bytes 786440 | tf_op jit(solution)/shard_map/ppermute | solution.py:370
  31.9 3.6 %collective-permute-start.2 = (bf16[16,8,1024]{2,1,0:T(8,128)(2,1)}, bf16[16,8,1024]{2,1,0:T(8,128)(2,1)}, u32[]{:S(2)}, u32[]{:S(2)}) collective-permute-start(bf16[16,8,1024]{2,1,0:T(8,128)(2,1)} %get-tuple-element.76), channel_id=1, source_target_pairs={{0,132},{4,128},{8,140},{12,136},{16,148},{20,144},{24,156},{28,15... | collective-permute-start | bytes 786440 | tf_op jit(solution)/shard_map/ppermute | solution.py:370
  35.5 3.3 %collective-permute-start.3 = (bf16[16,8,1024]{2,1,0:T(8,128)(2,1)}, bf16[16,8,1024]{2,1,0:T(8,128)(2,1)}, u32[]{:S(2)}, u32[]{:S(2)}) collective-permute-start(bf16[16,8,1024]{2,1,0:T(8,128)(2,1)} %get-tuple-element.75), channel_id=1, source_target_pairs={{0,256},{4,260},{8,264},{12,268},{16,272},{20,276},{24,280},{28,28... | collective-permute-start | bytes 786440 | tf_op jit(solution)/shard_map/ppermute | solution.py:370
  38.8 3.8 %collective-permute-start.4 = (bf16[16,8,1024]{2,1,0:T(8,128)(2,1)}, bf16[16,8,1024]{2,1,0:T(8,128)(2,1)}, u32[]{:S(2)}, u32[]{:S(2)}) collective-permute-start(bf16[16,8,1024]{2,1,0:T(8,128)(2,1)} %get-tuple-element.74), channel_id=1, source_target_pairs={{0,260},{4,256},{8,268},{12,264},{16,276},{20,272},{24,284},{28,28... | collective-permute-start | bytes 786440 | tf_op jit(solution)/shard_map/ppermute | solution.py:370
  42.5 0.6 select_reduce_fusion.2
  44.5 0.1 dynamic_slice.9
  44.6 0.1 copy.28
  45.4 0.1 fusion.17
  45.5 0.1 select_reduce_fusion.3
  45.6 0.1 multiply_reduce_fusion
  45.7 0.1 add_add_fusion
  45.8 0.4 select_reduce_fusion.1
  46.2 0.5 select_reduce_fusion
  46.7 0.2 fusion.18
  46.9 0.1 copy.29
  47.0 0.1 copy.30
  47.1 0.1 copy.27.point_ref
  47.2 3.2 %collective-permute-start.5 = (bf16[16,8,1024]{2,1,0:T(8,128)(2,1)}, bf16[16,8,1024]{2,1,0:T(8,128)(2,1)}, u32[]{:S(2)}, u32[]{:S(2)}) collective-permute-start(bf16[16,8,1024]{2,1,0:T(8,128)(2,1)} %get-tuple-element.73), channel_id=1, source_target_pairs={{0,384},{4,388},{8,392},{12,396},{16,400},{20,404},{24,408},{28,41... | collective-permute-start | bytes 786440 | tf_op jit(solution)/shard_map/ppermute | solution.py:370
  50.4 2.6 %collective-permute-start.6 = (bf16[16,8,1024]{2,1,0:T(8,128)(2,1)}, bf16[16,8,1024]{2,1,0:T(8,128)(2,1)}, u32[]{:S(2)}, u32[]{:S(2)}) collective-permute-start(bf16[16,8,1024]{2,1,0:T(8,128)(2,1)} %get-tuple-element.72), channel_id=1, source_target_pairs={{0,388},{4,384},{8,396},{12,392},{16,404},{20,400},{24,412},{28,40... | collective-permute-start | bytes 786440 | tf_op jit(solution)/shard_map/ppermute | solution.py:370
  53.1 2.5 %shard_map.132 = (f32[6,128,256]{2,1,0:T(8,128)S(1)}, f32[6,128,256]{2,1,0:T(8,128)}, bf16[1024,256]{1,0:T(8,128)(2,1)S(1)}, f32[1,256]{1,0:T(1,128)S(1)}) custom-call(s32[1]{0:T(128)} %bitcast.5.band_ref, bf16[128,256]{1,0:T(8,128)(2,1)S(1)} %copy-done.3, bf16[256,32]{1,0:T(8,128)(2,1)S(1)} %copy.27.point_ref, bf16[6,128,256]{2,1,0:T(8,128)(2,1)S(1)} %copy-done.1, ...), custom_call_target="tpu_custom_call" | custom-call | flops 1073741824 | bytes 4194304 | tf_op jit(solution)/shard_map/pallas_call | solution.py:50
  55.6 0.1 copy.31
  55.7 0.1 max.10.source_ref
  55.8 0.2 dynamic-slice_reduce_fusion.count_ref
  56.0 1.8 %collective-permute-done.3.refs_4_ = bf16[16,8,1024]{2,1,0:T(8,128)(2,1)} collective-permute-done((bf16[16,8,1024]{2,1,0:T(8,128)(2,1)}, bf16[16,8,1024]{2,1,0:T(8,128)(2,1)}, u32[]{:S(2)}, u32[]{:S(2)}) %collective-permute-start.3) | collective-permute-done | bytes 262176 | tf_op jit(solution)/shard_map/ppermute | solution.py:370
  57.8 7.9 %collective-permute-done.4.refs_5_ = bf16[16,8,1024]{2,1,0:T(8,128)(2,1)} collective-permute-done((bf16[16,8,1024]{2,1,0:T(8,128)(2,1)}, bf16[16,8,1024]{2,1,0:T(8,128)(2,1)}, u32[]{:S(2)}, u32[]{:S(2)}) %collective-permute-start.4) | collective-permute-done | bytes 262176 | tf_op jit(solution)/shard_map/ppermute | solution.py:370
  65.7 4.2 %collective-permute-done.6.refs_7_ = bf16[16,8,1024]{2,1,0:T(8,128)(2,1)} collective-permute-done((bf16[16,8,1024]{2,1,0:T(8,128)(2,1)}, bf16[16,8,1024]{2,1,0:T(8,128)(2,1)}, u32[]{:S(2)}, u32[]{:S(2)}) %collective-permute-start.6) | collective-permute-done | bytes 262176 | tf_op jit(solution)/shard_map/ppermute | solution.py:370
  69.8 8.6 %all-to-all-done.lane_ref = bf16[128,8,512]{2,1,0:T(8,128)(2,1)S(1)} async-done(((bf16[128,8,512]{2,1,0:T(8,128)(2,1)}), bf16[128,8,512]{2,1,0:T(8,128)(2,1)S(1)}, u32[]{:S(2)}, u32[]{:S(2)}) %all-to-all-start) | async-done | bytes 1048608 | tf_op jit(solution)/shard_map/all_to_all | solution.py:338
  78.5 0.6 shard_map.134
  79.1 11.3 %all_to_all.30.kv_ref = bf16[4,144,512]{2,1,0:T(8,128)(2,1)S(1)} all-to-all(bf16[4,144,512]{2,1,0:T(8,128)(2,1)S(1)} %bitcast.36), channel_id=1, replica_groups=mesh['dp'=128,'mp'=4] {'mp'}, dimensions={0} | all-to-all | bytes 1179648 | tf_op jit(solution)/shard_map/all_to_all | solution.py:426
  90.3 3.8 %shard_map.135 = (bf16[6,128,256]{2,1,0:T(8,128)(2,1)}, bf16[4,144,256]{2,1,0:T(8,128)(2,1)}) custom-call(s32[6]{0:T(128)S(1)} %dynamic-slice_reduce_fusion.count_ref, bf16[4,144,512]{2,1,0:T(8,128)(2,1)S(1)} %all_to_all.30.kv_ref, f32[6,128,256]{2,1,0:T(8,128)S(1)} %get-tuple-element.46.base_ref, f32[6,128,256]{2,1,0:T(8,128)} %get-tuple-element.47.pull_hbm, ...), custom_call_target="tpu_custom_call" | custom-call | flops 1048576 | bytes 1048576 | tf_op jit(solution)/shard_map/pallas_call | solution.py:50
  94.2 3.5 %all-to-all-start.2 = ((bf16[4,144,256]{2,1,0:T(8,128)(2,1)}), bf16[4,144,256]{2,1,0:T(8,128)(2,1)S(1)}, u32[]{:S(2)}, u32[]{:S(2)}) async-start(bf16[4,144,256]{2,1,0:T(8,128)(2,1)} %get-tuple-element.61), calls=%async_computation.2 | async-start | bytes 589824 | tf_op jit(solution)/shard_map/all_to_all | solution.py:452
  97.7 3.6 %shard_map.136.turned_ref = bf16[1024,1024]{1,0:T(8,128)(2,1)S(1)} custom-call(bf16[16,8,1024]{2,1,0:T(8,128)(2,1)} %get-tuple-element.62.refs_0_, bf16[16,8,1024]{2,1,0:T(8,128)(2,1)} %copy-done.6, bf16[16,8,1024]{2,1,0:T(8,128)(2,1)} %copy-done.7, bf16[16,8,1024]{2,1,0:T(8,128)(2,1)} %collective-permute-done.2.refs_3_, ...), custom_call_target="tpu_custom_call" | custom-call | flops 1073741824 | bytes 4194304 | tf_op jit(solution)/shard_map/pallas_call | solution.py:50
  101.2 2.1 %all-to-all-done.2 = bf16[4,144,256]{2,1,0:T(8,128)(2,1)S(1)} async-done(((bf16[4,144,256]{2,1,0:T(8,128)(2,1)}), bf16[4,144,256]{2,1,0:T(8,128)(2,1)S(1)}, u32[]{:S(2)}, u32[]{:S(2)}) %all-to-all-start.2) | async-done | bytes 294944 | tf_op jit(solution)/shard_map/all_to_all | solution.py:452
  103.3 1.0 shard_map.137
  104.3 31.3 %all_to_all.31 = bf16[16,64,256]{2,1,0:T(8,128)(2,1)S(1)} all-to-all(bf16[16,64,256]{2,1,0:T(8,128)(2,1)S(1)} %bitcast.37), channel_id=1, replica_groups={{0,8,16,24,32,40,48,56,64,72,80,88,96,104,112,120},{4,12,20,28,36,44,52..., dimensions={0} | all-to-all | bytes 1048576 | tf_op jit(solution)/shard_map/all_to_all | solution.py:477
  135.7 0.7 shard_map.138
  136.4 21.1 %all_to_all.32 = bf16[32,32,256]{2,1,0:T(8,128)(2,1)S(1)} all-to-all(bf16[32,32,256]{2,1,0:T(8,128)(2,1)S(1)} %bitcast.39), channel_id=1, replica_groups={{0,1,2,3,4,5,6,7,128,129,130,131,132,133,134,135,256,257,258,259,260,26..., dimensions={0} | all-to-all | bytes 1048576 | tf_op jit(solution)/shard_map/all_to_all | solution.py:477
  157.5 0.1 convert_reduce_fusion
  157.6 17.6 %all_to_all.33 = f32[16,2,256]{2,1,0:T(2,128)S(1)} all-to-all(f32[16,2,256]{2,1,0:T(2,128)S(1)} %copy.32), channel_id=1, replica_groups={{0,8,16,24,32,40,48,56,64,72,80,88,96,104,112,120},{4,12,20,28,36,44,52..., dimensions={0} | all-to-all | bytes 65536 | tf_op jit(solution)/shard_map/all_to_all | solution.py:477
  175.2 0.6 reduce_sum.79
  (34 shorter events, 0.2 us)
Async XLA Ops:
  0.6 23.6 %copy-start = (bf16[48,8,1024]{2,1,0:T(8,128)(2,1)S(1)}, bf16[48,8,1024]{2,1,0:T(8,128)(2,1)}, u32[]{:S(2)}) copy-start(bf16[48,8,1024]{2,1,0:T(8,128)(2,1)} %param.16) | copy-start | bytes 2359300
  3.5 74.9 %all-to-all-start = ((bf16[128,8,512]{2,1,0:T(8,128)(2,1)}), bf16[128,8,512]{2,1,0:T(8,128)(2,1)S(1)}, u32[]{:S(2)}, u32[]{:S(2)}) async-start(bf16[128,8,512]{2,1,0:T(8,128)(2,1)} %get-tuple-element.37), calls=%async_computation | async-start | bytes 2097152 | tf_op jit(solution)/shard_map/all_to_all | solution.py:338
  24.9 17.6 %copy-start.10 = (s32[768]{0:T(1024)S(1)}, s32[768]{0:T(1024)}, u32[]{:S(2)}) copy-start(s32[768]{0:T(1024)} %param.12) | copy-start | bytes 9220
  24.9 19.6 %copy-start.9 = (s32[6,11,4]{1,2,0:T(4,128)S(1)}, s32[6,11,4]{1,2,0:T(4,128)}, u32[]{:S(2)}) copy-start(s32[6,11,4]{1,2,0:T(4,128)} %param.14) | copy-start | bytes 3172
  24.9 20.4 %copy-start.8 = (s32[6144]{0:T(1024)S(1)}, s32[6144]{0:T(1024)}, u32[]{:S(2)}) copy-start(s32[6144]{0:T(1024)} %param.13) | copy-start | bytes 73732
  25.0 22.1 %copy-start.11 = (bf16[256,32]{0,1:T(8,128)(2,1)S(1)}, bf16[256,32]{0,1:T(8,128)(2,1)}, u32[]{:S(2)}) copy-start(bf16[256,32]{0,1:T(8,128)(2,1)} %param.21) | copy-start | bytes 49156
  25.0 28.1 %copy-start.1 = (bf16[6,128,256]{2,1,0:T(8,128)(2,1)S(1)}, bf16[6,128,256]{2,1,0:T(8,128)(2,1)}, u32[]{:S(2)}) copy-start(bf16[6,128,256]{2,1,0:T(8,128)(2,1)} %prev_ref.1) | copy-start | bytes 1179652
  25.0 28.1 %copy-start.2 = (bf16[6,128,256]{2,1,0:T(8,128)(2,1)S(1)}, bf16[6,128,256]{2,1,0:T(8,128)(2,1)}, u32[]{:S(2)}) copy-start(bf16[6,128,256]{2,1,0:T(8,128)(2,1)} %cotangent_ref.1) | copy-start | bytes 1179652
  25.0 28.1 %copy-start.3 = (bf16[128,256]{1,0:T(8,128)(2,1)S(1)}, bf16[128,256]{1,0:T(8,128)(2,1)}, u32[]{:S(2)}) copy-start(bf16[128,256]{1,0:T(8,128)(2,1)} %query_ref.1) | copy-start | bytes 196612
  25.0 28.1 %copy-start.4 = (s32[6,4,128]{2,1,0:T(4,128)S(1)}, s32[6,4,128]{2,1,0:T(4,128)}, u32[]{:S(2)}) copy-start(s32[6,4,128]{2,1,0:T(4,128)} %align_ref.1) | copy-start | bytes 36868
  25.0 28.1 %copy-start.5 = (f32[256]{0:T(256)S(1)}, f32[256]{0:T(256)}, u32[]{:S(2)}) copy-start(f32[256]{0:T(256)} %param.22) | copy-start | bytes 3076
  26.2 21.0 %collective-permute-start = (bf16[16,8,1024]{2,1,0:T(8,128)(2,1)S(1)}, bf16[16,8,1024]{2,1,0:T(8,128)(2,1)S(1)}, u32[]{:S(2)}, u32[]{:S(2)}) collective-permute-start(bf16[16,8,1024]{2,1,0:T(8,128)(2,1)S(1)} %get-tuple-element.78), channel_id=1, source_target_pairs={{0,4},{4,0},{8,12},{12,8},{16,20},{20,16},{24,28},{28,24},{32,36},... | collective-permute-start | bytes 786440 | tf_op jit(solution)/shard_map/ppermute | solution.py:370
  29.0 21.4 %collective-permute-start.1 = (bf16[16,8,1024]{2,1,0:T(8,128)(2,1)S(1)}, bf16[16,8,1024]{2,1,0:T(8,128)(2,1)S(1)}, u32[]{:S(2)}, u32[]{:S(2)}) collective-permute-start(bf16[16,8,1024]{2,1,0:T(8,128)(2,1)S(1)} %get-tuple-element.77), channel_id=1, source_target_pairs={{0,128},{4,132},{8,136},{12,140},{16,144},{20,148},{24,152},{28,15... | collective-permute-start | bytes 786440 | tf_op jit(solution)/shard_map/ppermute | solution.py:370
  31.9 24.2 %collective-permute-start.2 = (bf16[16,8,1024]{2,1,0:T(8,128)(2,1)}, bf16[16,8,1024]{2,1,0:T(8,128)(2,1)}, u32[]{:S(2)}, u32[]{:S(2)}) collective-permute-start(bf16[16,8,1024]{2,1,0:T(8,128)(2,1)} %get-tuple-element.76), channel_id=1, source_target_pairs={{0,132},{4,128},{8,140},{12,136},{16,148},{20,144},{24,156},{28,15... | collective-permute-start | bytes 786440 | tf_op jit(solution)/shard_map/ppermute | solution.py:370
  35.5 22.3 %collective-permute-start.3 = (bf16[16,8,1024]{2,1,0:T(8,128)(2,1)}, bf16[16,8,1024]{2,1,0:T(8,128)(2,1)}, u32[]{:S(2)}, u32[]{:S(2)}) collective-permute-start(bf16[16,8,1024]{2,1,0:T(8,128)(2,1)} %get-tuple-element.75), channel_id=1, source_target_pairs={{0,256},{4,260},{8,264},{12,268},{16,272},{20,276},{24,280},{28,28... | collective-permute-start | bytes 786440 | tf_op jit(solution)/shard_map/ppermute | solution.py:370
  38.8 26.9 %collective-permute-start.4 = (bf16[16,8,1024]{2,1,0:T(8,128)(2,1)}, bf16[16,8,1024]{2,1,0:T(8,128)(2,1)}, u32[]{:S(2)}, u32[]{:S(2)}) collective-permute-start(bf16[16,8,1024]{2,1,0:T(8,128)(2,1)} %get-tuple-element.74), channel_id=1, source_target_pairs={{0,260},{4,256},{8,268},{12,264},{16,276},{20,272},{24,284},{28,28... | collective-permute-start | bytes 786440 | tf_op jit(solution)/shard_map/ppermute | solution.py:370
  47.2 5.8 %copy-start.6 = (bf16[16,8,1024]{2,1,0:T(8,128)(2,1)}, bf16[16,8,1024]{2,1,0:T(8,128)(2,1)S(1)}, u32[]{:S(2)}) copy-start(bf16[16,8,1024]{2,1,0:T(8,128)(2,1)S(1)} %collective-permute-done.refs_1_) | copy-start | bytes 786436
  47.2 18.4 %collective-permute-start.5 = (bf16[16,8,1024]{2,1,0:T(8,128)(2,1)}, bf16[16,8,1024]{2,1,0:T(8,128)(2,1)}, u32[]{:S(2)}, u32[]{:S(2)}) collective-permute-start(bf16[16,8,1024]{2,1,0:T(8,128)(2,1)} %get-tuple-element.73), channel_id=1, source_target_pairs={{0,384},{4,388},{8,392},{12,396},{16,400},{20,404},{24,408},{28,41... | collective-permute-start | bytes 786440 | tf_op jit(solution)/shard_map/ppermute | solution.py:370
  50.4 2.6 %copy-start.7 = (bf16[16,8,1024]{2,1,0:T(8,128)(2,1)}, bf16[16,8,1024]{2,1,0:T(8,128)(2,1)S(1)}, u32[]{:S(2)}) copy-start(bf16[16,8,1024]{2,1,0:T(8,128)(2,1)S(1)} %collective-permute-done.1.refs_2_) | copy-start | bytes 786436
  50.4 19.4 %collective-permute-start.6 = (bf16[16,8,1024]{2,1,0:T(8,128)(2,1)}, bf16[16,8,1024]{2,1,0:T(8,128)(2,1)}, u32[]{:S(2)}, u32[]{:S(2)}) collective-permute-start(bf16[16,8,1024]{2,1,0:T(8,128)(2,1)} %get-tuple-element.72), channel_id=1, source_target_pairs={{0,388},{4,384},{8,396},{12,392},{16,404},{20,400},{24,412},{28,40... | collective-permute-start | bytes 786440 | tf_op jit(solution)/shard_map/ppermute | solution.py:370
  94.2 9.1 %all-to-all-start.2 = ((bf16[4,144,256]{2,1,0:T(8,128)(2,1)}), bf16[4,144,256]{2,1,0:T(8,128)(2,1)S(1)}, u32[]{:S(2)}, u32[]{:S(2)}) async-start(bf16[4,144,256]{2,1,0:T(8,128)(2,1)} %get-tuple-element.61), calls=%async_computation.2 | async-start | bytes 589824 | tf_op jit(solution)/shard_map/all_to_all | solution.py:452

commit v9 on v8

--- a/solution.py
+++ b/solution.py
@@ -41,7 +41,9 @@
     return pltpu.VMEM(shape, dtype)
 
 
-def call(body, outs, *args, specs=None, scratch=(), cost=(1 << 20, 1 << 20), pinned=True):
+def call(
+    body, outs, *args, specs=None, out_specs=None, scratch=(), cost=(1 << 20, 1 << 20), pinned=True
+):
     specs = specs or [vmem()] * len(args)
     if pinned:
         args = [
@@ -51,7 +53,7 @@
         body,
         out_shape=outs,
         in_specs=specs,
-        out_specs=jax.tree.map(lambda _: vmem(), outs),
+        out_specs=out_specs or jax.tree.map(lambda _: vmem(), outs),
         scratch_shapes=scratch,
         compiler_params=pltpu.CompilerParams(vmem_limit_bytes=24 << 20),
         cost_estimate=pl.CostEstimate(flops=cost[0], bytes_accessed=cost[1], transcendentals=0),
@@ -215,10 +217,12 @@
     pull_hbm,
     heads_ref,
     gain_ref,
+    out_hbm,
+    grad_ref,
     out_ref,
-    grad_ref,
     pull_ref,
     sem,
+    out_sems,
     score_ref,
     prob_ref,
     norm_ref,
@@ -254,12 +258,15 @@
         )
         norm_ref[m] = base_ref[m] + dot(tall, values, 0, 0)
     move.wait()
+    written = []
     for m in range(samples):
         pre_norm = norm_ref[m]
         centred = pre_norm - jnp.mean(pre_norm, axis=1, keepdims=True)
         scale = lax.rsqrt(jnp.mean(centred * centred, axis=1, keepdims=True) + NORM_EPS)
         unit = centred * scale
         out_ref[m] = (unit * gain).astype(BF16)
+        written.append(pltpu.make_async_copy(out_ref.at[m], out_hbm.at[m], out_sems.at[m]))
+        written[m].start()
         pull = pull_ref[m]
         pull = pull - unit * jnp.mean(pull * unit, axis=1, keepdims=True)
         cross_ref[m] = (pull * scale).astype(BF16)
@@ -267,6 +274,8 @@
         pull = cross_ref[m]
         pull = jnp.concatenate([pull * mask for mask in masks], axis=0)
         grad_ref[:, spans[m], :] = dot(prob_ref[m], pull).astype(BF16).reshape(parts, step, channels)
+    for move in written:
+        move.wait()
 
 
 def return_kernel(source_ref, grad_ref, lane_ref, sum_ref):
@@ -439,17 +448,35 @@
         heads,
         gain,
         specs=[smem(), vmem(), vmem(), pl.BlockSpec(memory_space=pltpu.HBM), vmem(), vmem()],
+        out_specs=(pl.BlockSpec(memory_space=pltpu.HBM), vmem()),
         scratch=[
+            pltpu.VMEM((samples, queries, channels), BF16),
             pltpu.VMEM((samples, queries, channels), F32),
             pltpu.SemaphoreType.DMA,
+            pltpu.SemaphoreType.DMA((samples,)),
             pltpu.VMEM((bands, piece, HEADS * queries), F32),
             pltpu.VMEM((samples, bands * SEEN * quarter, HEADS * queries), BF16),
             pltpu.VMEM((samples, queries, channels), F32),
             pltpu.VMEM((samples, queries, channels), BF16),
         ],
     )
+    grads = lax.all_to_all(grads, "mp", split_axis=0, concat_axis=0, tiled=True)
     grads, pieces = lax.optimization_barrier((grads, pieces))
-    grads = lax.all_to_all(grads, "mp", split_axis=0, concat_axis=0, tiled=True)
+    back = call(
+        return_kernel,
+        on_chip((owners, quarter, channels), BF16),
+        back_lane,
+        grads.reshape(bands * samples * SEEN, quarter, channels),
+        specs=[smem(), vmem()],
+        scratch=[pltpu.VMEM((owners, quarter, channels), F32)],
+    )
+
+    def exchange(part, axis, groups):
+        return lax.all_to_all(
+            part, axis, split_axis=0, concat_axis=0, tiled=True, axis_index_groups=groups
+        )
+
+    columns = [[device(y, z, c) for z in zs] for y in ys for c in cs]
     tokens = owners * quarter
     turned = call(
         functools.partial(turn_kernel, bands=bands, share=share),
@@ -463,22 +490,6 @@
         ],
         cost=cost,
     )
-    grads, turned = lax.optimization_barrier((grads, turned))
-    back = call(
-        return_kernel,
-        on_chip((owners, quarter, channels), BF16),
-        back_lane,
-        grads.reshape(bands * samples * SEEN, quarter, channels),
-        specs=[smem(), vmem()],
-        scratch=[pltpu.VMEM((owners, quarter, channels), F32)],
-    )
-
-    def exchange(part, axis, groups):
-        return lax.all_to_all(
-            part, axis, split_axis=0, concat_axis=0, tiled=True, axis_index_groups=groups
-        )
-
-    columns = [[device(y, z, c) for z in zs] for y in ys for c in cs]
     back = exchange(back.reshape(deep, tokens // deep, channels), "dp", columns)
     neck = call(
         functools.partial(neck_kernel, samples=cams.shape[0]),

time: 176 us -> 176 us (level)
  blocking collectives: 81.3 us -> 58.1 us
  waiting for transfers between devices: 24.5 us -> 41.7 us
  starting transfers between devices: 46.1 us -> 51.3 us
    all_to_all x3 -> x2, blocking collectives: 70 us -> 38.8 us  [exchange(): lax.all_to_all(part, axis, split_axis=0, concat_axis=0, tiled=True, axis_...]
    all_to_all x1, waiting for transfers between devices: 2.08 us -> 19.2 us  [exchange(): lax.all_to_all(part, axis, split_axis=0, concat_axis=0, tiled=True, axis_...]
    all_to_all x0 -> x1, blocking collectives: none -> 8.07 us  [on_device(): grads = lax.all_to_all(grads, 'mp', split_axis=0, concat_axis=0, tiled=True)]
    all_to_all x1, starting transfers between devices: 3.46 us -> 8.65 us  [exchange(): lax.all_to_all(part, axis, split_axis=0, concat_axis=0, tiled=True, axis_...]
where the time goes in v9:
time: 176 us; the launch traced here: 175 us
  blocking collectives  58.1 us (33%)
  starting transfers between devices  51.3 us (29%)
  waiting for transfers between devices  41.7 us (24%)
  Pallas kernels  16.2 us (9%)
  between operations  3 us (2%)
  other arithmetic  2.86 us (2%)
  local copies, waits for them, and re-layouts  2.18 us (1%)
    all_to_all x2, blocking collectives, exchange(): lax.all_to_all(part, axis, split_axis=0, concat_axis=0, tiled=True, axis_...  38.8 us
    ppermute x7, starting transfers between devices, on_device(): pieces.append(lax.ppermute(dealt[p], 'dp', moves))  22.1 us
    all_to_all x1, starting transfers between devices, on_device(): got = lax.all_to_all(lanes, 'dp', split_axis=0, concat_axis=0, tiled=True)  20.6 us
    all_to_all x1, waiting for transfers between devices, exchange(): lax.all_to_all(part, axis, split_axis=0, concat_axis=0, tiled=True, axis_...  19.2 us
    pallas_call x8, Pallas kernels, call(): pl.pallas_call(body, out_shape=outs, in_specs=specs, out_specs=out_specs...  16.2 us
    ppermute x7, waiting for transfers between devices, on_device(): pieces.append(lax.ppermute(dealt[p], 'dp', moves))  13.8 us
    all_to_all x1, blocking collectives, on_device(): lax.all_to_all(chosen_kv.reshape(bands, piece, 2 * channels), 'mp', split...  11.3 us
    all_to_all x1, starting transfers between devices, exchange(): lax.all_to_all(part, axis, split_axis=0, concat_axis=0, tiled=True, axis_...  8.65 us
  transfers between devices with their start and end apart: 9, of which 5 were waited for; matrix products, arithmetic and copies ran while one was open for 2% of the time, Pallas kernels for 4%

profile of v9, /device:TPU:1, one launch (start us, length us, event | category | flops | bytes accessed | tf_op | source)
XLA Modules:
  0.0 175.4 jit_solution(9377960569747094653)
XLA Ops:
  0.6 2.9 %shard_map.131 = (bf16[128,8,512]{2,1,0:T(8,128)(2,1)}, s32[8,128]{1,0:T(8,128)S(1)}) custom-call(s32[1]{0:T(128)} %bitcast.bin_ref, s32[6,128]{1,0:T(8,128)} %bitcast.46, s32[1,6144]{1,0:T(1,128)} %bitcast.45, bf16[384,1024]{1,0:T(8,128)(2,1)} %bitcast.40, bf16[384,256]{1,0:T(8,128)(2,1)} %bitcast.43, bf16[1024,256]{1,0:T(8,128)(2,1)} %weight_hbm.1), custom_call_target="tpu_custom_call" | custom-call | flops 1048576 | bytes 1048576 | tf_op jit(solution)/shard_map/pallas_call | solution.py:52
  3.5 20.6 %all-to-all-start = ((bf16[128,8,512]{2,1,0:T(8,128)(2,1)}), bf16[128,8,512]{2,1,0:T(8,128)(2,1)S(1)}, u32[]{:S(2)}, u32[]{:S(2)}) async-start(bf16[128,8,512]{2,1,0:T(8,128)(2,1)} %get-tuple-element.35), calls=%async_computation | async-start | bytes 2097152 | tf_op jit(solution)/shard_map/all_to_all | solution.py:347
  24.2 0.7 shard_map.133
  24.9 0.0 copy-start.9
  24.9 0.0 copy-start.8
  25.0 0.0 copy-start.1
  25.0 1.2 fusion.19
  26.2 2.8 %collective-permute-start = (bf16[16,8,1024]{2,1,0:T(8,128)(2,1)S(1)}, bf16[16,8,1024]{2,1,0:T(8,128)(2,1)S(1)}, u32[]{:S(2)}, u32[]{:S(2)}) collective-permute-start(bf16[16,8,1024]{2,1,0:T(8,128)(2,1)S(1)} %get-tuple-element.74), channel_id=1, source_target_pairs={{0,4},{4,0},{8,12},{12,8},{16,20},{20,16},{24,28},{28,24},{32,36},... | collective-permute-start | bytes 786440 | tf_op jit(solution)/shard_map/ppermute | solution.py:379
  29.0 2.9 %collective-permute-start.1 = (bf16[16,8,1024]{2,1,0:T(8,128)(2,1)S(1)}, bf16[16,8,1024]{2,1,0:T(8,128)(2,1)S(1)}, u32[]{:S(2)}, u32[]{:S(2)}) collective-permute-start(bf16[16,8,1024]{2,1,0:T(8,128)(2,1)S(1)} %get-tuple-element.73), channel_id=1, source_target_pairs={{0,128},{4,132},{8,136},{12,140},{16,144},{20,148},{24,152},{28,15... | collective-permute-start | bytes 786440 | tf_op jit(solution)/shard_map/ppermute | solution.py:379
  31.9 3.6 %collective-permute-start.2 = (bf16[16,8,1024]{2,1,0:T(8,128)(2,1)}, bf16[16,8,1024]{2,1,0:T(8,128)(2,1)}, u32[]{:S(2)}, u32[]{:S(2)}) collective-permute-start(bf16[16,8,1024]{2,1,0:T(8,128)(2,1)} %get-tuple-element.72), channel_id=1, source_target_pairs={{0,132},{4,128},{8,140},{12,136},{16,148},{20,144},{24,156},{28,15... | collective-permute-start | bytes 786440 | tf_op jit(solution)/shard_map/ppermute | solution.py:379
  35.5 3.3 %collective-permute-start.3 = (bf16[16,8,1024]{2,1,0:T(8,128)(2,1)}, bf16[16,8,1024]{2,1,0:T(8,128)(2,1)}, u32[]{:S(2)}, u32[]{:S(2)}) collective-permute-start(bf16[16,8,1024]{2,1,0:T(8,128)(2,1)} %get-tuple-element.71), channel_id=1, source_target_pairs={{0,256},{4,260},{8,264},{12,268},{16,272},{20,276},{24,280},{28,28... | collective-permute-start | bytes 786440 | tf_op jit(solution)/shard_map/ppermute | solution.py:379
  38.8 3.8 %collective-permute-start.4 = (bf16[16,8,1024]{2,1,0:T(8,128)(2,1)}, bf16[16,8,1024]{2,1,0:T(8,128)(2,1)}, u32[]{:S(2)}, u32[]{:S(2)}) collective-permute-start(bf16[16,8,1024]{2,1,0:T(8,128)(2,1)} %get-tuple-element.70), channel_id=1, source_target_pairs={{0,260},{4,256},{8,268},{12,264},{16,276},{20,272},{24,284},{28,28... | collective-permute-start | bytes 786440 | tf_op jit(solution)/shard_map/ppermute | solution.py:379
  42.5 0.6 select_reduce_fusion.2
  44.5 0.1 dynamic_slice.9
  44.6 0.1 copy.28
  45.4 0.1 fusion.17
  45.5 0.1 select_reduce_fusion.3
  45.6 0.1 multiply_reduce_fusion
  45.7 0.1 add_add_fusion
  45.8 0.4 select_reduce_fusion.1
  46.2 0.5 select_reduce_fusion
  46.7 0.2 fusion.18
  46.9 0.1 copy.29
  47.0 0.1 copy.30
  47.1 0.1 copy.27.point_ref
  47.2 3.2 %collective-permute-start.5 = (bf16[16,8,1024]{2,1,0:T(8,128)(2,1)}, bf16[16,8,1024]{2,1,0:T(8,128)(2,1)}, u32[]{:S(2)}, u32[]{:S(2)}) collective-permute-start(bf16[16,8,1024]{2,1,0:T(8,128)(2,1)} %get-tuple-element.69), channel_id=1, source_target_pairs={{0,384},{4,388},{8,392},{12,396},{16,400},{20,404},{24,408},{28,41... | collective-permute-start | bytes 786440 | tf_op jit(solution)/shard_map/ppermute | solution.py:379
  50.4 2.6 %collective-permute-start.6 = (bf16[16,8,1024]{2,1,0:T(8,128)(2,1)}, bf16[16,8,1024]{2,1,0:T(8,128)(2,1)}, u32[]{:S(2)}, u32[]{:S(2)}) collective-permute-start(bf16[16,8,1024]{2,1,0:T(8,128)(2,1)} %get-tuple-element.68), channel_id=1, source_target_pairs={{0,388},{4,384},{8,396},{12,392},{16,404},{20,400},{24,412},{28,40... | collective-permute-start | bytes 786440 | tf_op jit(solution)/shard_map/ppermute | solution.py:379
  53.1 2.5 %shard_map.132 = (f32[6,128,256]{2,1,0:T(8,128)S(1)}, f32[6,128,256]{2,1,0:T(8,128)}, bf16[1024,256]{1,0:T(8,128)(2,1)S(1)}, f32[1,256]{1,0:T(1,128)S(1)}) custom-call(s32[1]{0:T(128)} %bitcast.5.band_ref, bf16[128,256]{1,0:T(8,128)(2,1)S(1)} %copy-done.3, bf16[256,32]{1,0:T(8,128)(2,1)S(1)} %copy.27.point_ref, bf16[6,128,256]{2,1,0:T(8,128)(2,1)S(1)} %copy-done.1, ...), custom_call_target="tpu_custom_call" | custom-call | flops 1073741824 | bytes 4194304 | tf_op jit(solution)/shard_map/pallas_call | solution.py:52
  55.6 0.1 copy.31
  55.7 0.1 max.10.source_ref
  55.8 0.2 dynamic-slice_reduce_fusion.count_ref
  56.0 1.8 %collective-permute-done.3.refs_4_ = bf16[16,8,1024]{2,1,0:T(8,128)(2,1)} collective-permute-done((bf16[16,8,1024]{2,1,0:T(8,128)(2,1)}, bf16[16,8,1024]{2,1,0:T(8,128)(2,1)}, u32[]{:S(2)}, u32[]{:S(2)}) %collective-permute-start.3) | collective-permute-done | bytes 262176 | tf_op jit(solution)/shard_map/ppermute | solution.py:379
  57.8 7.9 %collective-permute-done.4.refs_5_ = bf16[16,8,1024]{2,1,0:T(8,128)(2,1)} collective-permute-done((bf16[16,8,1024]{2,1,0:T(8,128)(2,1)}, bf16[16,8,1024]{2,1,0:T(8,128)(2,1)}, u32[]{:S(2)}, u32[]{:S(2)}) %collective-permute-start.4) | collective-permute-done | bytes 262176 | tf_op jit(solution)/shard_map/ppermute | solution.py:379
  65.7 4.2 %collective-permute-done.6.refs_7_ = bf16[16,8,1024]{2,1,0:T(8,128)(2,1)} collective-permute-done((bf16[16,8,1024]{2,1,0:T(8,128)(2,1)}, bf16[16,8,1024]{2,1,0:T(8,128)(2,1)}, u32[]{:S(2)}, u32[]{:S(2)}) %collective-permute-start.6) | collective-permute-done | bytes 262176 | tf_op jit(solution)/shard_map/ppermute | solution.py:379
  69.8 8.6 %all-to-all-done.lane_ref = bf16[128,8,512]{2,1,0:T(8,128)(2,1)S(1)} async-done(((bf16[128,8,512]{2,1,0:T(8,128)(2,1)}), bf16[128,8,512]{2,1,0:T(8,128)(2,1)S(1)}, u32[]{:S(2)}, u32[]{:S(2)}) %all-to-all-start) | async-done | bytes 1048608 | tf_op jit(solution)/shard_map/all_to_all | solution.py:347
  78.5 0.6 shard_map.134
  79.1 11.3 %all_to_all.30.kv_ref = bf16[4,144,512]{2,1,0:T(8,128)(2,1)S(1)} all-to-all(bf16[4,144,512]{2,1,0:T(8,128)(2,1)S(1)} %bitcast.36), channel_id=1, replica_groups=mesh['dp'=128,'mp'=4] {'mp'}, dimensions={0} | all-to-all | bytes 1179648 | tf_op jit(solution)/shard_map/all_to_all | solution.py:435
  90.3 3.4 %shard_map.135 = (bf16[6,128,256]{2,1,0:T(8,128)(2,1)}, bf16[4,144,256]{2,1,0:T(8,128)(2,1)S(1)}) custom-call(s32[6]{0:T(128)S(1)} %dynamic-slice_reduce_fusion.count_ref, bf16[4,144,512]{2,1,0:T(8,128)(2,1)S(1)} %all_to_all.30.kv_ref, f32[6,128,256]{2,1,0:T(8,128)S(1)} %get-tuple-element.44.base_ref, f32[6,128,256]{2,1,0:T(8,128)} %get-tuple-element.45.pull_hbm, ...), custom_call_target="tpu_custom_call" | custom-call | flops 1048576 | bytes 1048576 | tf_op jit(solution)/shard_map/pallas_call | solution.py:52
  93.8 8.1 %all_to_all.31 = bf16[4,144,256]{2,1,0:T(8,128)(2,1)S(1)} all-to-all(bf16[4,144,256]{2,1,0:T(8,128)(2,1)S(1)} %get-tuple-element.50), channel_id=1, replica_groups=mesh['dp'=128,'mp'=4] {'mp'}, dimensions={0} | all-to-all | bytes 589824 | tf_op jit(solution)/shard_map/all_to_all | solution.py:463
  101.9 1.8 %shard_map.136 = bf16[128,8,256]{2,1,0:T(8,128)(2,1)} custom-call(s32[72]{0:T(128)S(1)} %fusion.6.source_ref, bf16[72,8,256]{2,1,0:T(8,128)(2,1)S(1)} %bitcast.39), custom_call_target="tpu_custom_call" | custom-call | flops 1048576 | bytes 1048576 | tf_op jit(solution)/shard_map/pallas_call | solution.py:52
  103.6 8.6 %all-to-all-start.3 = ((bf16[16,64,256]{2,1,0:T(8,128)(2,1)}), bf16[16,64,256]{2,1,0:T(8,128)(2,1)S(1)}, u32[]{:S(2)}, u32[]{:S(2)}) async-start(bf16[16,64,256]{2,1,0:T(8,128)(2,1)} %bitcast.13), calls=%async_computation.3 | async-start | bytes 1048576 | tf_op jit(solution)/shard_map/all_to_all | solution.py:475
  112.3 3.6 %shard_map.137.turned_ref = bf16[1024,1024]{1,0:T(8,128)(2,1)S(1)} custom-call(bf16[16,8,1024]{2,1,0:T(8,128)(2,1)} %get-tuple-element.60.refs_0_, bf16[16,8,1024]{2,1,0:T(8,128)(2,1)} %copy-done.6, bf16[16,8,1024]{2,1,0:T(8,128)(2,1)} %copy-done.7, bf16[16,8,1024]{2,1,0:T(8,128)(2,1)} %collective-permute-done.2.refs_3_, ...), custom_call_target="tpu_custom_call" | custom-call | flops 1073741824 | bytes 4194304 | tf_op jit(solution)/shard_map/pallas_call | solution.py:52
  115.9 19.2 %all-to-all-done.3 = bf16[16,64,256]{2,1,0:T(8,128)(2,1)S(1)} async-done(((bf16[16,64,256]{2,1,0:T(8,128)(2,1)}), bf16[16,64,256]{2,1,0:T(8,128)(2,1)S(1)}, u32[]{:S(2)}, u32[]{:S(2)}) %all-to-all-start.3) | async-done | bytes 524320 | tf_op jit(solution)/shard_map/all_to_all | solution.py:475
  135.1 0.7 shard_map.138
  135.8 21.1 %all_to_all.32 = bf16[32,32,256]{2,1,0:T(8,128)(2,1)S(1)} all-to-all(bf16[32,32,256]{2,1,0:T(8,128)(2,1)S(1)} %bitcast.38), channel_id=1, replica_groups={{0,1,2,3,4,5,6,7,128,129,130,131,132,133,134,135,256,257,258,259,260,26..., dimensions={0} | all-to-all | bytes 1048576 | tf_op jit(solution)/shard_map/all_to_all | solution.py:475
  156.9 0.1 convert_reduce_fusion
  157.0 17.7 %all_to_all.33 = f32[16,2,256]{2,1,0:T(2,128)S(1)} all-to-all(f32[16,2,256]{2,1,0:T(2,128)S(1)} %copy.32), channel_id=1, replica_groups={{0,8,16,24,32,40,48,56,64,72,80,88,96,104,112,120},{4,12,20,28,36,44,52..., dimensions={0} | all-to-all | bytes 65536 | tf_op jit(solution)/shard_map/all_to_all | solution.py:475
  174.8 0.6 reduce_sum.79
  (34 shorter events, 0.2 us)
Async XLA Ops:
  0.6 23.6 %copy-start = (bf16[48,8,1024]{2,1,0:T(8,128)(2,1)S(1)}, bf16[48,8,1024]{2,1,0:T(8,128)(2,1)}, u32[]{:S(2)}) copy-start(bf16[48,8,1024]{2,1,0:T(8,128)(2,1)} %param.16) | copy-start | bytes 2359300
  3.5 74.9 %all-to-all-start = ((bf16[128,8,512]{2,1,0:T(8,128)(2,1)}), bf16[128,8,512]{2,1,0:T(8,128)(2,1)S(1)}, u32[]{:S(2)}, u32[]{:S(2)}) async-start(bf16[128,8,512]{2,1,0:T(8,128)(2,1)} %get-tuple-element.35), calls=%async_computation | async-start | bytes 2097152 | tf_op jit(solution)/shard_map/all_to_all | solution.py:347
  24.9 17.6 %copy-start.10 = (s32[768]{0:T(1024)S(1)}, s32[768]{0:T(1024)}, u32[]{:S(2)}) copy-start(s32[768]{0:T(1024)} %param.12) | copy-start | bytes 9220
  24.9 19.6 %copy-start.9 = (s32[6,11,4]{1,2,0:T(4,128)S(1)}, s32[6,11,4]{1,2,0:T(4,128)}, u32[]{:S(2)}) copy-start(s32[6,11,4]{1,2,0:T(4,128)} %param.14) | copy-start | bytes 3172
  24.9 20.4 %copy-start.8 = (s32[6144]{0:T(1024)S(1)}, s32[6144]{0:T(1024)}, u32[]{:S(2)}) copy-start(s32[6144]{0:T(1024)} %param.13) | copy-start | bytes 73732
  25.0 22.1 %copy-start.11 = (bf16[256,32]{0,1:T(8,128)(2,1)S(1)}, bf16[256,32]{0,1:T(8,128)(2,1)}, u32[]{:S(2)}) copy-start(bf16[256,32]{0,1:T(8,128)(2,1)} %param.21) | copy-start | bytes 49156
  25.0 28.1 %copy-start.1 = (bf16[6,128,256]{2,1,0:T(8,128)(2,1)S(1)}, bf16[6,128,256]{2,1,0:T(8,128)(2,1)}, u32[]{:S(2)}) copy-start(bf16[6,128,256]{2,1,0:T(8,128)(2,1)} %prev_ref.1) | copy-start | bytes 1179652
  25.0 28.1 %copy-start.2 = (bf16[6,128,256]{2,1,0:T(8,128)(2,1)S(1)}, bf16[6,128,256]{2,1,0:T(8,128)(2,1)}, u32[]{:S(2)}) copy-start(bf16[6,128,256]{2,1,0:T(8,128)(2,1)} %cotangent_ref.1) | copy-start | bytes 1179652
  25.0 28.1 %copy-start.3 = (bf16[128,256]{1,0:T(8,128)(2,1)S(1)}, bf16[128,256]{1,0:T(8,128)(2,1)}, u32[]{:S(2)}) copy-start(bf16[128,256]{1,0:T(8,128)(2,1)} %query_ref.1) | copy-start | bytes 196612
  25.0 28.1 %copy-start.4 = (s32[6,4,128]{2,1,0:T(4,128)S(1)}, s32[6,4,128]{2,1,0:T(4,128)}, u32[]{:S(2)}) copy-start(s32[6,4,128]{2,1,0:T(4,128)} %align_ref.1) | copy-start | bytes 36868
  25.0 28.1 %copy-start.5 = (f32[256]{0:T(256)S(1)}, f32[256]{0:T(256)}, u32[]{:S(2)}) copy-start(f32[256]{0:T(256)} %param.22) | copy-start | bytes 3076
  26.2 21.0 %collective-permute-start = (bf16[16,8,1024]{2,1,0:T(8,128)(2,1)S(1)}, bf16[16,8,1024]{2,1,0:T(8,128)(2,1)S(1)}, u32[]{:S(2)}, u32[]{:S(2)}) collective-permute-start(bf16[16,8,1024]{2,1,0:T(8,128)(2,1)S(1)} %get-tuple-element.74), channel_id=1, source_target_pairs={{0,4},{4,0},{8,12},{12,8},{16,20},{20,16},{24,28},{28,24},{32,36},... | collective-permute-start | bytes 786440 | tf_op jit(solution)/shard_map/ppermute | solution.py:379
  29.0 21.4 %collective-permute-start.1 = (bf16[16,8,1024]{2,1,0:T(8,128)(2,1)S(1)}, bf16[16,8,1024]{2,1,0:T(8,128)(2,1)S(1)}, u32[]{:S(2)}, u32[]{:S(2)}) collective-permute-start(bf16[16,8,1024]{2,1,0:T(8,128)(2,1)S(1)} %get-tuple-element.73), channel_id=1, source_target_pairs={{0,128},{4,132},{8,136},{12,140},{16,144},{20,148},{24,152},{28,15... | collective-permute-start | bytes 786440 | tf_op jit(solution)/shard_map/ppermute | solution.py:379
  31.9 24.2 %collective-permute-start.2 = (bf16[16,8,1024]{2,1,0:T(8,128)(2,1)}, bf16[16,8,1024]{2,1,0:T(8,128)(2,1)}, u32[]{:S(2)}, u32[]{:S(2)}) collective-permute-start(bf16[16,8,1024]{2,1,0:T(8,128)(2,1)} %get-tuple-element.72), channel_id=1, source_target_pairs={{0,132},{4,128},{8,140},{12,136},{16,148},{20,144},{24,156},{28,15... | collective-permute-start | bytes 786440 | tf_op jit(solution)/shard_map/ppermute | solution.py:379
  35.5 22.3 %collective-permute-start.3 = (bf16[16,8,1024]{2,1,0:T(8,128)(2,1)}, bf16[16,8,1024]{2,1,0:T(8,128)(2,1)}, u32[]{:S(2)}, u32[]{:S(2)}) collective-permute-start(bf16[16,8,1024]{2,1,0:T(8,128)(2,1)} %get-tuple-element.71), channel_id=1, source_target_pairs={{0,256},{4,260},{8,264},{12,268},{16,272},{20,276},{24,280},{28,28... | collective-permute-start | bytes 786440 | tf_op jit(solution)/shard_map/ppermute | solution.py:379
  38.8 26.9 %collective-permute-start.4 = (bf16[16,8,1024]{2,1,0:T(8,128)(2,1)}, bf16[16,8,1024]{2,1,0:T(8,128)(2,1)}, u32[]{:S(2)}, u32[]{:S(2)}) collective-permute-start(bf16[16,8,1024]{2,1,0:T(8,128)(2,1)} %get-tuple-element.70), channel_id=1, source_target_pairs={{0,260},{4,256},{8,268},{12,264},{16,276},{20,272},{24,284},{28,28... | collective-permute-start | bytes 786440 | tf_op jit(solution)/shard_map/ppermute | solution.py:379
  47.2 5.8 %copy-start.6 = (bf16[16,8,1024]{2,1,0:T(8,128)(2,1)}, bf16[16,8,1024]{2,1,0:T(8,128)(2,1)S(1)}, u32[]{:S(2)}) copy-start(bf16[16,8,1024]{2,1,0:T(8,128)(2,1)S(1)} %collective-permute-done.refs_1_) | copy-start | bytes 786436
  47.2 18.4 %collective-permute-start.5 = (bf16[16,8,1024]{2,1,0:T(8,128)(2,1)}, bf16[16,8,1024]{2,1,0:T(8,128)(2,1)}, u32[]{:S(2)}, u32[]{:S(2)}) collective-permute-start(bf16[16,8,1024]{2,1,0:T(8,128)(2,1)} %get-tuple-element.69), channel_id=1, source_target_pairs={{0,384},{4,388},{8,392},{12,396},{16,400},{20,404},{24,408},{28,41... | collective-permute-start | bytes 786440 | tf_op jit(solution)/shard_map/ppermute | solution.py:379
  50.4 2.6 %copy-start.7 = (bf16[16,8,1024]{2,1,0:T(8,128)(2,1)}, bf16[16,8,1024]{2,1,0:T(8,128)(2,1)S(1)}, u32[]{:S(2)}) copy-start(bf16[16,8,1024]{2,1,0:T(8,128)(2,1)S(1)} %collective-permute-done.1.refs_2_) | copy-start | bytes 786436
  50.4 19.4 %collective-permute-start.6 = (bf16[16,8,1024]{2,1,0:T(8,128)(2,1)}, bf16[16,8,1024]{2,1,0:T(8,128)(2,1)}, u32[]{:S(2)}, u32[]{:S(2)}) collective-permute-start(bf16[16,8,1024]{2,1,0:T(8,128)(2,1)} %get-tuple-element.68), channel_id=1, source_target_pairs={{0,388},{4,384},{8,396},{12,392},{16,404},{20,400},{24,412},{28,40... | collective-permute-start | bytes 786440 | tf_op jit(solution)/shard_map/ppermute | solution.py:379
  103.6 31.5 %all-to-all-start.3 = ((bf16[16,64,256]{2,1,0:T(8,128)(2,1)}), bf16[16,64,256]{2,1,0:T(8,128)(2,1)S(1)}, u32[]{:S(2)}, u32[]{:S(2)}) async-start(bf16[16,64,256]{2,1,0:T(8,128)(2,1)} %bitcast.13), calls=%async_computation.3 | async-start | bytes 1048576 | tf_op jit(solution)/shard_map/all_to_all | solution.py:475

commit v10 on v9

--- a/solution.py
+++ b/solution.py
@@ -157,13 +157,14 @@
     step = CORES * bands * share
     at = 0
     for y in range(len(pieces) // CORES):
-        for c in range(CORES):
-            for j in range(bands * share):
-                first = y * deep * step + c * bands * share + j
-                for g in range(groups):
-                    part = turned_ref.at[g][pl.ds(first, deep, stride=step), :]
-                    out_ref[at : at + deep, g * width : (g + 1) * width] = part.astype(BF16)
-                at += deep
+        for band in range(bands):
+            for c in range(CORES):
+                for i in range(share):
+                    first = y * deep * step + (c * bands + band) * share + i
+                    for g in range(groups):
+                        part = turned_ref.at[g][pl.ds(first, deep, stride=step), :]
+                        out_ref[at : at + deep, g * width : (g + 1) * width] = part.astype(BF16)
+                    at += deep
 
 
 def temporal_kernel(
@@ -497,13 +498,14 @@
         back.reshape(tokens, channels),
         turned,
     )
-    planes = [
-        [device(y, z, c) * bands + x for y in ys for c in cs for x in range(bands)] for z in zs
+    squares = [
+        [device(y, z, c) * bands + x for y in ys for x in range(bands)] for z in zs for c in cs
     ]
-    neck = neck.reshape(chips * CORES * bands, share * deep, channels)
-    neck = exchange(neck, ("dp", "mp"), planes).astype(F32)
-    neck = jnp.sum(neck, axis=0).reshape(share, deep, channels).transpose(1, 0, 2)
-    neck = exchange(neck, "dp", columns)
+    lines = [[device(y, z, c) for z in zs for c in cs] for y in ys]
+    neck = neck.reshape(chips * bands, CORES * share * deep, channels)
+    neck = exchange(neck, ("dp", "mp"), squares).astype(F32)
+    neck = jnp.sum(neck, axis=0).reshape(CORES, share, deep, channels).transpose(2, 0, 1, 3)
+    neck = exchange(neck.reshape(deep * CORES, share, channels), "dp", lines)
     return bev_out, jnp.sum(neck, axis=0)
 
 

time: 176 us -> 178 us (1.011)
  no operation moved by 1% of the time
where the time goes in v10:
time: 178 us; the launch traced here: 177 us
  blocking collectives  59.8 us (34%)
  starting transfers between devices  51.3 us (29%)
  waiting for transfers between devices  41.7 us (23%)
  Pallas kernels  16.2 us (9%)
  between operations  3 us (2%)
  other arithmetic  2.87 us (2%)
  local copies, waits for them, and re-layouts  2.21 us (1%)
    all_to_all x2, blocking collectives, exchange(): lax.all_to_all(part, axis, split_axis=0, concat_axis=0, tiled=True, axis_...  40.5 us
    ppermute x7, starting transfers between devices, on_device(): pieces.append(lax.ppermute(dealt[p], 'dp', moves))  22.1 us
    all_to_all x1, starting transfers between devices, on_device(): got = lax.all_to_all(lanes, 'dp', split_axis=0, concat_axis=0, tiled=True)  20.6 us
    all_to_all x1, waiting for transfers between devices, exchange(): lax.all_to_all(part, axis, split_axis=0, concat_axis=0, tiled=True, axis_...  19.2 us
    pallas_call x8, Pallas kernels, call(): pl.pallas_call(body, out_shape=outs, in_specs=specs, out_specs=out_specs...  16.2 us
    ppermute x7, waiting for transfers between devices, on_device(): pieces.append(lax.ppermute(dealt[p], 'dp', moves))  13.8 us
    all_to_all x1, blocking collectives, on_device(): lax.all_to_all(chosen_kv.reshape(bands, piece, 2 * channels), 'mp', split...  11.3 us
    all_to_all x1, starting transfers between devices, exchange(): lax.all_to_all(part, axis, split_axis=0, concat_axis=0, tiled=True, axis_...  8.66 us
  transfers between devices with their start and end apart: 9, of which 5 were waited for; matrix products, arithmetic and copies ran while one was open for 2% of the time, Pallas kernels for 4%

profile of v10, /device:TPU:1, one launch (start us, length us, event | category | flops | bytes accessed | tf_op | source)
XLA Modules:
  0.0 177.1 jit_solution(10115877094499383348)
XLA Ops:
  0.6 2.9 %shard_map.131 = (bf16[128,8,512]{2,1,0:T(8,128)(2,1)}, s32[8,128]{1,0:T(8,128)S(1)}) custom-call(s32[1]{0:T(128)} %bitcast.bin_ref, s32[6,128]{1,0:T(8,128)} %bitcast.48, s32[1,6144]{1,0:T(1,128)} %bitcast.47, bf16[384,1024]{1,0:T(8,128)(2,1)} %bitcast.41, bf16[384,256]{1,0:T(8,128)(2,1)} %bitcast.46, bf16[1024,256]{1,0:T(8,128)(2,1)} %weight_hbm.1), custom_call_target="tpu_custom_call" | custom-call | flops 1048576 | bytes 1048576 | tf_op jit(solution)/shard_map/pallas_call | solution.py:52
  3.5 20.6 %all-to-all-start = ((bf16[128,8,512]{2,1,0:T(8,128)(2,1)}), bf16[128,8,512]{2,1,0:T(8,128)(2,1)S(1)}, u32[]{:S(2)}, u32[]{:S(2)}) async-start(bf16[128,8,512]{2,1,0:T(8,128)(2,1)} %get-tuple-element.35), calls=%async_computation | async-start | bytes 2097152 | tf_op jit(solution)/shard_map/all_to_all | solution.py:348
  24.2 0.7 shard_map.133
  24.9 0.0 copy-start.8
  25.0 0.0 copy-start.11
  25.0 1.2 fusion.19
  26.2 2.8 %collective-permute-start = (bf16[16,8,1024]{2,1,0:T(8,128)(2,1)S(1)}, bf16[16,8,1024]{2,1,0:T(8,128)(2,1)S(1)}, u32[]{:S(2)}, u32[]{:S(2)}) collective-permute-start(bf16[16,8,1024]{2,1,0:T(8,128)(2,1)S(1)} %get-tuple-element.74), channel_id=1, source_target_pairs={{0,4},{4,0},{8,12},{12,8},{16,20},{20,16},{24,28},{28,24},{32,36},... | collective-permute-start | bytes 786440 | tf_op jit(solution)/shard_map/ppermute | solution.py:380
  29.0 2.9 %collective-permute-start.1 = (bf16[16,8,1024]{2,1,0:T(8,128)(2,1)S(1)}, bf16[16,8,1024]{2,1,0:T(8,128)(2,1)S(1)}, u32[]{:S(2)}, u32[]{:S(2)}) collective-permute-start(bf16[16,8,1024]{2,1,0:T(8,128)(2,1)S(1)} %get-tuple-element.73), channel_id=1, source_target_pairs={{0,128},{4,132},{8,136},{12,140},{16,144},{20,148},{24,152},{28,15... | collective-permute-start | bytes 786440 | tf_op jit(solution)/shard_map/ppermute | solution.py:380
  31.9 3.6 %collective-permute-start.2 = (bf16[16,8,1024]{2,1,0:T(8,128)(2,1)}, bf16[16,8,1024]{2,1,0:T(8,128)(2,1)}, u32[]{:S(2)}, u32[]{:S(2)}) collective-permute-start(bf16[16,8,1024]{2,1,0:T(8,128)(2,1)} %get-tuple-element.72), channel_id=1, source_target_pairs={{0,132},{4,128},{8,140},{12,136},{16,148},{20,144},{24,156},{28,15... | collective-permute-start | bytes 786440 | tf_op jit(solution)/shard_map/ppermute | solution.py:380
  35.5 3.3 %collective-permute-start.3 = (bf16[16,8,1024]{2,1,0:T(8,128)(2,1)}, bf16[16,8,1024]{2,1,0:T(8,128)(2,1)}, u32[]{:S(2)}, u32[]{:S(2)}) collective-permute-start(bf16[16,8,1024]{2,1,0:T(8,128)(2,1)} %get-tuple-element.71), channel_id=1, source_target_pairs={{0,256},{4,260},{8,264},{12,268},{16,272},{20,276},{24,280},{28,28... | collective-permute-start | bytes 786440 | tf_op jit(solution)/shard_map/ppermute | solution.py:380
  38.8 3.8 %collective-permute-start.4 = (bf16[16,8,1024]{2,1,0:T(8,128)(2,1)}, bf16[16,8,1024]{2,1,0:T(8,128)(2,1)}, u32[]{:S(2)}, u32[]{:S(2)}) collective-permute-start(bf16[16,8,1024]{2,1,0:T(8,128)(2,1)} %get-tuple-element.70), channel_id=1, source_target_pairs={{0,260},{4,256},{8,268},{12,264},{16,276},{20,272},{24,284},{28,28... | collective-permute-start | bytes 786440 | tf_op jit(solution)/shard_map/ppermute | solution.py:380
  42.5 0.6 select_reduce_fusion.2
  44.5 0.1 dynamic_slice.9
  44.6 0.1 copy.33
  45.4 0.1 fusion.17
  45.5 0.1 select_reduce_fusion.3
  45.6 0.1 multiply_reduce_fusion
  45.7 0.1 add_add_fusion
  45.8 0.4 select_reduce_fusion.1
  46.2 0.5 select_reduce_fusion
  46.7 0.2 fusion.18
  46.9 0.1 copy.34
  47.0 0.1 copy.35
  47.1 0.1 copy.32.point_ref
  47.2 3.2 %collective-permute-start.5 = (bf16[16,8,1024]{2,1,0:T(8,128)(2,1)}, bf16[16,8,1024]{2,1,0:T(8,128)(2,1)}, u32[]{:S(2)}, u32[]{:S(2)}) collective-permute-start(bf16[16,8,1024]{2,1,0:T(8,128)(2,1)} %get-tuple-element.69), channel_id=1, source_target_pairs={{0,384},{4,388},{8,392},{12,396},{16,400},{20,404},{24,408},{28,41... | collective-permute-start | bytes 786440 | tf_op jit(solution)/shard_map/ppermute | solution.py:380
  50.4 2.6 %collective-permute-start.6 = (bf16[16,8,1024]{2,1,0:T(8,128)(2,1)}, bf16[16,8,1024]{2,1,0:T(8,128)(2,1)}, u32[]{:S(2)}, u32[]{:S(2)}) collective-permute-start(bf16[16,8,1024]{2,1,0:T(8,128)(2,1)} %get-tuple-element.68), channel_id=1, source_target_pairs={{0,388},{4,384},{8,396},{12,392},{16,404},{20,400},{24,412},{28,40... | collective-permute-start | bytes 786440 | tf_op jit(solution)/shard_map/ppermute | solution.py:380
  53.1 2.5 %shard_map.132 = (f32[6,128,256]{2,1,0:T(8,128)S(1)}, f32[6,128,256]{2,1,0:T(8,128)}, bf16[1024,256]{1,0:T(8,128)(2,1)S(1)}, f32[1,256]{1,0:T(1,128)S(1)}) custom-call(s32[1]{0:T(128)} %bitcast.5.band_ref, bf16[128,256]{1,0:T(8,128)(2,1)S(1)} %copy-done.3, bf16[256,32]{1,0:T(8,128)(2,1)S(1)} %copy.32.point_ref, bf16[6,128,256]{2,1,0:T(8,128)(2,1)S(1)} %copy-done.1, ...), custom_call_target="tpu_custom_call" | custom-call | flops 1073741824 | bytes 4194304 | tf_op jit(solution)/shard_map/pallas_call | solution.py:52
  55.6 0.1 copy.36
  55.7 0.1 max.10.source_ref
  55.8 0.2 dynamic-slice_reduce_fusion.count_ref
  56.0 1.8 collective-permute-done.3.refs_4_
  57.8 7.9 %collective-permute-done.4.refs_5_ = bf16[16,8,1024]{2,1,0:T(8,128)(2,1)} collective-permute-done((bf16[16,8,1024]{2,1,0:T(8,128)(2,1)}, bf16[16,8,1024]{2,1,0:T(8,128)(2,1)}, u32[]{:S(2)}, u32[]{:S(2)}) %collective-permute-start.4) | collective-permute-done | bytes 262176 | tf_op jit(solution)/shard_map/ppermute | solution.py:380
  65.7 4.2 %collective-permute-done.6.refs_7_ = bf16[16,8,1024]{2,1,0:T(8,128)(2,1)} collective-permute-done((bf16[16,8,1024]{2,1,0:T(8,128)(2,1)}, bf16[16,8,1024]{2,1,0:T(8,128)(2,1)}, u32[]{:S(2)}, u32[]{:S(2)}) %collective-permute-start.6) | collective-permute-done | bytes 262176 | tf_op jit(solution)/shard_map/ppermute | solution.py:380
  69.8 8.6 %all-to-all-done.lane_ref = bf16[128,8,512]{2,1,0:T(8,128)(2,1)S(1)} async-done(((bf16[128,8,512]{2,1,0:T(8,128)(2,1)}), bf16[128,8,512]{2,1,0:T(8,128)(2,1)S(1)}, u32[]{:S(2)}, u32[]{:S(2)}) %all-to-all-start) | async-done | bytes 1048608 | tf_op jit(solution)/shard_map/all_to_all | solution.py:348
  78.5 0.6 shard_map.134
  79.1 11.3 %all_to_all.30.kv_ref = bf16[4,144,512]{2,1,0:T(8,128)(2,1)S(1)} all-to-all(bf16[4,144,512]{2,1,0:T(8,128)(2,1)S(1)} %bitcast.37), channel_id=1, replica_groups=mesh['dp'=128,'mp'=4] {'mp'}, dimensions={0} | all-to-all | bytes 1179648 | tf_op jit(solution)/shard_map/all_to_all | solution.py:436
  90.3 3.4 %shard_map.135 = (bf16[6,128,256]{2,1,0:T(8,128)(2,1)}, bf16[4,144,256]{2,1,0:T(8,128)(2,1)S(1)}) custom-call(s32[6]{0:T(128)S(1)} %dynamic-slice_reduce_fusion.count_ref, bf16[4,144,512]{2,1,0:T(8,128)(2,1)S(1)} %all_to_all.30.kv_ref, f32[6,128,256]{2,1,0:T(8,128)S(1)} %get-tuple-element.44.base_ref, f32[6,128,256]{2,1,0:T(8,128)} %get-tuple-element.45.pull_hbm, ...), custom_call_target="tpu_custom_call" | custom-call | flops 1048576 | bytes 1048576 | tf_op jit(solution)/shard_map/pallas_call | solution.py:52
  93.8 8.1 %all_to_all.31 = bf16[4,144,256]{2,1,0:T(8,128)(2,1)S(1)} all-to-all(bf16[4,144,256]{2,1,0:T(8,128)(2,1)S(1)} %get-tuple-element.50), channel_id=1, replica_groups=mesh['dp'=128,'mp'=4] {'mp'}, dimensions={0} | all-to-all | bytes 589824 | tf_op jit(solution)/shard_map/all_to_all | solution.py:464
  101.9 1.8 %shard_map.136 = bf16[128,8,256]{2,1,0:T(8,128)(2,1)} custom-call(s32[72]{0:T(128)S(1)} %fusion.6.source_ref, bf16[72,8,256]{2,1,0:T(8,128)(2,1)S(1)} %bitcast.40), custom_call_target="tpu_custom_call" | custom-call | flops 1048576 | bytes 1048576 | tf_op jit(solution)/shard_map/pallas_call | solution.py:52
  103.6 8.7 %all-to-all-start.3 = ((bf16[16,64,256]{2,1,0:T(8,128)(2,1)}), bf16[16,64,256]{2,1,0:T(8,128)(2,1)S(1)}, u32[]{:S(2)}, u32[]{:S(2)}) async-start(bf16[16,64,256]{2,1,0:T(8,128)(2,1)} %bitcast.13), calls=%async_computation.3 | async-start | bytes 1048576 | tf_op jit(solution)/shard_map/all_to_all | solution.py:476
  112.3 3.6 %shard_map.137.turned_ref = bf16[1024,1024]{1,0:T(8,128)(2,1)S(1)} custom-call(bf16[16,8,1024]{2,1,0:T(8,128)(2,1)} %get-tuple-element.60.refs_0_, bf16[16,8,1024]{2,1,0:T(8,128)(2,1)} %copy-done.6, bf16[16,8,1024]{2,1,0:T(8,128)(2,1)} %copy-done.7, bf16[16,8,1024]{2,1,0:T(8,128)(2,1)} %collective-permute-done.2.refs_3_, ...), custom_call_target="tpu_custom_call" | custom-call | flops 1073741824 | bytes 4194304 | tf_op jit(solution)/shard_map/pallas_call | solution.py:52
  115.9 19.2 %all-to-all-done.3 = bf16[16,64,256]{2,1,0:T(8,128)(2,1)S(1)} async-done(((bf16[16,64,256]{2,1,0:T(8,128)(2,1)}), bf16[16,64,256]{2,1,0:T(8,128)(2,1)S(1)}, u32[]{:S(2)}, u32[]{:S(2)}) %all-to-all-start.3) | async-done | bytes 524320 | tf_op jit(solution)/shard_map/all_to_all | solution.py:476
  135.1 0.7 shard_map.138
  135.8 11.6 %all_to_all.32 = bf16[16,64,256]{2,1,0:T(8,128)(2,1)S(1)} all-to-all(bf16[16,64,256]{2,1,0:T(8,128)(2,1)S(1)} %bitcast.39), channel_id=1, replica_groups={{0,1,2,3,128,129,130,131,256,257,258,259,384,385,386,387},{4,5,6,7,132,..., dimensions={0} | all-to-all | bytes 1048576 | tf_op jit(solution)/shard_map/all_to_all | solution.py:476
  147.5 0.1 convert_reduce_fusion
  147.5 0.1 copy.37
  147.6 28.8 %all_to_all.33 = f32[32,2,256]{2,1,0:T(2,128)S(1)} all-to-all(f32[32,2,256]{2,1,0:T(2,128)S(1)} %bitcast.45), channel_id=1, replica_groups={{0,4,8,12,16,20,24,28,32,36,40,44,48,52,56,60,64,68,72,76,80,84,88,92,9..., dimensions={0} | all-to-all | bytes 131072 | tf_op jit(solution)/shard_map/all_to_all | solution.py:476
  176.5 0.6 reduce_sum.79
  (34 shorter events, 0.1 us)
Async XLA Ops:
  0.6 23.6 %copy-start = (bf16[48,8,1024]{2,1,0:T(8,128)(2,1)S(1)}, bf16[48,8,1024]{2,1,0:T(8,128)(2,1)}, u32[]{:S(2)}) copy-start(bf16[48,8,1024]{2,1,0:T(8,128)(2,1)} %param.16) | copy-start | bytes 2359300
  3.5 74.9 %all-to-all-start = ((bf16[128,8,512]{2,1,0:T(8,128)(2,1)}), bf16[128,8,512]{2,1,0:T(8,128)(2,1)S(1)}, u32[]{:S(2)}, u32[]{:S(2)}) async-start(bf16[128,8,512]{2,1,0:T(8,128)(2,1)} %get-tuple-element.35), calls=%async_computation | async-start | bytes 2097152 | tf_op jit(solution)/shard_map/all_to_all | solution.py:348
  24.9 17.6 %copy-start.10 = (s32[768]{0:T(1024)S(1)}, s32[768]{0:T(1024)}, u32[]{:S(2)}) copy-start(s32[768]{0:T(1024)} %param.12) | copy-start | bytes 9220
  24.9 19.6 %copy-start.9 = (s32[6,11,4]{1,2,0:T(4,128)S(1)}, s32[6,11,4]{1,2,0:T(4,128)}, u32[]{:S(2)}) copy-start(s32[6,11,4]{1,2,0:T(4,128)} %param.14) | copy-start | bytes 3172
  24.9 20.4 %copy-start.8 = (s32[6144]{0:T(1024)S(1)}, s32[6144]{0:T(1024)}, u32[]{:S(2)}) copy-start(s32[6144]{0:T(1024)} %param.13) | copy-start | bytes 73732
  25.0 22.1 %copy-start.11 = (bf16[256,32]{0,1:T(8,128)(2,1)S(1)}, bf16[256,32]{0,1:T(8,128)(2,1)}, u32[]{:S(2)}) copy-start(bf16[256,32]{0,1:T(8,128)(2,1)} %param.21) | copy-start | bytes 49156
  25.0 28.1 %copy-start.1 = (bf16[6,128,256]{2,1,0:T(8,128)(2,1)S(1)}, bf16[6,128,256]{2,1,0:T(8,128)(2,1)}, u32[]{:S(2)}) copy-start(bf16[6,128,256]{2,1,0:T(8,128)(2,1)} %prev_ref.1) | copy-start | bytes 1179652
  25.0 28.1 %copy-start.2 = (bf16[6,128,256]{2,1,0:T(8,128)(2,1)S(1)}, bf16[6,128,256]{2,1,0:T(8,128)(2,1)}, u32[]{:S(2)}) copy-start(bf16[6,128,256]{2,1,0:T(8,128)(2,1)} %cotangent_ref.1) | copy-start | bytes 1179652
  25.0 28.1 %copy-start.3 = (bf16[128,256]{1,0:T(8,128)(2,1)S(1)}, bf16[128,256]{1,0:T(8,128)(2,1)}, u32[]{:S(2)}) copy-start(bf16[128,256]{1,0:T(8,128)(2,1)} %query_ref.1) | copy-start | bytes 196612
  25.0 28.1 %copy-start.4 = (s32[6,4,128]{2,1,0:T(4,128)S(1)}, s32[6,4,128]{2,1,0:T(4,128)}, u32[]{:S(2)}) copy-start(s32[6,4,128]{2,1,0:T(4,128)} %align_ref.1) | copy-start | bytes 36868
  25.0 28.1 %copy-start.5 = (f32[256]{0:T(256)S(1)}, f32[256]{0:T(256)}, u32[]{:S(2)}) copy-start(f32[256]{0:T(256)} %param.22) | copy-start | bytes 3076
  26.2 21.0 %collective-permute-start = (bf16[16,8,1024]{2,1,0:T(8,128)(2,1)S(1)}, bf16[16,8,1024]{2,1,0:T(8,128)(2,1)S(1)}, u32[]{:S(2)}, u32[]{:S(2)}) collective-permute-start(bf16[16,8,1024]{2,1,0:T(8,128)(2,1)S(1)} %get-tuple-element.74), channel_id=1, source_target_pairs={{0,4},{4,0},{8,12},{12,8},{16,20},{20,16},{24,28},{28,24},{32,36},... | collective-permute-start | bytes 786440 | tf_op jit(solution)/shard_map/ppermute | solution.py:380
  29.0 21.4 %collective-permute-start.1 = (bf16[16,8,1024]{2,1,0:T(8,128)(2,1)S(1)}, bf16[16,8,1024]{2,1,0:T(8,128)(2,1)S(1)}, u32[]{:S(2)}, u32[]{:S(2)}) collective-permute-start(bf16[16,8,1024]{2,1,0:T(8,128)(2,1)S(1)} %get-tuple-element.73), channel_id=1, source_target_pairs={{0,128},{4,132},{8,136},{12,140},{16,144},{20,148},{24,152},{28,15... | collective-permute-start | bytes 786440 | tf_op jit(solution)/shard_map/ppermute | solution.py:380
  31.9 24.2 %collective-permute-start.2 = (bf16[16,8,1024]{2,1,0:T(8,128)(2,1)}, bf16[16,8,1024]{2,1,0:T(8,128)(2,1)}, u32[]{:S(2)}, u32[]{:S(2)}) collective-permute-start(bf16[16,8,1024]{2,1,0:T(8,128)(2,1)} %get-tuple-element.72), channel_id=1, source_target_pairs={{0,132},{4,128},{8,140},{12,136},{16,148},{20,144},{24,156},{28,15... | collective-permute-start | bytes 786440 | tf_op jit(solution)/shard_map/ppermute | solution.py:380
  35.5 22.3 %collective-permute-start.3 = (bf16[16,8,1024]{2,1,0:T(8,128)(2,1)}, bf16[16,8,1024]{2,1,0:T(8,128)(2,1)}, u32[]{:S(2)}, u32[]{:S(2)}) collective-permute-start(bf16[16,8,1024]{2,1,0:T(8,128)(2,1)} %get-tuple-element.71), channel_id=1, source_target_pairs={{0,256},{4,260},{8,264},{12,268},{16,272},{20,276},{24,280},{28,28... | collective-permute-start | bytes 786440 | tf_op jit(solution)/shard_map/ppermute | solution.py:380
  38.8 26.9 %collective-permute-start.4 = (bf16[16,8,1024]{2,1,0:T(8,128)(2,1)}, bf16[16,8,1024]{2,1,0:T(8,128)(2,1)}, u32[]{:S(2)}, u32[]{:S(2)}) collective-permute-start(bf16[16,8,1024]{2,1,0:T(8,128)(2,1)} %get-tuple-element.70), channel_id=1, source_target_pairs={{0,260},{4,256},{8,268},{12,264},{16,276},{20,272},{24,284},{28,28... | collective-permute-start | bytes 786440 | tf_op jit(solution)/shard_map/ppermute | solution.py:380
  47.2 5.8 %copy-start.6 = (bf16[16,8,1024]{2,1,0:T(8,128)(2,1)}, bf16[16,8,1024]{2,1,0:T(8,128)(2,1)S(1)}, u32[]{:S(2)}) copy-start(bf16[16,8,1024]{2,1,0:T(8,128)(2,1)S(1)} %collective-permute-done.refs_1_) | copy-start | bytes 786436
  47.2 18.4 %collective-permute-start.5 = (bf16[16,8,1024]{2,1,0:T(8,128)(2,1)}, bf16[16,8,1024]{2,1,0:T(8,128)(2,1)}, u32[]{:S(2)}, u32[]{:S(2)}) collective-permute-start(bf16[16,8,1024]{2,1,0:T(8,128)(2,1)} %get-tuple-element.69), channel_id=1, source_target_pairs={{0,384},{4,388},{8,392},{12,396},{16,400},{20,404},{24,408},{28,41... | collective-permute-start | bytes 786440 | tf_op jit(solution)/shard_map/ppermute | solution.py:380
  50.4 2.6 %copy-start.7 = (bf16[16,8,1024]{2,1,0:T(8,128)(2,1)}, bf16[16,8,1024]{2,1,0:T(8,128)(2,1)S(1)}, u32[]{:S(2)}) copy-start(bf16[16,8,1024]{2,1,0:T(8,128)(2,1)S(1)} %collective-permute-done.1.refs_2_) | copy-start | bytes 786436
  50.4 19.4 %collective-permute-start.6 = (bf16[16,8,1024]{2,1,0:T(8,128)(2,1)}, bf16[16,8,1024]{2,1,0:T(8,128)(2,1)}, u32[]{:S(2)}, u32[]{:S(2)}) collective-permute-start(bf16[16,8,1024]{2,1,0:T(8,128)(2,1)} %get-tuple-element.68), channel_id=1, source_target_pairs={{0,388},{4,384},{8,396},{12,392},{16,404},{20,400},{24,412},{28,40... | collective-permute-start | bytes 786440 | tf_op jit(solution)/shard_map/ppermute | solution.py:380
  103.6 31.5 %all-to-all-start.3 = ((bf16[16,64,256]{2,1,0:T(8,128)(2,1)}), bf16[16,64,256]{2,1,0:T(8,128)(2,1)S(1)}, u32[]{:S(2)}, u32[]{:S(2)}) async-start(bf16[16,64,256]{2,1,0:T(8,128)(2,1)} %bitcast.13), calls=%async_computation.3 | async-start | bytes 1048576 | tf_op jit(solution)/shard_map/all_to_all | solution.py:476
